TPU v7x, 128 devices: a whole 4x4x4 slice. The times are simulated.
128 devices in a mesh: resp: 32 (over x, z, y_lo), head: 4 (over y_hi, core).
Axes of the slice: x: 4, y: 4 (y_hi: 2, y_lo: 2; y = y_hi * 2 + y_lo), z: 4, core: 2. Of those that a mesh axis runs over, the one named last changes fastest.
Arguments:
- queries: bfloat16 [32, 512, 5120], P('resp', None, 'head'), may hold values from -8 to 8
- resp_keys: bfloat16 [32, 512, 1024], P('resp', None, 'head'), may hold values from -6 to 6
- resp_values: bfloat16 [32, 512, 1024], P('resp', None, 'head'), may hold values from -6 to 6
- prompt_keys: bfloat16 [1024, 1024], P(('resp', 'head')), may hold values from -8 to 8
- prompt_values: bfloat16 [1024, 1024], P(('resp', 'head')), may hold values from -6 to 6
- lengths: int32 [32], P('resp'), may hold values from 64 to 512, as said below
- loss_mask: int32 [32, 512], P('resp'), may hold values 0 or 1
- out_grad: bfloat16 [32, 512, 5120], P('resp', None, 'head'), may hold values from -6 to 6
Outputs:
- attended: bfloat16 [32, 512, 5120], P('resp', None, 'head')
- query_grad: bfloat16 [32, 512, 5120], P('resp', None, 'head')
- key_grad: bfloat16 [32, 512, 1024], P('resp', None, 'head')
- value_grad: bfloat16 [32, 512, 1024], P('resp', None, 'head')
- prompt_key_grad: float32 [1024, 1024], P(('resp', 'head'))
- prompt_value_grad: float32 [1024, 1024], P(('resp', 'head'))
Inputs may be any that keep to these rules, and one draw needn't show every extreme that they name: `lengths`: the longest response has exactly 512 live positions.
All inputs are finite; a program needn't handle non-finite values. No bound on the sum of `loss_mask` on one device may be relied on, other than what follows from the above.
Results may differ from a plain program's by a relative error of at most 0.035.
Values may be sent and summed in bfloat16 or wider, within the bound.
A program may use at most 128 MiB of HBM per device.

v0:
```python
import jax
import jax.numpy as jnp
from jax import lax
from jax.sharding import PartitionSpec as P

HEAD_DIM = 128


def respond(
    query_row, key_row, value_row, length, keep_row, grad_row, prompt_key3, prompt_value3, kv_count
):
    steps_len = query_row.shape[0]
    group_size = query_row.shape[1] // (kv_count * HEAD_DIM)
    score_scale = HEAD_DIM ** (-0.5)
    positions = jnp.arange(steps_len)
    query_five = query_row.reshape(steps_len, kv_count, group_size, HEAD_DIM)
    own_key = key_row.reshape(steps_len, kv_count, HEAD_DIM)
    own_value = value_row.reshape(steps_len, kv_count, HEAD_DIM)
    prompt_scores = (
        jnp.einsum("tkgd,jkd->kgtj", query_five, prompt_key3, preferred_element_type=jnp.float32)
        * score_scale
    )
    own_scores = (
        jnp.einsum("tkgd,jkd->kgtj", query_five, own_key, preferred_element_type=jnp.float32)
        * score_scale
    )
    allowed = (positions[None, :] <= positions[:, None]) & (positions[None, :] < length)
    own_scores = jnp.where(allowed, own_scores, -jnp.inf)
    row_top = jnp.maximum(prompt_scores.max(-1), own_scores.max(-1))
    row_total = jnp.exp(prompt_scores - row_top[..., None]).sum(-1) + jnp.exp(
        own_scores - row_top[..., None]
    ).sum(-1)
    log_total = row_top + jnp.log(row_total)
    prompt_prob = jnp.exp(prompt_scores - log_total[..., None])
    own_prob = jnp.exp(own_scores - log_total[..., None])
    prompt_weight = prompt_prob.astype(jnp.bfloat16)
    own_weight = own_prob.astype(jnp.bfloat16)
    live_rows = positions < length
    attended = jnp.einsum(
        "kgtj,jkd->tkgd", prompt_weight, prompt_value3, preferred_element_type=jnp.float32
    ) + jnp.einsum("kgtj,jkd->tkgd", own_weight, own_value, preferred_element_type=jnp.float32)
    attended = jnp.where(live_rows[:, None, None, None], attended, 0.0).astype(jnp.bfloat16)
    grad_factor = (keep_row * live_rows.astype(jnp.int32)).astype(jnp.bfloat16)
    grad_five = (
        grad_row.reshape(steps_len, kv_count, group_size, HEAD_DIM)
        * grad_factor[:, None, None, None]
    )
    row_delta = jnp.einsum(
        "tkgd,tkgd->kgt", grad_five, attended, preferred_element_type=jnp.float32
    )
    prompt_dprob = jnp.einsum(
        "tkgd,jkd->kgtj", grad_five, prompt_value3, preferred_element_type=jnp.float32
    )
    own_dprob = jnp.einsum(
        "tkgd,jkd->kgtj", grad_five, own_value, preferred_element_type=jnp.float32
    )
    prompt_ds = (prompt_prob * (prompt_dprob - row_delta[..., None]) * score_scale).astype(
        jnp.bfloat16
    )
    own_ds = (own_prob * (own_dprob - row_delta[..., None]) * score_scale).astype(jnp.bfloat16)
    query_grad = jnp.einsum(
        "kgtj,jkd->tkgd", prompt_ds, prompt_key3, preferred_element_type=jnp.float32
    ) + jnp.einsum("kgtj,jkd->tkgd", own_ds, own_key, preferred_element_type=jnp.float32)
    key_grad = jnp.einsum("kgtj,tkgd->jkd", own_ds, query_five, preferred_element_type=jnp.float32)
    value_grad = jnp.einsum(
        "kgtj,tkgd->jkd", own_weight, grad_five, preferred_element_type=jnp.float32
    )
    return (
        attended.reshape(query_row.shape),
        query_grad.astype(jnp.bfloat16).reshape(query_row.shape),
        key_grad.astype(jnp.bfloat16).reshape(key_row.shape),
        value_grad.astype(jnp.bfloat16).reshape(key_row.shape),
        prompt_ds,
        prompt_weight,
        grad_five,
    )


def per_device(
    queries, resp_keys, resp_values, prompt_keys, prompt_values, lengths, loss_mask, out_grad
):
    kv_width = resp_keys.shape[2]
    kv_count = kv_width // HEAD_DIM
    every_key, every_value = (
        lax.all_gather(prompt_keys, ("resp", "head"), axis=0, tiled=True),
        lax.all_gather(prompt_values, ("resp", "head"), axis=0, tiled=True),
    )
    head_start = lax.axis_index("head") * kv_width
    group_keys = lax.dynamic_slice_in_dim(every_key, head_start, kv_width, 1)
    group_values = lax.dynamic_slice_in_dim(every_value, head_start, kv_width, 1)
    prompt_rows = group_keys.shape[0]
    prompt_key3 = group_keys.reshape(prompt_rows, kv_count, HEAD_DIM)
    prompt_value3 = group_values.reshape(prompt_rows, kv_count, HEAD_DIM)

    def one_response(inputs):
        query_row, key_row, value_row, length, keep_row, grad_row = inputs
        return respond(
            query_row,
            key_row,
            value_row,
            length,
            keep_row,
            grad_row,
            prompt_key3,
            prompt_value3,
            kv_count,
        )

    results = lax.map(one_response, (queries, resp_keys, resp_values, lengths, loss_mask, out_grad))
    attended, query_grad, key_grad, value_grad, prompt_ds, prompt_weight, grad_all = results
    query_all = queries.reshape(queries.shape[0], queries.shape[1], kv_count, -1, HEAD_DIM)
    local_rows = prompt_rows // lax.axis_size("resp")
    key_part = jnp.einsum(
        "rkgtj,rtkgd->jkd", prompt_ds, query_all, preferred_element_type=jnp.float32
    )
    value_part = jnp.einsum(
        "rkgtj,rtkgd->jkd", prompt_weight, grad_all, preferred_element_type=jnp.float32
    )
    whole_sum = lax.psum(
        jnp.concatenate(
            [key_part.reshape(prompt_rows, kv_width), value_part.reshape(prompt_rows, kv_width)], 1
        ),
        "resp",
    )
    summed = lax.dynamic_slice_in_dim(whole_sum, lax.axis_index("resp") * local_rows, local_rows, 0)
    key_sum = summed[:, :kv_width]
    value_sum = summed[:, kv_width:]
    prompt_key_grad, prompt_value_grad = (
        lax.all_to_all(key_sum, "head", split_axis=0, concat_axis=1, tiled=True),
        lax.all_to_all(value_sum, "head", split_axis=0, concat_axis=1, tiled=True),
    )
    return (attended, query_grad, key_grad, value_grad, prompt_key_grad, prompt_value_grad)


def solution(mesh):
    placed = (
        P("resp", None, "head"),
        P("resp", None, "head"),
        P("resp", None, "head"),
        P(("resp", "head"), None),
        P(("resp", "head"), None),
        P("resp"),
        P("resp", None),
        P("resp", None, "head"),
    )
    return jax.shard_map(
        per_device,
        mesh=mesh,
        in_specs=placed,
        out_specs=(
            P("resp", None, "head"),
            P("resp", None, "head"),
            P("resp", None, "head"),
            P("resp", None, "head"),
            P(("resp", "head"), None),
            P(("resp", "head"), None),
        ),
        check_vma=False,
    )
```

profile of v0, /device:TPU:1, one launch (start us, length us, event | category | flops | bytes accessed | tf_op | source)
XLA Modules:
  0.0 827.9 jit_solution(10407376835702045725)
XLA Ops:
  7.2 0.0 all-gather.3.cloned.1.call-start
  7.2 0.7 all-gather.3.cloned.1.call-update
  7.9 0.0 all-gather.5.cloned.1.call-start
  7.9 0.7 all-gather.5.cloned.1.call-update
  8.6 0.0 all-reduce.2.cloned.1.call-start
  8.7 1.6 copy.74
  11.0 1.0 reshape.109
  12.0 0.2 copy.123
  12.2 2.5 copy.82
  14.7 1.7 reshape.110
  16.4 0.7 select_convert_fusion
  17.1 0.1 fusion.22
  17.3 6.3 fusion.11
  23.6 183.4 %all-gather.3.cloned.1.call-done = bf16[1024,1024]{1,0:T(8,128)(2,1)} async-done(((bf16[8,1024]{1,0:T(8,128)(2,1)}), bf16[1024,1024]{1,0:T(8,128)(2,1)}) %all-gather.3.cloned.1.call-update) | async-done | bytes 2097168 | tf_op jit(solution)/shard_map/all_gather | solution.py:86
  207.0 194.5 %all-gather.5.cloned.1.call-done = bf16[1024,1024]{1,0:T(8,128)(2,1)} async-done(((bf16[8,1024]{1,0:T(8,128)(2,1)}), bf16[1024,1024]{1,0:T(8,128)(2,1)}) %all-gather.5.cloned.1.call-update) | async-done | bytes 2097168 | tf_op jit(solution)/shard_map/all_gather | solution.py:85
  401.5 2.1 constant_dynamic-slice_fusion
  403.6 1.0 copy.145
  404.6 4.0 bitcast_reduce_fusion
  408.6 14.2 %exponential_reduce_fusion = f32[2,5,512]{2,1,0:T(8,128)} fusion(f32[2,512,512,5]{2,1,3,0:T(8,128)} %get-tuple-element.77, f32[2,5,512]{2,1,0:T(8,128)S(1)} %max.11, pred[512,512]{0,1:T(8,128)(4,1)S(1)} %fusion.22), kind=kLoop, calls=%fused_computation.17 | loop fusion | flops 10480640 | bytes 10788864 | tf_op jit(solution)/shard_map/while/body/eval_jaxpr/reduce_sum | solution.py:32
  422.8 3.7 fusion.4
  426.5 12.4 %fusion.16 = f32[2,128,1024,1]{2,1,3,0:T(8,128)} fusion(f32[2,1024,512,5]{2,1,3,0:T(8,128)} %copy-done, f32[2,5,512]{2,1,0:T(8,128)S(1)} %log_add_fusion, bf16[512,2,5,128]{0,3,2,1:T(8,128)(2,1)} %bitcast.152, bf16[512]{0:T(512)(128)(2,1)S(1)} %select_convert_fusion), kind=kOutput, calls=%fused_computation.28 | convolution fusion | flops 1358561280 | bytes 23352320 | tf_op jit(solution)/shard_map/rkgtj,rtkgd->jkd/dot_general | solution.py:116
  439.0 2.7 copy.96
  441.7 2.0 copy.72
  443.7 9.3 %fusion.18 = f32[2,128,5,512]{3,1,2,0:T(8,128)S(1)} fusion(bf16[1024,2,128,1]{0,2,3,1:T(8,128)(2,1)} %bitcast.162, f32[2,1024,512,5]{2,1,3,0:T(8,128)} %copy-done, f32[2,5,512]{2,1,0:T(8,128)S(1)} %log_add_fusion), kind=kOutput, calls=%fused_computation.29 | convolution fusion | flops 1357905920 | bytes 24137728 | tf_op jit(solution)/shard_map/while/body/eval_jaxpr/kgtj,jkd->tkgd/dot_general | solution.py:39
  453.1 0.2 slice-done.2
  453.3 0.3 copy-done.1
  453.6 0.1 copy-done.9
  453.7 4.2 fusion.13
  457.8 13.0 %fusion.2 = bf16[2,5,512,1024]{2,3,1,0:T(8,128)(2,1)} fusion(f32[2,1024,512,5]{2,1,3,0:T(8,128)} %copy-done, f32[2,5,512]{2,1,0:T(8,128)S(1)} %get-tuple-element.78, f32[2,5,512]{2,1,0:T(8,128)S(1)} %log_add_fusion, bf16[1024,2,128,1]{0,2,3,1:T(8,128)(2,1)} %bitcast.163, bf16[512,2,5,128]{0,3,2,1:T(8,128)(2,1)} %bitcast.153, ...), kind=kOutput, calls=%fused_computation.3 | convolution fusion | flops 1376256000 | bytes 33334272 | tf_op jit(solution)/shard_map/while/body/eval_jaxpr/tkgd,jkd->kgtj/dot_general | solution.py:51
  470.8 7.5 fusion.38
  478.3 1.3 copy.95
  479.6 3.3 pad_maximum_fusion
  483.0 7.2 fusion.37
  490.1 7.5 fusion.21
  497.7 5.2 fusion.9
  503.0 270.5 %all-reduce.2.cloned.1.call-done = f32[1024,512]{1,0:T(8,128)} async-done(((f32[1024,512]{1,0:T(8,128)}), f32[1024,512]{1,0:T(8,128)}) %all-reduce.2.cloned.1.call-update) | async-done | bytes 2097168 | tf_op jit(solution)/shard_map/psum | solution.py:119
  773.4 1.4 dynamic-slice_bitcast_fusion
  774.8 26.5 %all-to-all-start = ((f32[4,8,256]{2,1,0:T(8,128)}), f32[4,8,256]{2,1,0:T(8,128)S(1)}, u32[]{:S(2)}, u32[]{:S(2)}) async-start(f32[4,8,256]{2,1,0:T(8,128)} %get-tuple-element.73), calls=%async_computation | async-start | bytes 65536 | tf_op jit(solution)/shard_map/all_to_all | solution.py:129
  801.3 4.2 fusion.12
  805.5 0.5 all-to-all-done
  806.0 4.3 all-to-all-start.1
  810.3 4.3 fusion.20
  814.6 1.4 copy.98
  816.0 0.8 copy.99
  816.9 0.8 copy.100
  817.7 2.4 copy.97
  820.1 0.6 copy.156
  820.7 0.6 copy.157
  (44 shorter events, 0.1 us)
Async XLA Ops:
  7.2 199.8 %all-gather.3.cloned.1.call-start = ((), (), s32[]{:S(2)}) async-start(), calls=%async_computation.2 | async-start | bytes 2113536 | tf_op jit(solution)/shard_map/all_gather | solution.py:86
  7.9 393.6 %all-gather.5.cloned.1.call-start = ((), (), s32[]{:S(2)}) async-start(), calls=%async_computation.3 | async-start | bytes 2113536 | tf_op jit(solution)/shard_map/all_gather | solution.py:85
  8.6 764.8 %all-reduce.2.cloned.1.call-start = ((), (), s32[]{:S(2)}) async-start(), calls=%async_computation.4 | async-start | bytes 4194304 | tf_op jit(solution)/shard_map/psum | solution.py:119
  12.2 392.4 %copy-start.7 = (bf16[512,2,128,1]{0,2,3,1:T(8,128)(2,1)}, bf16[512,2,128,1]{0,2,3,1:T(8,128)(2,1)S(1)}, u32[]{:S(2)}) copy-start(bf16[512,2,128,1]{0,2,3,1:T(8,128)(2,1)S(1)} %copy.123) | copy-start | bytes 786436
  17.2 391.4 %copy-start.4 = (pred[512,512]{0,1:T(8,128)(4,1)}, pred[512,512]{0,1:T(8,128)(4,1)S(1)}, u32[]{:S(2)}) copy-start(pred[512,512]{0,1:T(8,128)(4,1)S(1)} %fusion.22) | copy-start | bytes 786436
  404.6 4.0 copy-start.12
  408.6 17.9 %copy-start = (f32[2,1024,512,5]{2,1,3,0:T(8,128)}, f32[2,1024,512,5]{2,1,3,0:T(8,128)S(1)}, u32[]{:S(2)}) copy-start(f32[2,1024,512,5]{2,1,3,0:T(8,128)S(1)} %get-tuple-element.75) | copy-start | bytes 62914564
  422.8 3.7 copy-start.13
  439.0 14.1 %slice-start = ((s8[10485760]{0:T(1024)(128)(4,1)}), s8[2097152]{0:T(1024)(128)(4,1)S(1)}, s32[]{:S(2)}) async-start(s8[10485760]{0:T(1024)(128)(4,1)} %bitcast.144), calls=%async_computation.5 | async-start | bytes 4194304
  443.7 9.4 %slice-start.1 = ((s8[10485760]{0:T(1024)(128)(4,1)}), s8[4194304]{0:T(1024)(128)(4,1)S(1)}, s32[]{:S(2)}) async-start(s8[10485760]{0:T(1024)(128)(4,1)} %bitcast.144), calls=%async_computation.6 | async-start | bytes 8388608
  443.7 9.6 %slice-start.2 = ((s8[10485760]{0:T(1024)(128)(4,1)}), s8[4194304]{0:T(1024)(128)(4,1)S(1)}, s32[]{:S(2)}) async-start(s8[10485760]{0:T(1024)(128)(4,1)} %bitcast.144), calls=%async_computation.7 | async-start | bytes 8388608
  443.7 9.9 %copy-start.1 = (bf16[1,512,1280]{1,2,0:T(8,128)(2,1)S(1)}, bf16[1,512,1280]{1,2,0:T(8,128)(2,1)}, u32[]{:S(2)}) copy-start(bf16[1,512,1280]{1,2,0:T(8,128)(2,1)} %copy.82) | copy-start | bytes 3932164
  443.7 9.9 %copy-start.5 = (pred[512,512]{0,1:T(8,128)(4,1)S(1)}, pred[512,512]{0,1:T(8,128)(4,1)}, u32[]{:S(2)}) copy-start(pred[512,512]{0,1:T(8,128)(4,1)} %copy-done.4) | copy-start | bytes 786436
  443.7 10.0 %copy-start.9 = (bf16[512,2,128]{2,1,0:T(2,128)(2,1)S(1)}, bf16[512,2,128]{2,1,0:T(2,128)(2,1)}, u32[]{:S(2)}) copy-start(bf16[512,2,128]{2,1,0:T(2,128)(2,1)} %reshape.110) | copy-start | bytes 786436
  470.8 12.1 %copy-start.3 = (bf16[1024,256]{0,1:T(8,128)(2,1)S(1)}, bf16[1024,256]{0,1:T(8,128)(2,1)}, u32[]{:S(2)}) copy-start(bf16[1024,256]{0,1:T(8,128)(2,1)} %copy.145) | copy-start | bytes 1572868
  479.6 10.5 %copy-start.2 = (bf16[1,512,1280]{1,2,0:T(8,128)(2,1)S(1)}, bf16[1,512,1280]{1,2,0:T(8,128)(2,1)}, u32[]{:S(2)}) copy-start(bf16[1,512,1280]{1,2,0:T(8,128)(2,1)} %copy.82) | copy-start | bytes 3932164
  479.6 10.5 %copy-start.6 = (pred[512,512]{0,1:T(8,128)(4,1)S(1)}, pred[512,512]{0,1:T(8,128)(4,1)}, u32[]{:S(2)}) copy-start(pred[512,512]{0,1:T(8,128)(4,1)} %copy-done.4) | copy-start | bytes 786436
  482.9 14.7 %slice-start.3 = ((s8[10485760]{0:T(1024)(128)(4,1)}), s8[4194304]{0:T(1024)(128)(4,1)S(1)}, s32[]{:S(2)}) async-start(s8[10485760]{0:T(1024)(128)(4,1)} %bitcast.146), calls=%async_computation.8 | async-start | bytes 8388608
  482.9 14.7 %slice-start.4 = ((s8[10485760]{0:T(1024)(128)(4,1)}), s8[4194304]{0:T(1024)(128)(4,1)S(1)}, s32[]{:S(2)}) async-start(s8[10485760]{0:T(1024)(128)(4,1)} %bitcast.146), calls=%async_computation.9 | async-start | bytes 8388608
  490.1 7.6 slice-start.5
  490.1 7.6 copy-start.10
  497.7 303.6 %copy-start.8 = (bf16[512,2,128,1]{0,2,3,1:T(8,128)(2,1)S(1)}, bf16[512,2,128,1]{0,2,3,1:T(8,128)(2,1)}, u32[]{:S(2)}) copy-start(bf16[512,2,128,1]{0,2,3,1:T(8,128)(2,1)} %copy-done.7) | copy-start | bytes 786436
  502.9 313.9 %copy-start.11 = (bf16[2,128,512]{2,1,0:T(8,128)(2,1)S(1)}, bf16[2,128,512]{2,1,0:T(8,128)(2,1)}, u32[]{:S(2)}) copy-start(bf16[2,128,512]{2,1,0:T(8,128)(2,1)} %fusion.21) | copy-start | bytes 786436
  774.8 31.2 %all-to-all-start = ((f32[4,8,256]{2,1,0:T(8,128)}), f32[4,8,256]{2,1,0:T(8,128)S(1)}, u32[]{:S(2)}, u32[]{:S(2)}) async-start(f32[4,8,256]{2,1,0:T(8,128)} %get-tuple-element.73), calls=%async_computation | async-start | bytes 65536 | tf_op jit(solution)/shard_map/all_to_all | solution.py:129
  806.0 14.1 %all-to-all-start.1 = ((f32[4,8,256]{2,1,0:T(8,128)}), f32[4,8,256]{2,1,0:T(8,128)S(1)}, u32[]{:S(2)}, u32[]{:S(2)}) async-start(f32[4,8,256]{2,1,0:T(8,128)} %get-tuple-element.72), calls=%async_computation.1 | async-start | bytes 65536 | tf_op jit(solution)/shard_map/all_to_all | solution.py:130
Sparse Core Ops, SparseCore 0:
  9.7 197.1 all-gather.2
  208.7 192.7 all-gather.4
  483.0 290.3 all-reduce.1
where the time goes:
time: 829 us; the launch traced here: 828 us
  waiting for transfers between devices  650 us (78%)
  matrix products  85 us (10%)
  starting transfers between devices  30.9 us (4%)
  local copies, waits for them, and re-layouts  25 us (3%)
  other arithmetic  22 us (3%)
  between operations  14.6 us (2%)
    psum x1, waiting for transfers between devices, per_device(): lax.psum(jnp.concatenate([key_part.reshape(prompt_rows, kv_width), value_...  270 us
    all_gather x1, waiting for transfers between devices, per_device(): lax.all_gather(prompt_keys, ('resp', 'head'), axis=0, tiled=True)  195 us
    all_gather x1, waiting for transfers between devices, per_device(): lax.all_gather(prompt_values, ('resp', 'head'), axis=0, tiled=True)  183 us
    all_to_all x1, starting transfers between devices, per_device(): lax.all_to_all(key_sum, 'head', split_axis=0, concat_axis=1, tiled=True)  26.5 us
  transfers between devices with their start and end apart: 5, of which 4 were waited for; matrix products, arithmetic and copies ran while one was open for 6% of the time, Pallas kernels for 0%

commit v1 on v0

--- a/solution.py
+++ b/solution.py
@@ -81,13 +81,20 @@
 ):
     kv_width = resp_keys.shape[2]
     kv_count = kv_width // HEAD_DIM
-    every_key, every_value = (
-        lax.all_gather(prompt_keys, ("resp", "head"), axis=0, tiled=True),
-        lax.all_gather(prompt_values, ("resp", "head"), axis=0, tiled=True),
+    rows_here = prompt_keys.shape[0]
+    groups = lax.axis_size("head")
+    devices = lax.axis_size("resp") * groups
+    both = jnp.concatenate(
+        [prompt_keys.reshape(rows_here, groups, kv_width), prompt_values.reshape(rows_here, groups, kv_width)],
+        2,
+    ).transpose(1, 0, 2)
+    outgoing = jnp.broadcast_to(both[None], (devices // groups,) + both.shape).reshape(
+        devices, rows_here, 2 * kv_width
     )
-    head_start = lax.axis_index("head") * kv_width
-    group_keys = lax.dynamic_slice_in_dim(every_key, head_start, kv_width, 1)
-    group_values = lax.dynamic_slice_in_dim(every_value, head_start, kv_width, 1)
+    gathered = lax.all_to_all(outgoing, ("resp", "head"), split_axis=0, concat_axis=0, tiled=True)
+    gathered = gathered.reshape(devices * rows_here, 2 * kv_width)
+    group_keys = gathered[:, :kv_width]
+    group_values = gathered[:, kv_width:]
     prompt_rows = group_keys.shape[0]
     prompt_key3 = group_keys.reshape(prompt_rows, kv_count, HEAD_DIM)
     prompt_value3 = group_values.reshape(prompt_rows, kv_count, HEAD_DIM)
@@ -109,26 +116,26 @@
     results = lax.map(one_response, (queries, resp_keys, resp_values, lengths, loss_mask, out_grad))
     attended, query_grad, key_grad, value_grad, prompt_ds, prompt_weight, grad_all = results
     query_all = queries.reshape(queries.shape[0], queries.shape[1], kv_count, -1, HEAD_DIM)
-    local_rows = prompt_rows // lax.axis_size("resp")
     key_part = jnp.einsum(
         "rkgtj,rtkgd->jkd", prompt_ds, query_all, preferred_element_type=jnp.float32
     )
     value_part = jnp.einsum(
         "rkgtj,rtkgd->jkd", prompt_weight, grad_all, preferred_element_type=jnp.float32
     )
-    whole_sum = lax.psum(
-        jnp.concatenate(
-            [key_part.reshape(prompt_rows, kv_width), value_part.reshape(prompt_rows, kv_width)], 1
-        ),
-        "resp",
+    both_parts = jnp.concatenate(
+        [key_part.reshape(prompt_rows, kv_width), value_part.reshape(prompt_rows, kv_width)], 1
     )
-    summed = lax.dynamic_slice_in_dim(whole_sum, lax.axis_index("resp") * local_rows, local_rows, 0)
-    key_sum = summed[:, :kv_width]
-    value_sum = summed[:, kv_width:]
-    prompt_key_grad, prompt_value_grad = (
-        lax.all_to_all(key_sum, "head", split_axis=0, concat_axis=1, tiled=True),
-        lax.all_to_all(value_sum, "head", split_axis=0, concat_axis=1, tiled=True),
+    arrived = lax.all_to_all(
+        both_parts.reshape(devices, rows_here, 2 * kv_width),
+        ("resp", "head"),
+        split_axis=0,
+        concat_axis=0,
+        tiled=True,
     )
+    summed = arrived.reshape(devices // groups, groups, rows_here, 2 * kv_width).sum(0)
+    summed = summed.transpose(1, 0, 2)
+    prompt_key_grad = summed[:, :, :kv_width].reshape(rows_here, groups * kv_width)
+    prompt_value_grad = summed[:, :, kv_width:].reshape(rows_here, groups * kv_width)
     return (attended, query_grad, key_grad, value_grad, prompt_key_grad, prompt_value_grad)
 
 

time: 829 us -> 159 us (0.19)
  waiting for transfers between devices: 650 us -> 9.5 us
  starting transfers between devices: 30.9 us -> 17.5 us
  between operations: 14.6 us -> 1.57 us
    all_gather x2 -> x0, waiting for transfers between devices: 378 us -> none  [the longest x1 195 us: per_device(): lax.all_gather(prompt_keys, ('resp', 'head'), axis=0, tiled=True)]
    psum x1 -> x0, waiting for transfers between devices: 270 us -> none  [per_device(): lax.psum(jnp.concatenate([key_part.reshape(prompt_rows, kv_width), value_...]
    all_to_all x2, starting transfers between devices: 30.8 us -> 17.5 us  [the longest x1 11.5 us: per_device(): lax.all_to_all(outgoing, ('resp', 'head'), split_axis=0, concat_axis=0, t...]
    all_to_all x2, waiting for transfers between devices: 0.5 us -> 9.5 us  [the longest x1 5.31 us: per_device(): lax.all_to_all(both_parts.reshape(devices, rows_here, 2 * kv_width), ('re...]
  transfers between devices with their start and end apart: 5 -> 2, of which waited for: 4 -> 2; matrix products, arithmetic and copies ran while one was open for 6% -> 24% of each run, Pallas kernels for 0% -> 0%
where the time goes in v1:
time: 159 us
  matrix products  81.8 us (51%)
  other arithmetic  25.7 us (16%)
  local copies, waits for them, and re-layouts  22.5 us (14%)
  starting transfers between devices  17.5 us (11%)
  waiting for transfers between devices  9.5 us (6%)
    reduce_sum x1, other arithmetic, respond(): row_total = jnp.exp(prompt_scores - row_top[..., None]).sum(-1) + jnp.exp...  14.2 us
    dot_general x1, matrix products, respond(): jnp.einsum('tkgd,jkd->kgtj', grad_five, prompt_value3, preferred_element_...  12.2 us
    all_to_all x1, starting transfers between devices, per_device(): lax.all_to_all(outgoing, ('resp', 'head'), split_axis=0, concat_axis=0, t...  11.5 us
    unnamed x34, local copies, waits for them, and re-layouts  9.74 us
    dot_general x1, matrix products, per_device(): jnp.einsum('rkgtj,rtkgd->jkd', prompt_weight, grad_all, preferred_element...  9.3 us
    dot_general x1, matrix products, respond(): jnp.einsum('kgtj,jkd->tkgd', prompt_weight, prompt_value3, preferred_elem...  9.11 us
    dot_general x1, matrix products, respond(): jnp.einsum('kgtj,jkd->tkgd', own_weight, own_value, preferred_element_typ...  8.37 us
    dot_general x1, matrix products, respond(): jnp.einsum('tkgd,jkd->kgtj', grad_five, own_value, preferred_element_type...  7.69 us
  transfers between devices with their start and end apart: 2, of which 2 were waited for; matrix products, arithmetic and copies ran while one was open for 24% of the time, Pallas kernels for 0%

profile of v1, /device:TPU:1, one launch (start us, length us, event | category | flops | bytes accessed | tf_op | source)
XLA Modules:
  0.0 158.6 jit_solution(11994433908290928384)
XLA Ops:
  0.6 0.7 maximum_bitcast_fusion
  1.4 1.1 broadcast_in_dim.78
  2.5 11.5 %all-to-all-start = ((bf16[128,8,512]{2,1,0:T(8,128)(2,1)}), bf16[128,8,512]{2,1,0:T(8,128)(2,1)S(1)}, u32[]{:S(2)}, u32[]{:S(2)}) async-start(bf16[128,8,512]{2,1,0:T(8,128)(2,1)} %bitcast.6), calls=%async_computation | async-start | bytes 2097152 | tf_op jit(solution)/shard_map/all_to_all | solution.py:94
  14.6 1.6 %copy.42 = bf16[1,512,1280]{1,2,0:T(8,128)(2,1)S(1)} copy(bf16[1,512,1280]{2,1,0:T(8,128)(2,1)} %param.8) | data formatting | bytes 2621440 | tf_op args[0]
  16.2 1.0 reshape.130
  17.3 0.2 copy.91
  17.4 0.0 copy-start.5
  17.4 2.5 %copy.50 = bf16[1,512,1280]{1,2,0:T(8,128)(2,1)} copy(bf16[1,512,1280]{2,1,0:T(8,128)(2,1)} %param.15) | data formatting | bytes 2621440 | tf_op args[7]
  20.0 1.7 %reshape.131 = bf16[512,2,128]{2,1,0:T(2,128)(2,1)} reshape(bf16[1,512,256]{2,1,0:T(8,128)(2,1)} %param.10) | data formatting | bytes 524288 | tf_op jit(solution)/shard_map/while/body/eval_jaxpr/reshape | solution.py:18
  21.7 0.7 select_convert_fusion
  22.4 0.1 fusion.25
  22.5 6.3 %fusion.11 = (f32[2,5,512]{2,1,0:T(8,128)}, f32[2,512,512,5]{2,1,3,0:T(8,128)}) fusion(pred[512,512]{0,1:T(8,128)(4,1)S(1)} %fusion.25, bf16[512,2,128,1]{0,2,3,1:T(8,128)(2,1)S(1)} %copy.91, bf16[512,2,5,128]{0,3,2,1:T(8,128)(2,1)S(1)} %bitcast.144), kind=kOutput, calls=%fused_computation.19 | convolution fusion | flops 678947840 | bytes 12341248 | tf_op jit(solution)/shard_map/while/body/eval_jaxpr/tkgd,jkd->kgtj/dot_general | solution.py:24
  28.9 4.2 %all-to-all-done = bf16[128,8,512]{2,1,0:T(8,128)(2,1)S(1)} async-done(((bf16[128,8,512]{2,1,0:T(8,128)(2,1)}), bf16[128,8,512]{2,1,0:T(8,128)(2,1)S(1)}, u32[]{:S(2)}, u32[]{:S(2)}) %all-to-all-start) | async-done | bytes 1048608 | tf_op jit(solution)/shard_map/all_to_all | solution.py:94
  33.0 0.9 fusion.40
  33.9 1.0 copy.41
  34.9 4.0 %bitcast_reduce_fusion = (f32[2,5,512]{2,1,0:T(8,128)S(1)}, f32[2,1024,512,5]{2,1,3,0:T(8,128)S(1)}) fusion(bf16[1024,2,128,1]{0,2,3,1:T(8,128)(2,1)} %bitcast.156, bf16[512,2,5,128]{0,3,2,1:T(8,128)(2,1)S(1)} %bitcast.145), kind=kOutput, calls=%fused_computation.6 | convolution fusion | flops 1352657920 | bytes 22827008 | tf_op jit(solution)/shard_map/while/body/eval_jaxpr/tkgd,jkd->kgtj/dot_general | solution.py:20
  38.9 14.2 %exponential_reduce_fusion = f32[2,5,512]{2,1,0:T(8,128)} fusion(f32[2,512,512,5]{2,1,3,0:T(8,128)} %get-tuple-element.73, f32[2,5,512]{2,1,0:T(8,128)S(1)} %max.11, pred[512,512]{0,1:T(8,128)(4,1)S(1)} %fusion.25), kind=kLoop, calls=%fused_computation.17 | loop fusion | flops 10480640 | bytes 10788864 | tf_op jit(solution)/shard_map/while/body/eval_jaxpr/reduce_sum | solution.py:32
  53.1 4.1 %fusion.4 = f32[2,5,512]{2,1,0:T(8,128)} fusion(f32[2,1024,512,5]{2,1,3,0:T(8,128)S(1)} %get-tuple-element.71, f32[2,5,512]{2,1,0:T(8,128)S(1)} %max.11), kind=kLoop, calls=%fused_computation.8 | loop fusion | flops 15723520 | bytes 21012480 | tf_op jit(solution)/shard_map/while/body/eval_jaxpr/reduce_sum | solution.py:30
  57.2 1.2 copy.40
  58.5 0.8 log_add_fusion
  59.3 0.0 copy-start.8
  59.3 0.0 copy-start.1
  59.3 9.1 %fusion.18 = f32[2,128,5,512]{3,1,2,0:T(8,128)S(1)} fusion(bf16[1024,2,128,1]{0,2,3,1:T(8,128)(2,1)S(1)} %bitcast.159, f32[2,1024,512,5]{2,1,3,0:T(8,128)} %copy-done, f32[2,5,512]{2,1,0:T(8,128)S(1)} %log_add_fusion), kind=kOutput, calls=%fused_computation.29 | convolution fusion | flops 1357905920 | bytes 24137728 | tf_op jit(solution)/shard_map/while/body/eval_jaxpr/kgtj,jkd->tkgd/dot_general | solution.py:39
  68.4 0.0 copy-start.10
  68.5 9.3 %fusion.20 = f32[1024,2,128]{0,2,1:T(8,128)S(1)} fusion(f32[2,1024,512,5]{2,1,3,0:T(8,128)} %copy-done, f32[2,5,512]{2,1,0:T(8,128)S(1)} %log_add_fusion, bf16[512,2,5,128]{0,3,2,1:T(8,128)(2,1)S(1)} %bitcast.151, bf16[512]{0:T(512)(128)(2,1)S(1)} %select_convert_fusion), kind=kOutput, calls=%fused_computation.30 | convolution fusion | flops 1358561280 | bytes 23352320 | tf_op jit(solution)/shard_map/rkgtj,rtkgd->jkd/dot_general | solution.py:122
  77.8 8.4 %fusion.13 = (f32[2,5,512]{2,1,0:T(8,128)S(1)}, bf16[512,2,5,128]{0,3,2,1:T(8,128)(2,1)}) fusion(bf16[512,2,5,128]{0,3,2,1:T(8,128)(2,1)S(1)} %bitcast.152, bf16[512]{0:T(512)(128)(2,1)S(1)} %select_convert_fusion, f32[2,512,512,5]{2,1,3,0:T(8,128)} %get-tuple-element.73, f32[2,5,512]{2,1,0:T(8,128)S(1)} %log_add_fusion, pred[512,512]{0,1:T(8,128)(4,1)S(1)} %fusion.25, ...), kind=kOutput, calls=%fused_computation.23 | convolution fusion | flops 686812160 | bytes 16295424 | tf_op jit(solution)/shard_map/while/body/eval_jaxpr/kgtj,jkd->tkgd/dot_general | solution.py:41
  86.1 12.2 %fusion.2 = bf16[2,5,512,1024]{2,3,1,0:T(8,128)(2,1)} fusion(f32[2,1024,512,5]{2,1,3,0:T(8,128)} %copy-done, f32[2,5,512]{2,1,0:T(8,128)S(1)} %get-tuple-element.74, f32[2,5,512]{2,1,0:T(8,128)S(1)} %log_add_fusion, bf16[1024,2,128,1]{0,2,3,1:T(8,128)(2,1)S(1)} %bitcast.160, bf16[512,2,5,128]{0,3,2,1:T(8,128)(2,1)S(1)} %bitcast.153, ...), kind=kOutput, calls=%fused_computation.3 | convolution fusion | flops 1376256000 | bytes 33334272 | tf_op jit(solution)/shard_map/while/body/eval_jaxpr/tkgd,jkd->kgtj/dot_general | solution.py:51
  98.4 7.7 %fusion.9 = bf16[2,5,512,512]{2,3,1,0:T(8,128)(2,1)} fusion(f32[2,512,512,5]{2,1,3,0:T(8,128)} %get-tuple-element.73, f32[2,5,512]{2,1,0:T(8,128)S(1)} %get-tuple-element.74, f32[2,5,512]{2,1,0:T(8,128)S(1)} %log_add_fusion, pred[512,512]{0,1:T(8,128)(4,1)S(1)} %fusion.25, bf16[512,2,5,128]{0,3,2,1:T(8,128)(2,1)S(1)} %bitcast.154, ...), kind=kOutput, calls=%fused_computation.14 | convolution fusion | flops 692060160 | bytes 17605632 | tf_op jit(solution)/shard_map/while/body/eval_jaxpr/tkgd,jkd->kgtj/dot_general | solution.py:54
  106.1 0.6 copy.64
  106.7 1.8 %concatenate.13 = f32[128,8,256]{2,1,0:T(8,128)} reshape(f32[1024,2,128]{2,1,0:T(2,128)S(1)} %copy.64) | data formatting | bytes 2097152 | tf_op jit(solution)/shard_map/concatenate | solution.py:125
  108.5 5.9 %convolution_bitcast_fusion = f32[1024,2,128]{2,0,1:T(8,128)S(1)} fusion(bf16[2,5,512,1024]{2,3,1,0:T(8,128)(2,1)} %fusion.2, bf16[512,2,5,128]{0,3,2,1:T(8,128)(2,1)S(1)} %bitcast.146), kind=kOutput, calls=%fused_computation.31 | convolution fusion | flops 1342177280 | bytes 12845056 | tf_op jit(solution)/shard_map/rkgtj,rtkgd->jkd/dot_general | solution.py:119
  114.3 0.8 copy.62
  115.1 1.8 %concatenate.12 = f32[128,8,256]{2,1,0:T(8,128)} reshape(f32[1024,2,128]{2,1,0:T(2,128)S(1)} %copy.62) | data formatting | bytes 2097152 | tf_op jit(solution)/shard_map/concatenate | solution.py:125
  117.0 3.3 %pad_maximum_fusion = f32[128,8,512]{2,1,0:T(8,128)} fusion(f32[128,8,256]{2,1,0:T(8,128)} %concatenate.13, f32[128,8,256]{2,1,0:T(8,128)} %concatenate.12), kind=kLoop, calls=%fused_computation.27 | loop fusion | flops 524288 | bytes 4194304 | tf_op jit(solution)/shard_map/concatenate | solution.py:125
  120.3 6.0 %all-to-all-start.1 = ((f32[128,8,512]{2,1,0:T(8,128)}), f32[128,8,512]{2,1,0:T(8,128)}, u32[]{:S(2)}, u32[]{:S(2)}) async-start(f32[128,8,512]{2,1,0:T(8,128)} %pad_maximum_fusion), calls=%async_computation.1 | async-start | bytes 4194304 | tf_op jit(solution)/shard_map/all_to_all | solution.py:128
  126.3 0.0 slice-start.1
  126.3 5.7 %fusion.42 = f32[2,128,5,512]{3,1,2,0:T(8,128)S(1)} fusion(bf16[1024,2,128,1]{0,2,3,1:T(8,128)(2,1)S(1)} %bitcast.157, bf16[2,5,512,1024]{2,3,1,0:T(8,128)(2,1)} %fusion.2), kind=kOutput, calls=%fused_computation.56 | convolution fusion | flops 1342177280 | bytes 13631488 | tf_op jit(solution)/shard_map/while/body/eval_jaxpr/kgtj,jkd->tkgd/dot_general | solution.py:61
  132.0 0.0 copy-start.9
  132.1 1.9 %fusion.12 = bf16[512,2,5,128]{0,3,2,1:T(8,128)(2,1)} fusion(f32[2,128,5,512]{3,1,2,0:T(8,128)S(1)} %fusion.42, bf16[512,2,128,1]{0,2,3,1:T(8,128)(2,1)S(1)} %copy-done.6, bf16[2,5,512,512]{2,3,1,0:T(8,128)(2,1)S(1)} %bitcast.149), kind=kOutput, calls=%fused_computation.21 | convolution fusion | flops 672399360 | bytes 9437184 | tf_op jit(solution)/shard_map/while/body/eval_jaxpr/kgtj,jkd->tkgd/dot_general | solution.py:63
  134.0 2.4 %copy.66 = bf16[1,512,1280]{2,1,0:T(8,128)(2,1)} copy(bf16[1,512,1280]{1,2,0:T(8,128)(2,1)} %bitcast.155) | data formatting | bytes 2621440
  136.4 4.3 %fusion.23 = bf16[2,512,128]{1,2,0:T(8,128)(2,1)S(1)} fusion(bf16[2,5,512,512]{2,3,1,0:T(8,128)(2,1)} %fusion.9, bf16[512,2,5,128]{0,3,2,1:T(8,128)(2,1)S(1)} %bitcast.147), kind=kOutput, calls=%fused_computation.34 | convolution fusion | flops 671219712 | bytes 6815744 | tf_op jit(solution)/shard_map/while/body/eval_jaxpr/kgtj,tkgd->jkd/dot_general | solution.py:64
  140.7 0.8 copy.67
  141.6 7.1 %fusion.24 = bf16[2,128,512]{2,1,0:T(8,128)(2,1)S(1)} fusion(bf16[512,2,5,128]{0,3,2,1:T(8,128)(2,1)} %bitcast.150, bf16[512]{0:T(512)(128)(2,1)S(1)} %select_convert_fusion, f32[2,512,512,5]{2,1,3,0:T(8,128)} %get-tuple-element.73, f32[2,5,512]{2,1,0:T(8,128)S(1)} %copy-done.9, pred[512,512]{0,1:T(8,128)(4,1)S(1)} %copy-done.4), kind=kOutput, calls=%fused_computation.35 | convolution fusion | flops 682360832 | bytes 12342272 | tf_op jit(solution)/shard_map/while/body/eval_jaxpr/kgtj,tkgd->jkd/dot_general | solution.py:65
  148.7 0.8 copy.68
  149.5 1.4 copy.65
  150.9 5.3 %all-to-all-done.1 = f32[128,8,512]{2,1,0:T(8,128)} async-done(((f32[128,8,512]{2,1,0:T(8,128)}), f32[128,8,512]{2,1,0:T(8,128)}, u32[]{:S(2)}, u32[]{:S(2)}) %all-to-all-start.1) | async-done | bytes 2097184 | tf_op jit(solution)/shard_map/all_to_all | solution.py:128
  156.3 1.7 %reduce_sum.31 = f32[4,8,512]{2,1,0:T(8,128)S(1)} reduce(f32[32,4,8,512]{3,2,1,0:T(8,128)} %bitcast.47, f32[]{:T(128)} %constant.39.clone.1), dimensions={0}, to_apply=%region_4.5 | reduce | flops 507904 | bytes 2162692 | tf_op jit(solution)/shard_map/reduce_sum | solution.py:135
  158.0 0.6 fusion.41
  (25 shorter events, 0.1 us)
Async XLA Ops:
  2.5 30.6 %all-to-all-start = ((bf16[128,8,512]{2,1,0:T(8,128)(2,1)}), bf16[128,8,512]{2,1,0:T(8,128)(2,1)S(1)}, u32[]{:S(2)}, u32[]{:S(2)}) async-start(bf16[128,8,512]{2,1,0:T(8,128)(2,1)} %bitcast.6), calls=%async_computation | async-start | bytes 2097152 | tf_op jit(solution)/shard_map/all_to_all | solution.py:94
  17.4 17.5 %copy-start.5 = (bf16[512,2,128,1]{0,2,3,1:T(8,128)(2,1)}, bf16[512,2,128,1]{0,2,3,1:T(8,128)(2,1)S(1)}, u32[]{:S(2)}) copy-start(bf16[512,2,128,1]{0,2,3,1:T(8,128)(2,1)S(1)} %copy.91) | copy-start | bytes 786436
  22.5 75.9 %copy-start.3 = (pred[512,512]{0,1:T(8,128)(4,1)}, pred[512,512]{0,1:T(8,128)(4,1)S(1)}, u32[]{:S(2)}) copy-start(pred[512,512]{0,1:T(8,128)(4,1)S(1)} %fusion.25) | copy-start | bytes 786436
  34.9 4.0 %copy-start.11 = (f32[2,5,512]{2,1,0:T(8,128)S(1)}, f32[2,5,512]{2,1,0:T(8,128)}, u32[]{:S(2)}) copy-start(f32[2,5,512]{2,1,0:T(8,128)} %get-tuple-element.72) | copy-start | bytes 61444
  38.9 18.3 %copy-start = (f32[2,1024,512,5]{2,1,3,0:T(8,128)}, f32[2,1024,512,5]{2,1,3,0:T(8,128)S(1)}, u32[]{:S(2)}) copy-start(f32[2,1024,512,5]{2,1,3,0:T(8,128)S(1)} %get-tuple-element.71) | copy-start | bytes 62914564
  59.3 39.1 %copy-start.8 = (f32[2,5,512]{2,1,0:T(8,128)}, f32[2,5,512]{2,1,0:T(8,128)S(1)}, u32[]{:S(2)}) copy-start(f32[2,5,512]{2,1,0:T(8,128)S(1)} %log_add_fusion) | copy-start | bytes 61444
  59.3 9.1 %copy-start.1 = (bf16[1,512,1280]{1,2,0:T(8,128)(2,1)S(1)}, bf16[1,512,1280]{1,2,0:T(8,128)(2,1)}, u32[]{:S(2)}) copy-start(bf16[1,512,1280]{1,2,0:T(8,128)(2,1)} %copy.50) | copy-start | bytes 3932164
  68.4 9.3 %copy-start.10 = (bf16[512,2,128]{2,1,0:T(2,128)(2,1)S(1)}, bf16[512,2,128]{2,1,0:T(2,128)(2,1)}, u32[]{:S(2)}) copy-start(bf16[512,2,128]{2,1,0:T(2,128)(2,1)} %reshape.131) | copy-start | bytes 786436
  108.5 17.8 %copy-start.2 = (bf16[1024,256]{0,1:T(8,128)(2,1)S(1)}, bf16[1024,256]{0,1:T(8,128)(2,1)}, u32[]{:S(2)}) copy-start(bf16[1024,256]{0,1:T(8,128)(2,1)} %copy.41) | copy-start | bytes 1572868
  117.0 15.0 %slice-start = ((s8[5242880]{0:T(1024)(128)(4,1)}), s8[1048576]{0:T(1024)(128)(4,1)S(1)}, s32[]{:S(2)}) async-start(s8[5242880]{0:T(1024)(128)(4,1)} %bitcast.148), calls=%async_computation.2 | async-start | bytes 2097152
  117.0 15.0 %copy-start.6 = (bf16[512,2,128,1]{0,2,3,1:T(8,128)(2,1)S(1)}, bf16[512,2,128,1]{0,2,3,1:T(8,128)(2,1)}, u32[]{:S(2)}) copy-start(bf16[512,2,128,1]{0,2,3,1:T(8,128)(2,1)} %copy-done.5) | copy-start | bytes 786436
  120.3 36.0 %all-to-all-start.1 = ((f32[128,8,512]{2,1,0:T(8,128)}), f32[128,8,512]{2,1,0:T(8,128)}, u32[]{:S(2)}, u32[]{:S(2)}) async-start(f32[128,8,512]{2,1,0:T(8,128)} %pad_maximum_fusion), calls=%async_computation.1 | async-start | bytes 4194304 | tf_op jit(solution)/shard_map/all_to_all | solution.py:128
  126.3 5.7 %slice-start.1 = ((s8[5242880]{0:T(1024)(128)(4,1)}), s8[4194304]{0:T(1024)(128)(4,1)S(1)}, s32[]{:S(2)}) async-start(s8[5242880]{0:T(1024)(128)(4,1)} %bitcast.148), calls=%async_computation.3 | async-start | bytes 8388608
  132.0 9.5 %copy-start.4 = (pred[512,512]{0,1:T(8,128)(4,1)S(1)}, pred[512,512]{0,1:T(8,128)(4,1)}, u32[]{:S(2)}) copy-start(pred[512,512]{0,1:T(8,128)(4,1)} %copy-done.3) | copy-start | bytes 786436
  132.0 9.5 %copy-start.9 = (f32[2,5,512]{2,1,0:T(8,128)S(1)}, f32[2,5,512]{2,1,0:T(8,128)}, u32[]{:S(2)}) copy-start(f32[2,5,512]{2,1,0:T(8,128)} %copy-done.8) | copy-start | bytes 61444
  140.7 8.8 %copy-start.7 = (bf16[512,2,5,128]{0,3,2,1:T(8,128)(2,1)S(1)}, bf16[512,2,5,128]{0,3,2,1:T(8,128)(2,1)}, u32[]{:S(2)}) copy-start(bf16[512,2,5,128]{0,3,2,1:T(8,128)(2,1)} %get-tuple-element.75) | copy-start | bytes 3932164

commit v2 on v1

v2 whole, which is shorter than its diff:
```python
import functools

import jax
import jax.numpy as jnp
from jax import lax
from jax.experimental import pallas as pl
from jax.experimental.pallas import tpu as pltpu
from jax.sharding import PartitionSpec as P

HEAD_DIM = 128
NT = (((1,), (1,)), ((), ()))
TN = (((0,), (0,)), ((), ()))


def attention_kernel(
    length_ref, q_ref, do_ref, kp_ref, vp_ref, ko_ref, vo_ref, keep_ref,
    att_ref, dq_ref, dko_ref, dvo_ref, pg_ref, dko_acc, dvo_acc,
):
    f32, bf16 = jnp.float32, jnp.bfloat16
    k = pl.program_id(0)
    g = pl.program_id(1)
    scale = HEAD_DIM ** (-0.5)
    length = length_ref[0]
    steps = q_ref.shape[0]
    q = q_ref[...]
    kp = kp_ref[...]
    ko = ko_ref[...]
    vp = vp_ref[...]
    vo = vo_ref[...]
    sp = lax.dot_general(q, kp, NT, preferred_element_type=f32) * scale
    so = lax.dot_general(q, ko, NT, preferred_element_type=f32) * scale
    t = lax.broadcasted_iota(jnp.int32, (steps, 1), 0)
    j = lax.broadcasted_iota(jnp.int32, (1, steps), 1)
    allowed = (j <= t) & (j < length)
    so = jnp.where(allowed, so, -jnp.inf)
    top = jnp.maximum(sp.max(-1, keepdims=True), so.max(-1, keepdims=True))
    total = jnp.exp(sp - top).sum(-1, keepdims=True) + jnp.exp(so - top).sum(-1, keepdims=True)
    log_total = top + jnp.log(total)
    pp = jnp.exp(sp - log_total)
    po = jnp.exp(so - log_total)
    wp = pp.astype(bf16)
    wo = po.astype(bf16)
    live = t < length
    out = jnp.dot(wp, vp, preferred_element_type=f32) + jnp.dot(wo, vo, preferred_element_type=f32)
    att = jnp.where(live, out, 0.0).astype(bf16)
    att_ref[...] = att
    factor = (keep_ref[...] * live.astype(jnp.int32)).astype(bf16)
    do = do_ref[...] * factor
    delta = (do.astype(f32) * att.astype(f32)).sum(-1, keepdims=True)
    dpp = lax.dot_general(do, vp, NT, preferred_element_type=f32)
    dpo = lax.dot_general(do, vo, NT, preferred_element_type=f32)
    dsp = (pp * (dpp - delta) * scale).astype(bf16)
    dso = (po * (dpo - delta) * scale).astype(bf16)
    dq = jnp.dot(dsp, kp, preferred_element_type=f32) + jnp.dot(dso, ko, preferred_element_type=f32)
    dq_ref[...] = dq.astype(bf16)
    dkp = lax.dot_general(dsp, q, TN, preferred_element_type=f32)
    dvp = lax.dot_general(wp, do, TN, preferred_element_type=f32)
    dko = lax.dot_general(dso, q, TN, preferred_element_type=f32)
    dvo = lax.dot_general(wo, do, TN, preferred_element_type=f32)
    width = HEAD_DIM
    kcol = pl.ds(pl.multiple_of(k * width, width), width)
    vcol = pl.ds(pl.multiple_of((k + pl.num_programs(0)) * width, width), width)

    @pl.when(g == 0)
    def _():
        dko_acc[...] = dko
        dvo_acc[...] = dvo
        pg_ref[:, kcol] = dkp
        pg_ref[:, vcol] = dvp

    @pl.when(g > 0)
    def _():
        dko_acc[...] += dko
        dvo_acc[...] += dvo
        pg_ref[:, kcol] += dkp
        pg_ref[:, vcol] += dvp

    @pl.when(g == pl.num_programs(1) - 1)
    def _():
        dko_ref[...] = dko_acc[...].astype(bf16)
        dvo_ref[...] = dvo_acc[...].astype(bf16)


def attend(length, queries, out_grad, prompt_kv, keys, values, keep, kv_count):
    steps, width = queries.shape
    group_size = width // (kv_count * HEAD_DIM)
    prompt_rows = prompt_kv.shape[0]
    head_block = lambda k, g, n: (0, k * group_size + g)
    kv_block = lambda k, g, n: (0, k)
    bf16, f32 = jnp.bfloat16, jnp.float32
    return pl.pallas_call(
        attention_kernel,
        out_shape=(
            jax.ShapeDtypeStruct((steps, width), bf16),
            jax.ShapeDtypeStruct((steps, width), bf16),
            jax.ShapeDtypeStruct(keys.shape, bf16),
            jax.ShapeDtypeStruct(keys.shape, bf16),
            jax.ShapeDtypeStruct((prompt_rows, 2 * kv_count * HEAD_DIM), f32),
        ),
        grid_spec=pltpu.PrefetchScalarGridSpec(
            num_scalar_prefetch=1,
            grid=(kv_count, group_size),
            in_specs=[
                pl.BlockSpec((steps, HEAD_DIM), head_block),
                pl.BlockSpec((steps, HEAD_DIM), head_block),
                pl.BlockSpec((prompt_rows, HEAD_DIM), kv_block),
                pl.BlockSpec((prompt_rows, HEAD_DIM), lambda k, g, n: (0, k + kv_count)),
                pl.BlockSpec((steps, HEAD_DIM), kv_block),
                pl.BlockSpec((steps, HEAD_DIM), kv_block),
                pl.BlockSpec((steps, 1), lambda k, g, n: (0, 0)),
            ],
            out_specs=[
                pl.BlockSpec((steps, HEAD_DIM), head_block),
                pl.BlockSpec((steps, HEAD_DIM), head_block),
                pl.BlockSpec((steps, HEAD_DIM), kv_block),
                pl.BlockSpec((steps, HEAD_DIM), kv_block),
                pl.BlockSpec((prompt_rows, 2 * kv_count * HEAD_DIM), lambda k, g, n: (0, 0)),
            ],
            scratch_shapes=[pltpu.VMEM((steps, HEAD_DIM), f32)] * 2,
        ),
        compiler_params=pltpu.CompilerParams(
            dimension_semantics=("arbitrary", "arbitrary"),
            vmem_limit_bytes=60 * 1024 * 1024,
        ),
    )(length, queries, out_grad, prompt_kv, prompt_kv, keys, values, keep)


def per_device(
    queries, resp_keys, resp_values, prompt_keys, prompt_values, lengths, loss_mask, out_grad
):
    kv_width = resp_keys.shape[2]
    kv_count = kv_width // HEAD_DIM
    rows_here = prompt_keys.shape[0]
    groups = lax.axis_size("head")
    devices = lax.axis_size("resp") * groups
    both = jnp.concatenate(
        [prompt_keys.reshape(rows_here, groups, kv_width), prompt_values.reshape(rows_here, groups, kv_width)],
        2,
    ).transpose(1, 0, 2)
    outgoing = jnp.broadcast_to(both[None], (devices // groups,) + both.shape).reshape(
        devices, rows_here, 2 * kv_width
    )
    gathered = lax.all_to_all(outgoing, ("resp", "head"), split_axis=0, concat_axis=0, tiled=True)
    prompt_kv = gathered.reshape(devices * rows_here, 2 * kv_width)

    steps = queries.shape[1]
    att, dq, dk, dv, prompt_parts = attend(
        lengths,
        queries.reshape(steps, -1),
        out_grad.reshape(steps, -1),
        prompt_kv,
        resp_keys.reshape(steps, kv_width),
        resp_values.reshape(steps, kv_width),
        loss_mask.reshape(steps, 1),
        kv_count,
    )
    arrived = lax.all_to_all(
        prompt_parts.reshape(devices, rows_here, 2 * kv_width),
        ("resp", "head"),
        split_axis=0,
        concat_axis=0,
        tiled=True,
    )
    summed = arrived.reshape(devices // groups, groups, rows_here, 2 * kv_width).sum(0)
    summed = summed.transpose(1, 0, 2)
    prompt_key_grad = summed[:, :, :kv_width].reshape(rows_here, groups * kv_width)
    prompt_value_grad = summed[:, :, kv_width:].reshape(rows_here, groups * kv_width)
    return (
        att.reshape(queries.shape),
        dq.reshape(queries.shape),
        dk.reshape(resp_keys.shape),
        dv.reshape(resp_keys.shape),
        prompt_key_grad,
        prompt_value_grad,
    )


def solution(mesh):
    placed = (
        P("resp", None, "head"),
        P("resp", None, "head"),
        P("resp", None, "head"),
        P(("resp", "head"), None),
        P(("resp", "head"), None),
        P("resp"),
        P("resp", None),
        P("resp", None, "head"),
    )
    return jax.shard_map(
        per_device,
        mesh=mesh,
        in_specs=placed,
        out_specs=(
            P("resp", None, "head"),
            P("resp", None, "head"),
            P("resp", None, "head"),
            P("resp", None, "head"),
            P(("resp", "head"), None),
            P(("resp", "head"), None),
        ),
        check_vma=False,
    )
```

time: 159 us -> 113 us (0.71)
  matrix products: 81.8 us -> 0 us
  Pallas kernels: 0 us -> 42.5 us
  blocking collectives: 0 us -> 35.3 us
  other arithmetic: 25.7 us -> 0.88 us
  local copies, waits for them, and re-layouts: 22.5 us -> 3.57 us
  waiting for transfers between devices: 9.5 us -> 17.6 us
  starting transfers between devices: 17.5 us -> 11.5 us
    dot_general x12 -> x0, matrix products: 81.8 us -> none  [the longest x1 12.2 us: respond(): jnp.einsum('tkgd,jkd->kgtj', grad_five, prompt_value3, preferred_element_...]
    pallas_call x0 -> x1, Pallas kernels: none -> 42.5 us  [attend(): pl.pallas_call(attention_kernel, out_shape=(jax.ShapeDtypeStruct((steps,...]
    all_to_all x0 -> x1, blocking collectives: none -> 35.3 us  [per_device(): lax.all_to_all(prompt_parts.reshape(devices, rows_here, 2 * kv_width), ('...]
    reduce_sum x2 -> x0, other arithmetic: 18.3 us -> none  [the longest x1 14.2 us: respond(): row_total = jnp.exp(prompt_scores - row_top[..., None]).sum(-1) + jnp.exp...]
    all_to_all x1, waiting for transfers between devices: 4.19 us -> 17.6 us  [per_device(): lax.all_to_all(outgoing, ('resp', 'head'), split_axis=0, concat_axis=0, t...]
    unnamed x34 -> x4, local copies, waits for them, and re-layouts: 9.74 us -> 1 us
    all_to_all x1 -> x0, starting transfers between devices: 6.04 us -> none  [per_device(): lax.all_to_all(both_parts.reshape(devices, rows_here, 2 * kv_width), ('re...]
    all_to_all x1 -> x0, waiting for transfers between devices: 5.31 us -> none  [per_device(): lax.all_to_all(both_parts.reshape(devices, rows_here, 2 * kv_width), ('re...]
  transfers between devices with their start and end apart: 2 -> 1, of which waited for: 2 -> 1; matrix products, arithmetic and copies ran while one was open for 24% -> 1% of each run, Pallas kernels for 0% -> 0%
where the time goes in v2:
time: 113 us
  Pallas kernels  42.5 us (38%)
  blocking collectives  35.3 us (31%)
  waiting for transfers between devices  17.6 us (16%)
  starting transfers between devices  11.5 us (10%)
  local copies, waits for them, and re-layouts  3.57 us (3%)
  between operations  1.31 us (1%)
    pallas_call x1, Pallas kernels, attend(): pl.pallas_call(attention_kernel, out_shape=(jax.ShapeDtypeStruct((steps,...  42.5 us
    all_to_all x1, blocking collectives, per_device(): lax.all_to_all(prompt_parts.reshape(devices, rows_here, 2 * kv_width), ('...  35.3 us
    all_to_all x1, waiting for transfers between devices, per_device(): lax.all_to_all(outgoing, ('resp', 'head'), split_axis=0, concat_axis=0, t...  17.6 us
    all_to_all x1, starting transfers between devices, per_device(): lax.all_to_all(outgoing, ('resp', 'head'), split_axis=0, concat_axis=0, t...  11.5 us
  transfers between devices with their start and end apart: 1, of which 1 were waited for; matrix products, arithmetic and copies ran while one was open for 1% of the time, Pallas kernels for 0%

profile of v2, /device:TPU:1, one launch (start us, length us, event | category | flops | bytes accessed | tf_op | source)
XLA Modules:
  0.0 112.6 jit_solution(1884972851062974684)
XLA Ops:
  0.6 0.7 maximum_bitcast_fusion
  1.4 1.1 broadcast_in_dim.2
  2.5 0.0 copy-start.1
  2.5 11.5 %all-to-all-start = ((bf16[128,8,512]{2,1,0:T(8,128)(2,1)}), bf16[128,8,512]{2,1,0:T(8,128)(2,1)S(1)}, u32[]{:S(2)}, u32[]{:S(2)}) async-start(bf16[128,8,512]{2,1,0:T(8,128)(2,1)} %bitcast.5), calls=%async_computation | async-start | bytes 2097152 | tf_op jit(solution)/shard_map/all_to_all | solution.py:143
  14.6 0.0 copy-done.1
  14.6 0.8 copy.14.keep_ref
  15.5 17.6 %all-to-all-done = bf16[128,8,512]{2,1,0:T(8,128)(2,1)S(1)} async-done(((bf16[128,8,512]{2,1,0:T(8,128)(2,1)}), bf16[128,8,512]{2,1,0:T(8,128)(2,1)S(1)}, u32[]{:S(2)}, u32[]{:S(2)}) %all-to-all-start) | async-done | bytes 1048608 | tf_op jit(solution)/shard_map/all_to_all | solution.py:143
  33.0 0.0 copy-start
  33.0 1.0 copy-done
  34.0 42.5 %shard_map.127 = (bf16[512,1280]{1,0:T(8,128)(2,1)}, bf16[512,1280]{1,0:T(8,128)(2,1)}, bf16[512,256]{1,0:T(8,128)(2,1)}, bf16[512,256]{1,0:T(8,128)(2,1)}, f32[1024,512]{1,0:T(8,128)}) custom-call(s32[1]{0:T(128)S(6)} %copy.15.length_ref, bf16[512,1280]{1,0:T(8,128)(2,1)} %bitcast.24, bf16[512,1280]{1,0:T(8,128)(2,1)} %bitcast.25, ...), custom_call_target="tpu_custom_call" | custom-call | tf_op jit(solution)/shard_map/pallas_call | solution.py:91
  76.5 35.3 %all_to_all.10 = f32[128,8,512]{2,1,0:T(8,128)S(1)} all-to-all(f32[128,8,512]{2,1,0:T(8,128)} %bitcast.23), channel_id=1, replica_groups=mesh['resp'=32,'head'=4] {'resp','head'}, dimensions={0} | all-to-all | bytes 4194304 | tf_op jit(solution)/shard_map/all_to_all | solution.py:157
  111.8 0.1 reduce_sum.9
  112.0 0.6 fusion
Async XLA Ops:
  2.5 12.2 %copy-start.1 = (s32[1,512]{1,0:T(1,128)S(1)}, s32[1,512]{1,0:T(1,128)}, u32[]{:S(2)}) copy-start(s32[1,512]{1,0:T(1,128)} %param.14) | copy-start | bytes 6148
  2.5 30.6 %all-to-all-start = ((bf16[128,8,512]{2,1,0:T(8,128)(2,1)}), bf16[128,8,512]{2,1,0:T(8,128)(2,1)S(1)}, u32[]{:S(2)}, u32[]{:S(2)}) async-start(bf16[128,8,512]{2,1,0:T(8,128)(2,1)} %bitcast.5), calls=%async_computation | async-start | bytes 2097152 | tf_op jit(solution)/shard_map/all_to_all | solution.py:143
  33.0 1.0 copy-start

commit v3 on v2

--- a/solution.py
+++ b/solution.py
@@ -155,13 +155,13 @@
         kv_count,
     )
     arrived = lax.all_to_all(
-        prompt_parts.reshape(devices, rows_here, 2 * kv_width),
+        prompt_parts.astype(jnp.bfloat16).reshape(devices, rows_here, 2 * kv_width),
         ("resp", "head"),
         split_axis=0,
         concat_axis=0,
         tiled=True,
     )
-    summed = arrived.reshape(devices // groups, groups, rows_here, 2 * kv_width).sum(0)
+    summed = arrived.astype(jnp.float32).reshape(devices // groups, groups, rows_here, 2 * kv_width).sum(0)
     summed = summed.transpose(1, 0, 2)
     prompt_key_grad = summed[:, :, :kv_width].reshape(rows_here, groups * kv_width)
     prompt_value_grad = summed[:, :, kv_width:].reshape(rows_here, groups * kv_width)

time: 113 us -> 103 us (0.912)
  blocking collectives: 35.3 us -> 23.2 us
  other arithmetic: 0.88 us -> 2.62 us
    all_to_all x1, blocking collectives: 35.3 us -> 23.2 us  [per_device(): lax.all_to_all(prompt_parts.astype(jnp.bfloat16).reshape(devices, rows_he...]
    reshape x0 -> x1, other arithmetic: none -> 1.73 us  [per_device(): prompt_parts.astype(jnp.bfloat16).reshape(devices, rows_here, 2 * kv_width)]
where the time goes in v3:
time: 103 us; the launch traced here: 102 us
  Pallas kernels  42.5 us (41%)
  blocking collectives  23.2 us (23%)
  waiting for transfers between devices  17.6 us (17%)
  starting transfers between devices  11.5 us (11%)
  local copies, waits for them, and re-layouts  3.57 us (3%)
  other arithmetic  2.62 us (3%)
  between operations  1.31 us (1%)
    pallas_call x1, Pallas kernels, attend(): pl.pallas_call(attention_kernel, out_shape=(jax.ShapeDtypeStruct((steps,...  42.5 us
    all_to_all x1, blocking collectives, per_device(): lax.all_to_all(prompt_parts.astype(jnp.bfloat16).reshape(devices, rows_he...  23.2 us
    all_to_all x1, waiting for transfers between devices, per_device(): lax.all_to_all(outgoing, ('resp', 'head'), split_axis=0, concat_axis=0, t...  17.6 us
    all_to_all x1, starting transfers between devices, per_device(): lax.all_to_all(outgoing, ('resp', 'head'), split_axis=0, concat_axis=0, t...  11.5 us
  transfers between devices with their start and end apart: 1, of which 1 were waited for; matrix products, arithmetic and copies ran while one was open for 1% of the time, Pallas kernels for 0%

profile of v3, /device:TPU:1, one launch (start us, length us, event | category | flops | bytes accessed | tf_op | source)
XLA Modules:
  0.0 102.2 jit_solution(6009456687957654941)
XLA Ops:
  0.6 0.7 maximum_bitcast_fusion
  1.4 1.1 %broadcast_in_dim.2 = bf16[32,4,8,512]{3,2,1,0:T(8,128)(2,1)} broadcast(bf16[4,8,512]{2,1,0:T(8,128)(2,1)S(1)} %maximum_bitcast_fusion), dimensions={1,2,3} | broadcast | bytes 1081344 | tf_op jit(solution)/shard_map/broadcast_in_dim | solution.py:140
  2.5 0.0 copy-start.1
  2.5 11.5 %all-to-all-start = ((bf16[128,8,512]{2,1,0:T(8,128)(2,1)}), bf16[128,8,512]{2,1,0:T(8,128)(2,1)S(1)}, u32[]{:S(2)}, u32[]{:S(2)}) async-start(bf16[128,8,512]{2,1,0:T(8,128)(2,1)} %bitcast.5), calls=%async_computation | async-start | bytes 2097152 | tf_op jit(solution)/shard_map/all_to_all | solution.py:143
  14.6 0.0 copy-done.1
  14.6 0.8 copy.14.keep_ref
  15.5 17.6 %all-to-all-done = bf16[128,8,512]{2,1,0:T(8,128)(2,1)S(1)} async-done(((bf16[128,8,512]{2,1,0:T(8,128)(2,1)}), bf16[128,8,512]{2,1,0:T(8,128)(2,1)S(1)}, u32[]{:S(2)}, u32[]{:S(2)}) %all-to-all-start) | async-done | bytes 1048608 | tf_op jit(solution)/shard_map/all_to_all | solution.py:143
  33.0 0.0 copy-start
  33.0 1.0 copy-done
  34.0 42.5 %shard_map.127 = (bf16[512,1280]{1,0:T(8,128)(2,1)}, bf16[512,1280]{1,0:T(8,128)(2,1)}, bf16[512,256]{1,0:T(8,128)(2,1)}, bf16[512,256]{1,0:T(8,128)(2,1)}, f32[1024,512]{1,0:T(8,128)}) custom-call(s32[1]{0:T(128)S(6)} %copy.15.length_ref, bf16[512,1280]{1,0:T(8,128)(2,1)} %bitcast.25, bf16[512,1280]{1,0:T(8,128)(2,1)} %bitcast.26, ...), custom_call_target="tpu_custom_call" | custom-call | tf_op jit(solution)/shard_map/pallas_call | solution.py:91
  76.5 1.7 %convert_bitcast_fusion = bf16[128,8,512]{2,1,0:T(8,128)(2,1)S(1)} fusion(f32[1024,512]{1,0:T(8,128)} %get-tuple-element.15), kind=kLoop, calls=%fused_computation.1 | loop fusion | flops 524288 | bytes 3145728 | tf_op jit(solution)/shard_map/reshape | solution.py:158
  78.3 23.2 %all_to_all.10 = bf16[128,8,512]{2,1,0:T(8,128)(2,1)S(1)} all-to-all(bf16[128,8,512]{2,1,0:T(8,128)(2,1)S(1)} %convert_bitcast_fusion), channel_id=1, replica_groups=mesh['resp'=32,'head'=4] {'resp','head'}, dimensions={0} | all-to-all | bytes 2097152 | tf_op jit(solution)/shard_map/all_to_all | solution.py:157
  101.4 0.2 convert_reduce_fusion
  101.6 0.6 fusion
Async XLA Ops:
  2.5 12.2 %copy-start.1 = (s32[1,512]{1,0:T(1,128)S(1)}, s32[1,512]{1,0:T(1,128)}, u32[]{:S(2)}) copy-start(s32[1,512]{1,0:T(1,128)} %param.14) | copy-start | bytes 6148
  2.5 30.6 %all-to-all-start = ((bf16[128,8,512]{2,1,0:T(8,128)(2,1)}), bf16[128,8,512]{2,1,0:T(8,128)(2,1)S(1)}, u32[]{:S(2)}, u32[]{:S(2)}) async-start(bf16[128,8,512]{2,1,0:T(8,128)(2,1)} %bitcast.5), calls=%async_computation | async-start | bytes 2097152 | tf_op jit(solution)/shard_map/all_to_all | solution.py:143
  33.0 1.0 copy-start

commit v4 on v3

--- a/solution.py
+++ b/solution.py
@@ -13,12 +13,11 @@
 
 
 def attention_kernel(
-    length_ref, q_ref, do_ref, kp_ref, vp_ref, ko_ref, vo_ref, keep_ref,
-    att_ref, dq_ref, dko_ref, dvo_ref, pg_ref, dko_acc, dvo_acc,
+    n_alias, length_ref, q_ref, do_ref, kp_ref, vp_ref, ko_ref, vo_ref, keep_ref, *rest
 ):
+    att_ref, dq_ref, dko_ref, dvo_ref, pg_ref, dko_acc, dvo_acc = rest[n_alias:]
     f32, bf16 = jnp.float32, jnp.bfloat16
-    k = pl.program_id(0)
-    g = pl.program_id(1)
+    g = pl.program_id(0)
     scale = HEAD_DIM ** (-0.5)
     length = length_ref[0]
     steps = q_ref.shape[0]
@@ -57,9 +56,8 @@
     dvp = lax.dot_general(wp, do, TN, preferred_element_type=f32)
     dko = lax.dot_general(dso, q, TN, preferred_element_type=f32)
     dvo = lax.dot_general(wo, do, TN, preferred_element_type=f32)
-    width = HEAD_DIM
-    kcol = pl.ds(pl.multiple_of(k * width, width), width)
-    vcol = pl.ds(pl.multiple_of((k + pl.num_programs(0)) * width, width), width)
+    kcol = slice(0, HEAD_DIM)
+    vcol = slice(HEAD_DIM, 2 * HEAD_DIM)
 
     @pl.when(g == 0)
     def _():
@@ -75,54 +73,63 @@
         pg_ref[:, kcol] += dkp
         pg_ref[:, vcol] += dvp
 
-    @pl.when(g == pl.num_programs(1) - 1)
+    @pl.when(g == pl.num_programs(0) - 1)
     def _():
         dko_ref[...] = dko_acc[...].astype(bf16)
         dvo_ref[...] = dvo_acc[...].astype(bf16)
 
 
-def attend(length, queries, out_grad, prompt_kv, keys, values, keep, kv_count):
+def attend(k, length, queries, out_grad, prompt_kv, keys, values, keep, kv_count, earlier):
     steps, width = queries.shape
     group_size = width // (kv_count * HEAD_DIM)
     prompt_rows = prompt_kv.shape[0]
-    head_block = lambda k, g, n: (0, k * group_size + g)
-    kv_block = lambda k, g, n: (0, k)
+    head_block = lambda g, n: (0, k * group_size + g)
+    kv_block = lambda g, n: (0, k)
     bf16, f32 = jnp.bfloat16, jnp.float32
+    n_alias = len(earlier)
+    heads_flops = 2 * steps * (prompt_rows + steps) * HEAD_DIM * 6 * group_size
     return pl.pallas_call(
-        attention_kernel,
+        functools.partial(attention_kernel, n_alias),
         out_shape=(
             jax.ShapeDtypeStruct((steps, width), bf16),
             jax.ShapeDtypeStruct((steps, width), bf16),
             jax.ShapeDtypeStruct(keys.shape, bf16),
             jax.ShapeDtypeStruct(keys.shape, bf16),
-            jax.ShapeDtypeStruct((prompt_rows, 2 * kv_count * HEAD_DIM), f32),
+            jax.ShapeDtypeStruct((prompt_rows, 2 * HEAD_DIM), f32),
         ),
         grid_spec=pltpu.PrefetchScalarGridSpec(
             num_scalar_prefetch=1,
-            grid=(kv_count, group_size),
+            grid=(group_size,),
             in_specs=[
                 pl.BlockSpec((steps, HEAD_DIM), head_block),
                 pl.BlockSpec((steps, HEAD_DIM), head_block),
-                pl.BlockSpec((prompt_rows, HEAD_DIM), kv_block),
-                pl.BlockSpec((prompt_rows, HEAD_DIM), lambda k, g, n: (0, k + kv_count)),
-                pl.BlockSpec((steps, HEAD_DIM), kv_block),
-                pl.BlockSpec((steps, HEAD_DIM), kv_block),
-                pl.BlockSpec((steps, 1), lambda k, g, n: (0, 0)),
-            ],
+                pl.BlockSpec((prompt_rows, HEAD_DIM), lambda g, n: (0, 0)),
+                pl.BlockSpec((prompt_rows, HEAD_DIM), lambda g, n: (0, 1)),
+                pl.BlockSpec((steps, HEAD_DIM), kv_block),
+                pl.BlockSpec((steps, HEAD_DIM), kv_block),
+                pl.BlockSpec((steps, 1), lambda g, n: (0, 0)),
+            ]
+            + [pl.BlockSpec(memory_space=pl.ANY)] * n_alias,
             out_specs=[
                 pl.BlockSpec((steps, HEAD_DIM), head_block),
                 pl.BlockSpec((steps, HEAD_DIM), head_block),
                 pl.BlockSpec((steps, HEAD_DIM), kv_block),
                 pl.BlockSpec((steps, HEAD_DIM), kv_block),
-                pl.BlockSpec((prompt_rows, 2 * kv_count * HEAD_DIM), lambda k, g, n: (0, 0)),
+                pl.BlockSpec((prompt_rows, 2 * HEAD_DIM), lambda g, n: (0, 0)),
             ],
             scratch_shapes=[pltpu.VMEM((steps, HEAD_DIM), f32)] * 2,
         ),
+        input_output_aliases={8 + i: i for i in range(n_alias)},
         compiler_params=pltpu.CompilerParams(
-            dimension_semantics=("arbitrary", "arbitrary"),
+            dimension_semantics=("arbitrary",),
             vmem_limit_bytes=60 * 1024 * 1024,
         ),
-    )(length, queries, out_grad, prompt_kv, prompt_kv, keys, values, keep)
+        cost_estimate=pl.CostEstimate(
+            flops=heads_flops,
+            transcendentals=steps * (prompt_rows + steps) * group_size,
+            bytes_accessed=4 * steps * width // kv_count + 4 * prompt_rows * HEAD_DIM * 4,
+        ),
+    )(length, queries, out_grad, prompt_kv, prompt_kv, keys, values, keep, *earlier)
 
 
 def per_device(
@@ -133,38 +140,45 @@
     rows_here = prompt_keys.shape[0]
     groups = lax.axis_size("head")
     devices = lax.axis_size("resp") * groups
-    both = jnp.concatenate(
-        [prompt_keys.reshape(rows_here, groups, kv_width), prompt_values.reshape(rows_here, groups, kv_width)],
-        2,
-    ).transpose(1, 0, 2)
-    outgoing = jnp.broadcast_to(both[None], (devices // groups,) + both.shape).reshape(
-        devices, rows_here, 2 * kv_width
-    )
-    gathered = lax.all_to_all(outgoing, ("resp", "head"), split_axis=0, concat_axis=0, tiled=True)
-    prompt_kv = gathered.reshape(devices * rows_here, 2 * kv_width)
-
     steps = queries.shape[1]
-    att, dq, dk, dv, prompt_parts = attend(
-        lengths,
-        queries.reshape(steps, -1),
-        out_grad.reshape(steps, -1),
-        prompt_kv,
-        resp_keys.reshape(steps, kv_width),
-        resp_values.reshape(steps, kv_width),
-        loss_mask.reshape(steps, 1),
-        kv_count,
-    )
-    arrived = lax.all_to_all(
-        prompt_parts.astype(jnp.bfloat16).reshape(devices, rows_here, 2 * kv_width),
-        ("resp", "head"),
-        split_axis=0,
-        concat_axis=0,
-        tiled=True,
-    )
-    summed = arrived.astype(jnp.float32).reshape(devices // groups, groups, rows_here, 2 * kv_width).sum(0)
-    summed = summed.transpose(1, 0, 2)
-    prompt_key_grad = summed[:, :, :kv_width].reshape(rows_here, groups * kv_width)
-    prompt_value_grad = summed[:, :, kv_width:].reshape(rows_here, groups * kv_width)
+    queries2 = queries.reshape(steps, -1)
+    out_grad2 = out_grad.reshape(steps, -1)
+    keys2 = resp_keys.reshape(steps, kv_width)
+    values2 = resp_values.reshape(steps, kv_width)
+    keep = loss_mask.reshape(steps, 1)
+    both = jnp.stack(
+        [
+            prompt_keys.reshape(rows_here, groups, kv_count, HEAD_DIM),
+            prompt_values.reshape(rows_here, groups, kv_count, HEAD_DIM),
+        ],
+        3,
+    )
+    earlier = ()
+    grads = []
+    for k in range(kv_count):
+        mine = both[:, :, k].transpose(1, 0, 2, 3).reshape(groups, rows_here, 2 * HEAD_DIM)
+        outgoing = jnp.broadcast_to(mine[None], (devices // groups,) + mine.shape).reshape(
+            devices, rows_here, 2 * HEAD_DIM
+        )
+        gathered = lax.all_to_all(outgoing, ("resp", "head"), split_axis=0, concat_axis=0, tiled=True)
+        prompt_kv = gathered.reshape(devices * rows_here, 2 * HEAD_DIM)
+        *earlier, prompt_parts = attend(
+            k, lengths, queries2, out_grad2, prompt_kv, keys2, values2, keep, kv_count, tuple(earlier)
+        )
+        arrived = lax.all_to_all(
+            prompt_parts.astype(jnp.bfloat16).reshape(devices, rows_here, 2 * HEAD_DIM),
+            ("resp", "head"),
+            split_axis=0,
+            concat_axis=0,
+            tiled=True,
+        )
+        grads.append(
+            arrived.astype(jnp.float32).reshape(devices // groups, groups, rows_here, 2, HEAD_DIM).sum(0)
+        )
+    att, dq, dk, dv = earlier
+    summed = jnp.stack(grads, 3).transpose(2, 1, 0, 3, 4)
+    prompt_key_grad = summed[0].reshape(rows_here, groups * kv_width)
+    prompt_value_grad = summed[1].reshape(rows_here, groups * kv_width)
     return (
         att.reshape(queries.shape),
         dq.reshape(queries.shape),

time: 103 us -> 123 us (1.19)
  blocking collectives: 23.2 us -> 0 us
  waiting for transfers between devices: 17.6 us -> 38.2 us
  starting transfers between devices: 11.5 us -> 30.4 us
  other arithmetic: 2.62 us -> 3.95 us
    all_to_all x0 -> x2, waiting for transfers between devices: none -> 26.2 us  [per_device(): lax.all_to_all(prompt_parts.astype(jnp.bfloat16).reshape(devices, rows_he...]
    all_to_all x1 -> x0, blocking collectives: 23.2 us -> none  [per_device(): lax.all_to_all(prompt_parts.astype(jnp.bfloat16).reshape(devices, rows_he...]
    all_to_all x0 -> x2, starting transfers between devices: none -> 14.4 us  [per_device(): lax.all_to_all(prompt_parts.astype(jnp.bfloat16).reshape(devices, rows_he...]
    all_to_all x1 -> x2, waiting for transfers between devices: 17.6 us -> 12 us  [per_device(): lax.all_to_all(outgoing, ('resp', 'head'), split_axis=0, concat_axis=0, t...]
    all_to_all x1 -> x2, starting transfers between devices: 11.5 us -> 16 us  [per_device(): lax.all_to_all(outgoing, ('resp', 'head'), split_axis=0, concat_axis=0, t...]
    reshape x1 -> x2, other arithmetic: 1.73 us -> 3.02 us  [per_device(): prompt_parts.astype(jnp.bfloat16).reshape(devices, rows_here, 2 * HEAD_DIM)]
    pallas_call x1 -> x2, Pallas kernels: 42.5 us -> 43.4 us  [attend(): pl.pallas_call(functools.partial(attention_kernel, n_alias), out_shape=(j...]
  transfers between devices with their start and end apart: 1 -> 4, of which waited for: 1 -> 3; matrix products, arithmetic and copies ran while one was open for 1% -> 1% of each run, Pallas kernels for 0% -> 18%
where the time goes in v4:
time: 123 us; the launch traced here: 122 us
  Pallas kernels  43.4 us (35%)
  waiting for transfers between devices  38.2 us (31%)
  starting transfers between devices  30.4 us (25%)
  local copies, waits for them, and re-layouts  4.74 us (4%)
  other arithmetic  3.95 us (3%)
  between operations  1.4 us (1%)
    pallas_call x2, Pallas kernels, attend(): pl.pallas_call(functools.partial(attention_kernel, n_alias), out_shape=(j...  43.4 us
    all_to_all x2, waiting for transfers between devices, per_device(): lax.all_to_all(prompt_parts.astype(jnp.bfloat16).reshape(devices, rows_he...  26.2 us
    all_to_all x2, starting transfers between devices, per_device(): lax.all_to_all(outgoing, ('resp', 'head'), split_axis=0, concat_axis=0, t...  16 us
    all_to_all x2, starting transfers between devices, per_device(): lax.all_to_all(prompt_parts.astype(jnp.bfloat16).reshape(devices, rows_he...  14.4 us
    all_to_all x2, waiting for transfers between devices, per_device(): lax.all_to_all(outgoing, ('resp', 'head'), split_axis=0, concat_axis=0, t...  12 us
    reshape x2, other arithmetic, per_device(): prompt_parts.astype(jnp.bfloat16).reshape(devices, rows_here, 2 * HEAD_DIM)  3.02 us
  transfers between devices with their start and end apart: 4, of which 3 were waited for; matrix products, arithmetic and copies ran while one was open for 1% of the time, Pallas kernels for 18%

profile of v4, /device:TPU:1, one launch (start us, length us, event | category | flops | bytes accessed | tf_op | source)
XLA Modules:
  0.0 122.2 jit_solution(2372550127966474173)
XLA Ops:
  0.6 0.0 copy-start.3
  0.6 0.8 fusion.2
  1.4 0.9 broadcast_in_dim.17
  2.3 11.5 %all-to-all-start.1 = ((bf16[128,8,256]{2,1,0:T(8,128)(2,1)}), bf16[128,8,256]{2,1,0:T(8,128)(2,1)S(1)}, u32[]{:S(2)}, u32[]{:S(2)}) async-start(bf16[128,8,256]{2,1,0:T(8,128)(2,1)} %bitcast.15), calls=%async_computation.1 | async-start | bytes 1048576 | tf_op jit(solution)/shard_map/all_to_all | solution.py:163
  14.4 0.0 copy-done.3
  14.4 0.9 copy.25.keep_ref
  15.3 12.0 %all-to-all-done.1 = bf16[128,8,256]{2,1,0:T(8,128)(2,1)S(1)} async-done(((bf16[128,8,256]{2,1,0:T(8,128)(2,1)}), bf16[128,8,256]{2,1,0:T(8,128)(2,1)S(1)}, u32[]{:S(2)}, u32[]{:S(2)}) %all-to-all-start.1) | async-done | bytes 524320 | tf_op jit(solution)/shard_map/all_to_all | solution.py:163
  27.3 0.0 copy-start.1
  27.3 1.0 broadcast_in_dim.15
  28.3 4.5 %all-to-all-start = ((bf16[128,8,256]{2,1,0:T(8,128)(2,1)}), bf16[128,8,256]{2,1,0:T(8,128)(2,1)S(1)}, u32[]{:S(2)}, u32[]{:S(2)}) async-start(bf16[128,8,256]{2,1,0:T(8,128)(2,1)} %bitcast.7), calls=%async_computation | async-start | bytes 1048576 | tf_op jit(solution)/shard_map/all_to_all | solution.py:163
  32.8 0.0 copy-done.1
  32.8 21.7 %shard_map.127 = (bf16[512,1280]{1,0:T(8,128)(2,1)}, bf16[512,1280]{1,0:T(8,128)(2,1)}, bf16[512,256]{1,0:T(8,128)(2,1)}, bf16[512,256]{1,0:T(8,128)(2,1)}, f32[1024,256]{1,0:T(8,128)}) custom-call(s32[1]{0:T(128)S(6)} %copy.32.length_ref, bf16[512,1280]{1,0:T(8,128)(2,1)} %bitcast.54, bf16[512,1280]{1,0:T(8,128)(2,1)} %bitcast.56, ...), custom_call_target="tpu_custom_call" | custom-call | flops 6039797760 | bytes 3407872 | tf_op jit(solution)/shard_map/pallas_call | solution.py:91
  54.5 0.0 all-to-all-done
  54.5 0.0 copy-start.2
  54.5 0.8 copy-done.2
  55.3 21.7 %shard_map.128 = (bf16[512,1280]{1,0:T(8,128)(2,1)}, bf16[512,1280]{1,0:T(8,128)(2,1)}, bf16[512,256]{1,0:T(8,128)(2,1)}, bf16[512,256]{1,0:T(8,128)(2,1)}, f32[1024,256]{1,0:T(8,128)}) custom-call(s32[1]{0:T(128)S(6)} %copy.32.length_ref, bf16[512,1280]{1,0:T(8,128)(2,1)} %bitcast.55, ...), custom_call_target="tpu_custom_call", output_to_operand_aliasing={{0}: (8, {}), {1}: (9, {}), {2}: (10, {}), {3}: (11, {})} | custom-call | flops 6039797760 | bytes 3407872 | tf_op jit(solution)/shard_map/pallas_call | solution.py:91
  77.1 0.0 copy-start
  77.1 2.2 %convert_bitcast_fusion = bf16[128,8,256]{2,1,0:T(8,128)(2,1)} fusion(f32[1024,256]{1,0:T(8,128)} %get-tuple-element.25), kind=kLoop, calls=%fused_computation.2 | loop fusion | flops 262144 | bytes 1572864 | tf_op jit(solution)/shard_map/reshape | solution.py:169
  79.2 9.9 %all-to-all-start.3 = ((bf16[128,8,256]{2,1,0:T(8,128)(2,1)}), bf16[128,8,256]{2,1,0:T(8,128)(2,1)S(1)}, u32[]{:S(2)}, u32[]{:S(2)}) async-start(bf16[128,8,256]{2,1,0:T(8,128)(2,1)} %convert_bitcast_fusion), calls=%async_computation.3 | async-start | bytes 1048576 | tf_op jit(solution)/shard_map/all_to_all | solution.py:168
  89.1 0.0 copy-done
  89.2 0.8 convert_bitcast_fusion.1
  90.0 12.7 %all-to-all-done.3 = bf16[128,8,256]{2,1,0:T(8,128)(2,1)S(1)} async-done(((bf16[128,8,256]{2,1,0:T(8,128)(2,1)}), bf16[128,8,256]{2,1,0:T(8,128)(2,1)S(1)}, u32[]{:S(2)}, u32[]{:S(2)}) %all-to-all-start.3) | async-done | bytes 524320 | tf_op jit(solution)/shard_map/all_to_all | solution.py:168
  102.7 4.5 %all-to-all-start.2 = ((bf16[128,8,256]{2,1,0:T(8,128)(2,1)}), bf16[128,8,256]{2,1,0:T(8,128)(2,1)S(1)}, u32[]{:S(2)}, u32[]{:S(2)}) async-start(bf16[128,8,256]{2,1,0:T(8,128)(2,1)} %convert_bitcast_fusion.1), calls=%async_computation.2 | async-start | bytes 1048576 | tf_op jit(solution)/shard_map/all_to_all | solution.py:168
  107.2 0.1 convert_reduce_fusion
  107.3 13.6 %all-to-all-done.2 = bf16[128,8,256]{2,1,0:T(8,128)(2,1)S(1)} async-done(((bf16[128,8,256]{2,1,0:T(8,128)(2,1)}), bf16[128,8,256]{2,1,0:T(8,128)(2,1)S(1)}, u32[]{:S(2)}, u32[]{:S(2)}) %all-to-all-start.2) | async-done | bytes 524320 | tf_op jit(solution)/shard_map/all_to_all | solution.py:168
  120.8 0.1 convert_reduce_fusion.1
  121.0 0.6 copy.27
  121.6 0.6 copy.26
  (2 shorter events, 0.0 us)
Async XLA Ops:
  0.6 13.8 %copy-start.3 = (s32[1,512]{1,0:T(1,128)S(1)}, s32[1,512]{1,0:T(1,128)}, u32[]{:S(2)}) copy-start(s32[1,512]{1,0:T(1,128)} %param.14) | copy-start | bytes 6148
  2.3 25.0 %all-to-all-start.1 = ((bf16[128,8,256]{2,1,0:T(8,128)(2,1)}), bf16[128,8,256]{2,1,0:T(8,128)(2,1)S(1)}, u32[]{:S(2)}, u32[]{:S(2)}) async-start(bf16[128,8,256]{2,1,0:T(8,128)(2,1)} %bitcast.15), calls=%async_computation.1 | async-start | bytes 1048576 | tf_op jit(solution)/shard_map/all_to_all | solution.py:163
  27.3 5.5 %copy-start.1 = (bf16[128,8,256]{2,1,0:T(8,128)(2,1)}, bf16[128,8,256]{2,1,0:T(8,128)(2,1)S(1)}, u32[]{:S(2)}) copy-start(bf16[128,8,256]{2,1,0:T(8,128)(2,1)S(1)} %all-to-all-done.1) | copy-start | bytes 1572868
  28.3 26.2 %all-to-all-start = ((bf16[128,8,256]{2,1,0:T(8,128)(2,1)}), bf16[128,8,256]{2,1,0:T(8,128)(2,1)S(1)}, u32[]{:S(2)}, u32[]{:S(2)}) async-start(bf16[128,8,256]{2,1,0:T(8,128)(2,1)} %bitcast.7), calls=%async_computation | async-start | bytes 1048576 | tf_op jit(solution)/shard_map/all_to_all | solution.py:163
  54.5 0.8 copy-start.2
  77.1 12.1 %copy-start = (f32[1024,256]{1,0:T(8,128)S(1)}, f32[1024,256]{1,0:T(8,128)}, u32[]{:S(2)}) copy-start(f32[1024,256]{1,0:T(8,128)} %get-tuple-element.24) | copy-start | bytes 3145732
  79.2 23.4 %all-to-all-start.3 = ((bf16[128,8,256]{2,1,0:T(8,128)(2,1)}), bf16[128,8,256]{2,1,0:T(8,128)(2,1)S(1)}, u32[]{:S(2)}, u32[]{:S(2)}) async-start(bf16[128,8,256]{2,1,0:T(8,128)(2,1)} %convert_bitcast_fusion), calls=%async_computation.3 | async-start | bytes 1048576 | tf_op jit(solution)/shard_map/all_to_all | solution.py:168
  102.7 18.2 %all-to-all-start.2 = ((bf16[128,8,256]{2,1,0:T(8,128)(2,1)}), bf16[128,8,256]{2,1,0:T(8,128)(2,1)S(1)}, u32[]{:S(2)}, u32[]{:S(2)}) async-start(bf16[128,8,256]{2,1,0:T(8,128)(2,1)} %convert_bitcast_fusion.1), calls=%async_computation.2 | async-start | bytes 1048576 | tf_op jit(solution)/shard_map/all_to_all | solution.py:168

commit v5 on v3

--- a/solution.py
+++ b/solution.py
@@ -34,10 +34,11 @@
     allowed = (j <= t) & (j < length)
     so = jnp.where(allowed, so, -jnp.inf)
     top = jnp.maximum(sp.max(-1, keepdims=True), so.max(-1, keepdims=True))
-    total = jnp.exp(sp - top).sum(-1, keepdims=True) + jnp.exp(so - top).sum(-1, keepdims=True)
-    log_total = top + jnp.log(total)
-    pp = jnp.exp(sp - log_total)
-    po = jnp.exp(so - log_total)
+    ep = jnp.exp(sp - top)
+    eo = jnp.exp(so - top)
+    inverse = 1.0 / (ep.sum(-1, keepdims=True) + eo.sum(-1, keepdims=True))
+    pp = ep * inverse
+    po = eo * inverse
     wp = pp.astype(bf16)
     wo = po.astype(bf16)
     live = t < length
@@ -49,13 +50,13 @@
     delta = (do.astype(f32) * att.astype(f32)).sum(-1, keepdims=True)
     dpp = lax.dot_general(do, vp, NT, preferred_element_type=f32)
     dpo = lax.dot_general(do, vo, NT, preferred_element_type=f32)
-    dsp = (pp * (dpp - delta) * scale).astype(bf16)
-    dso = (po * (dpo - delta) * scale).astype(bf16)
+    dsp = (pp * (dpp - delta)).astype(bf16)
+    dso = (po * (dpo - delta)).astype(bf16)
     dq = jnp.dot(dsp, kp, preferred_element_type=f32) + jnp.dot(dso, ko, preferred_element_type=f32)
-    dq_ref[...] = dq.astype(bf16)
-    dkp = lax.dot_general(dsp, q, TN, preferred_element_type=f32)
+    dq_ref[...] = (dq * scale).astype(bf16)
+    dkp = lax.dot_general(dsp, q, TN, preferred_element_type=f32) * scale
     dvp = lax.dot_general(wp, do, TN, preferred_element_type=f32)
-    dko = lax.dot_general(dso, q, TN, preferred_element_type=f32)
+    dko = lax.dot_general(dso, q, TN, preferred_element_type=f32) * scale
     dvo = lax.dot_general(wo, do, TN, preferred_element_type=f32)
     width = HEAD_DIM
     kcol = pl.ds(pl.multiple_of(k * width, width), width)

time: 103 us -> 102 us (level)
  no operation moved by 1% of the time
where the time goes in v5:
time: 102 us
  Pallas kernels  42.1 us (41%)
  blocking collectives  23.2 us (23%)
  waiting for transfers between devices  17.6 us (17%)
  starting transfers between devices  11.5 us (11%)
  local copies, waits for them, and re-layouts  3.57 us (4%)
  other arithmetic  2.62 us (3%)
  between operations  1.31 us (1%)
    pallas_call x1, Pallas kernels, attend(): pl.pallas_call(attention_kernel, out_shape=(jax.ShapeDtypeStruct((steps,...  42.1 us
    all_to_all x1, blocking collectives, per_device(): lax.all_to_all(prompt_parts.astype(jnp.bfloat16).reshape(devices, rows_he...  23.2 us
    all_to_all x1, waiting for transfers between devices, per_device(): lax.all_to_all(outgoing, ('resp', 'head'), split_axis=0, concat_axis=0, t...  17.6 us
    all_to_all x1, starting transfers between devices, per_device(): lax.all_to_all(outgoing, ('resp', 'head'), split_axis=0, concat_axis=0, t...  11.5 us
  transfers between devices with their start and end apart: 1, of which 1 were waited for; matrix products, arithmetic and copies ran while one was open for 1% of the time, Pallas kernels for 0%

profile of v5, /device:TPU:1, one launch (start us, length us, event | category | flops | bytes accessed | tf_op | source)
XLA Modules:
  0.0 101.8 jit_solution(1120467094452972079)
XLA Ops:
  0.6 0.7 maximum_bitcast_fusion
  1.4 1.1 %broadcast_in_dim.2 = bf16[32,4,8,512]{3,2,1,0:T(8,128)(2,1)} broadcast(bf16[4,8,512]{2,1,0:T(8,128)(2,1)S(1)} %maximum_bitcast_fusion), dimensions={1,2,3} | broadcast | bytes 1081344 | tf_op jit(solution)/shard_map/broadcast_in_dim | solution.py:141
  2.5 0.0 copy-start.1
  2.5 11.5 %all-to-all-start = ((bf16[128,8,512]{2,1,0:T(8,128)(2,1)}), bf16[128,8,512]{2,1,0:T(8,128)(2,1)S(1)}, u32[]{:S(2)}, u32[]{:S(2)}) async-start(bf16[128,8,512]{2,1,0:T(8,128)(2,1)} %bitcast.5), calls=%async_computation | async-start | bytes 2097152 | tf_op jit(solution)/shard_map/all_to_all | solution.py:144
  14.6 0.0 copy-done.1
  14.6 0.8 copy.14.keep_ref
  15.5 17.6 %all-to-all-done = bf16[128,8,512]{2,1,0:T(8,128)(2,1)S(1)} async-done(((bf16[128,8,512]{2,1,0:T(8,128)(2,1)}), bf16[128,8,512]{2,1,0:T(8,128)(2,1)S(1)}, u32[]{:S(2)}, u32[]{:S(2)}) %all-to-all-start) | async-done | bytes 1048608 | tf_op jit(solution)/shard_map/all_to_all | solution.py:144
  33.0 0.0 copy-start
  33.0 1.0 copy-done
  34.0 42.1 %shard_map.127 = (bf16[512,1280]{1,0:T(8,128)(2,1)}, bf16[512,1280]{1,0:T(8,128)(2,1)}, bf16[512,256]{1,0:T(8,128)(2,1)}, bf16[512,256]{1,0:T(8,128)(2,1)}, f32[1024,512]{1,0:T(8,128)}) custom-call(s32[1]{0:T(128)S(6)} %copy.15.length_ref, bf16[512,1280]{1,0:T(8,128)(2,1)} %bitcast.25, bf16[512,1280]{1,0:T(8,128)(2,1)} %bitcast.26, ...), custom_call_target="tpu_custom_call" | custom-call | tf_op jit(solution)/shard_map/pallas_call | solution.py:92
  76.1 1.7 %convert_bitcast_fusion = bf16[128,8,512]{2,1,0:T(8,128)(2,1)S(1)} fusion(f32[1024,512]{1,0:T(8,128)} %get-tuple-element.15), kind=kLoop, calls=%fused_computation.1 | loop fusion | flops 524288 | bytes 3145728 | tf_op jit(solution)/shard_map/reshape | solution.py:159
  77.8 23.2 %all_to_all.10 = bf16[128,8,512]{2,1,0:T(8,128)(2,1)S(1)} all-to-all(bf16[128,8,512]{2,1,0:T(8,128)(2,1)S(1)} %convert_bitcast_fusion), channel_id=1, replica_groups=mesh['resp'=32,'head'=4] {'resp','head'}, dimensions={0} | all-to-all | bytes 2097152 | tf_op jit(solution)/shard_map/all_to_all | solution.py:158
  101.0 0.2 convert_reduce_fusion
  101.2 0.6 fusion
Async XLA Ops:
  2.5 12.2 %copy-start.1 = (s32[1,512]{1,0:T(1,128)S(1)}, s32[1,512]{1,0:T(1,128)}, u32[]{:S(2)}) copy-start(s32[1,512]{1,0:T(1,128)} %param.14) | copy-start | bytes 6148
  2.5 30.6 %all-to-all-start = ((bf16[128,8,512]{2,1,0:T(8,128)(2,1)}), bf16[128,8,512]{2,1,0:T(8,128)(2,1)S(1)}, u32[]{:S(2)}, u32[]{:S(2)}) async-start(bf16[128,8,512]{2,1,0:T(8,128)(2,1)} %bitcast.5), calls=%async_computation | async-start | bytes 2097152 | tf_op jit(solution)/shard_map/all_to_all | solution.py:144
  33.0 1.0 copy-start

commit v6 on v5

--- a/solution.py
+++ b/solution.py
@@ -13,7 +13,7 @@
 
 
 def attention_kernel(
-    length_ref, q_ref, do_ref, kp_ref, vp_ref, ko_ref, vo_ref, keep_ref,
+    length_ref, q_ref, do_ref, kp_ref, vp_ref, ko_ref, vo_ref, keep_col_ref,
     att_ref, dq_ref, dko_ref, dvo_ref, pg_ref, dko_acc, dvo_acc,
 ):
     f32, bf16 = jnp.float32, jnp.bfloat16
@@ -27,37 +27,42 @@
     ko = ko_ref[...]
     vp = vp_ref[...]
     vo = vo_ref[...]
-    sp = lax.dot_general(q, kp, NT, preferred_element_type=f32) * scale
-    so = lax.dot_general(q, ko, NT, preferred_element_type=f32) * scale
-    t = lax.broadcasted_iota(jnp.int32, (steps, 1), 0)
-    j = lax.broadcasted_iota(jnp.int32, (1, steps), 1)
+    sp = lax.dot_general(kp, q, NT, preferred_element_type=f32) * scale
+    so = lax.dot_general(ko, q, NT, preferred_element_type=f32) * scale
+    j = lax.broadcasted_iota(jnp.int32, (steps, 1), 0)
+    t = lax.broadcasted_iota(jnp.int32, (1, steps), 1)
     allowed = (j <= t) & (j < length)
     so = jnp.where(allowed, so, -jnp.inf)
-    top = jnp.maximum(sp.max(-1, keepdims=True), so.max(-1, keepdims=True))
+    top = jnp.maximum(sp.max(0, keepdims=True), so.max(0, keepdims=True))
     ep = jnp.exp(sp - top)
     eo = jnp.exp(so - top)
-    inverse = 1.0 / (ep.sum(-1, keepdims=True) + eo.sum(-1, keepdims=True))
+    inverse = 1.0 / (ep.sum(0, keepdims=True) + eo.sum(0, keepdims=True))
     pp = ep * inverse
     po = eo * inverse
     wp = pp.astype(bf16)
     wo = po.astype(bf16)
     live = t < length
-    out = jnp.dot(wp, vp, preferred_element_type=f32) + jnp.dot(wo, vo, preferred_element_type=f32)
-    att = jnp.where(live, out, 0.0).astype(bf16)
-    att_ref[...] = att
-    factor = (keep_ref[...] * live.astype(jnp.int32)).astype(bf16)
+    out = lax.dot_general(vp, wp, TN, preferred_element_type=f32) + lax.dot_general(
+        vo, wo, TN, preferred_element_type=f32
+    )
+    att = jnp.where(live, out, 0.0).astype(bf16).astype(f32)
+    att_ref[...] = att.T.astype(bf16)
+    live_col = lax.broadcasted_iota(jnp.int32, (steps, 1), 0) < length
+    factor = (keep_col_ref[...] * live_col.astype(jnp.int32)).astype(bf16)
     do = do_ref[...] * factor
-    delta = (do.astype(f32) * att.astype(f32)).sum(-1, keepdims=True)
-    dpp = lax.dot_general(do, vp, NT, preferred_element_type=f32)
-    dpo = lax.dot_general(do, vo, NT, preferred_element_type=f32)
+    delta = (do.astype(f32).T * att).sum(0, keepdims=True)
+    dpp = lax.dot_general(vp, do, NT, preferred_element_type=f32)
+    dpo = lax.dot_general(vo, do, NT, preferred_element_type=f32)
     dsp = (pp * (dpp - delta)).astype(bf16)
     dso = (po * (dpo - delta)).astype(bf16)
-    dq = jnp.dot(dsp, kp, preferred_element_type=f32) + jnp.dot(dso, ko, preferred_element_type=f32)
-    dq_ref[...] = (dq * scale).astype(bf16)
-    dkp = lax.dot_general(dsp, q, TN, preferred_element_type=f32) * scale
-    dvp = lax.dot_general(wp, do, TN, preferred_element_type=f32)
-    dko = lax.dot_general(dso, q, TN, preferred_element_type=f32) * scale
-    dvo = lax.dot_general(wo, do, TN, preferred_element_type=f32)
+    dq = lax.dot_general(kp, dsp, TN, preferred_element_type=f32) + lax.dot_general(
+        ko, dso, TN, preferred_element_type=f32
+    )
+    dq_ref[...] = (dq * scale).T.astype(bf16)
+    dkp = jnp.dot(dsp, q, preferred_element_type=f32) * scale
+    dvp = jnp.dot(wp, do, preferred_element_type=f32)
+    dko = jnp.dot(dso, q, preferred_element_type=f32) * scale
+    dvo = jnp.dot(wo, do, preferred_element_type=f32)
     width = HEAD_DIM
     kcol = pl.ds(pl.multiple_of(k * width, width), width)
     vcol = pl.ds(pl.multiple_of((k + pl.num_programs(0)) * width, width), width)

time: 102 us -> 99.2 us (0.973)
  Pallas kernels: 42.1 us -> 39.1 us
    pallas_call x1, Pallas kernels: 42.1 us -> 39.1 us  [attend(): pl.pallas_call(attention_kernel, out_shape=(jax.ShapeDtypeStruct((steps,...]
where the time goes in v6:
time: 99.2 us; the launch traced here: 98.8 us
  Pallas kernels  39.1 us (39%)
  blocking collectives  23.2 us (23%)
  waiting for transfers between devices  17.6 us (18%)
  starting transfers between devices  11.5 us (12%)
  local copies, waits for them, and re-layouts  3.57 us (4%)
  other arithmetic  2.62 us (3%)
  between operations  1.31 us (1%)
    pallas_call x1, Pallas kernels, attend(): pl.pallas_call(attention_kernel, out_shape=(jax.ShapeDtypeStruct((steps,...  39.1 us
    all_to_all x1, blocking collectives, per_device(): lax.all_to_all(prompt_parts.astype(jnp.bfloat16).reshape(devices, rows_he...  23.2 us
    all_to_all x1, waiting for transfers between devices, per_device(): lax.all_to_all(outgoing, ('resp', 'head'), split_axis=0, concat_axis=0, t...  17.6 us
    all_to_all x1, starting transfers between devices, per_device(): lax.all_to_all(outgoing, ('resp', 'head'), split_axis=0, concat_axis=0, t...  11.5 us
  transfers between devices with their start and end apart: 1, of which 1 were waited for; matrix products, arithmetic and copies ran while one was open for 1% of the time, Pallas kernels for 0%

profile of v6, /device:TPU:1, one launch (start us, length us, event | category | flops | bytes accessed | tf_op | source)
XLA Modules:
  0.0 98.8 jit_solution(16550593770027127824)
XLA Ops:
  0.6 0.7 maximum_bitcast_fusion
  1.4 1.1 %broadcast_in_dim.2 = bf16[32,4,8,512]{3,2,1,0:T(8,128)(2,1)} broadcast(bf16[4,8,512]{2,1,0:T(8,128)(2,1)S(1)} %maximum_bitcast_fusion), dimensions={1,2,3} | broadcast | bytes 1081344 | tf_op jit(solution)/shard_map/broadcast_in_dim | solution.py:146
  2.5 0.0 copy-start.1
  2.5 11.5 %all-to-all-start = ((bf16[128,8,512]{2,1,0:T(8,128)(2,1)}), bf16[128,8,512]{2,1,0:T(8,128)(2,1)S(1)}, u32[]{:S(2)}, u32[]{:S(2)}) async-start(bf16[128,8,512]{2,1,0:T(8,128)(2,1)} %bitcast.5), calls=%async_computation | async-start | bytes 2097152 | tf_op jit(solution)/shard_map/all_to_all | solution.py:149
  14.6 0.0 copy-done.1
  14.6 0.8 copy.14.keep_col_ref
  15.5 17.6 %all-to-all-done = bf16[128,8,512]{2,1,0:T(8,128)(2,1)S(1)} async-done(((bf16[128,8,512]{2,1,0:T(8,128)(2,1)}), bf16[128,8,512]{2,1,0:T(8,128)(2,1)S(1)}, u32[]{:S(2)}, u32[]{:S(2)}) %all-to-all-start) | async-done | bytes 1048608 | tf_op jit(solution)/shard_map/all_to_all | solution.py:149
  33.0 0.0 copy-start
  33.0 1.0 %copy-done = bf16[128,8,512]{2,1,0:T(8,128)(2,1)} copy-done((bf16[128,8,512]{2,1,0:T(8,128)(2,1)}, bf16[128,8,512]{2,1,0:T(8,128)(2,1)S(1)}, u32[]{:S(2)}) %copy-start) | copy-done | bytes 1048600
  34.0 39.1 %shard_map.127 = (bf16[512,1280]{1,0:T(8,128)(2,1)}, bf16[512,1280]{1,0:T(8,128)(2,1)}, bf16[512,256]{1,0:T(8,128)(2,1)}, bf16[512,256]{1,0:T(8,128)(2,1)}, f32[1024,512]{1,0:T(8,128)}) custom-call(s32[1]{0:T(128)S(6)} %copy.15.length_ref, bf16[512,1280]{1,0:T(8,128)(2,1)} %bitcast.25, bf16[512,1280]{1,0:T(8,128)(2,1)} %bitcast.26, ...), custom_call_target="tpu_custom_call" | custom-call | tf_op jit(solution)/shard_map/pallas_call | solution.py:97
  73.1 1.7 %convert_bitcast_fusion = bf16[128,8,512]{2,1,0:T(8,128)(2,1)S(1)} fusion(f32[1024,512]{1,0:T(8,128)} %get-tuple-element.15), kind=kLoop, calls=%fused_computation.1 | loop fusion | flops 524288 | bytes 3145728 | tf_op jit(solution)/shard_map/reshape | solution.py:164
  74.9 23.2 %all_to_all.10 = bf16[128,8,512]{2,1,0:T(8,128)(2,1)S(1)} all-to-all(bf16[128,8,512]{2,1,0:T(8,128)(2,1)S(1)} %convert_bitcast_fusion), channel_id=1, replica_groups=mesh['resp'=32,'head'=4] {'resp','head'}, dimensions={0} | all-to-all | bytes 2097152 | tf_op jit(solution)/shard_map/all_to_all | solution.py:163
  98.0 0.2 convert_reduce_fusion
  98.2 0.6 fusion
Async XLA Ops:
  2.5 12.2 %copy-start.1 = (s32[1,512]{1,0:T(1,128)S(1)}, s32[1,512]{1,0:T(1,128)}, u32[]{:S(2)}) copy-start(s32[1,512]{1,0:T(1,128)} %param.14) | copy-start | bytes 6148
  2.5 30.6 %all-to-all-start = ((bf16[128,8,512]{2,1,0:T(8,128)(2,1)}), bf16[128,8,512]{2,1,0:T(8,128)(2,1)S(1)}, u32[]{:S(2)}, u32[]{:S(2)}) async-start(bf16[128,8,512]{2,1,0:T(8,128)(2,1)} %bitcast.5), calls=%async_computation | async-start | bytes 2097152 | tf_op jit(solution)/shard_map/all_to_all | solution.py:149
  33.0 1.0 %copy-start = (bf16[128,8,512]{2,1,0:T(8,128)(2,1)}, bf16[128,8,512]{2,1,0:T(8,128)(2,1)S(1)}, u32[]{:S(2)}) copy-start(bf16[128,8,512]{2,1,0:T(8,128)(2,1)S(1)} %all-to-all-done) | copy-start | bytes 3145732

commit v7 on v6

--- a/solution.py
+++ b/solution.py
@@ -131,6 +131,74 @@
     )(length, queries, out_grad, prompt_kv, prompt_kv, keys, values, keep)
 
 
+def exchange_kernel(n_head, x_ref, o_ref, send_sem, recv_sem):
+    count = x_ref.shape[0]
+    me = lax.axis_index("resp") * n_head + lax.axis_index("head")
+    barrier = pltpu.get_barrier_semaphore()
+
+    def where(d):
+        return (d // n_head, d % n_head)
+
+    def greet(d, carry):
+        @pl.when(d != me)
+        def _():
+            pl.semaphore_signal(barrier, 1, device_id=where(d), device_id_type=pl.DeviceIdType.MESH)
+
+        return carry
+
+    lax.fori_loop(0, count, greet, 0)
+    pl.semaphore_wait(barrier, count - 1)
+
+    def send(d):
+        return pltpu.make_async_remote_copy(
+            src_ref=x_ref.at[d],
+            dst_ref=o_ref.at[me],
+            send_sem=send_sem.at[d],
+            recv_sem=recv_sem.at[me],
+            device_id=where(d),
+            device_id_type=pl.DeviceIdType.MESH,
+        )
+
+    def start(d, carry):
+        @pl.when(d != me)
+        def _():
+            send(d).start()
+
+        return carry
+
+    lax.fori_loop(0, count, start, 0)
+    o_ref[me] = x_ref[me]
+
+    def finish(d, carry):
+        @pl.when(d != me)
+        def _():
+            send(d).wait_send()
+            pltpu.make_async_remote_copy(
+                src_ref=x_ref.at[d],
+                dst_ref=o_ref.at[d],
+                send_sem=send_sem.at[d],
+                recv_sem=recv_sem.at[d],
+                device_id=where(d),
+                device_id_type=pl.DeviceIdType.MESH,
+            ).wait_recv()
+
+        return carry
+
+    lax.fori_loop(0, count, finish, 0)
+
+
+def exchange(x, n_head, collective_id):
+    count = x.shape[0]
+    return pl.pallas_call(
+        functools.partial(exchange_kernel, n_head),
+        out_shape=jax.ShapeDtypeStruct(x.shape, x.dtype),
+        in_specs=[pl.BlockSpec(memory_space=pltpu.VMEM)],
+        out_specs=pl.BlockSpec(memory_space=pltpu.VMEM),
+        scratch_shapes=[pltpu.SemaphoreType.DMA((count,)), pltpu.SemaphoreType.DMA((count,))],
+        compiler_params=pltpu.CompilerParams(collective_id=collective_id, has_side_effects=True),
+    )(x)
+
+
 def per_device(
     queries, resp_keys, resp_values, prompt_keys, prompt_values, lengths, loss_mask, out_grad
 ):
@@ -146,7 +214,7 @@
     outgoing = jnp.broadcast_to(both[None], (devices // groups,) + both.shape).reshape(
         devices, rows_here, 2 * kv_width
     )
-    gathered = lax.all_to_all(outgoing, ("resp", "head"), split_axis=0, concat_axis=0, tiled=True)
+    gathered = exchange(outgoing, groups, 0)
     prompt_kv = gathered.reshape(devices * rows_here, 2 * kv_width)
 
     steps = queries.shape[1]
@@ -160,12 +228,8 @@
         loss_mask.reshape(steps, 1),
         kv_count,
     )
-    arrived = lax.all_to_all(
-        prompt_parts.astype(jnp.bfloat16).reshape(devices, rows_here, 2 * kv_width),
-        ("resp", "head"),
-        split_axis=0,
-        concat_axis=0,
-        tiled=True,
+    arrived = exchange(
+        prompt_parts.astype(jnp.bfloat16).reshape(devices, rows_here, 2 * kv_width), groups, 1
     )
     summed = arrived.astype(jnp.float32).reshape(devices // groups, groups, rows_here, 2 * kv_width).sum(0)
     summed = summed.transpose(1, 0, 2)

time: 99.2 us -> 113 us (1.14)
  Pallas kernels: 39.1 us -> 103 us
  blocking collectives: 23.2 us -> 0 us
  waiting for transfers between devices: 17.6 us -> 0 us
  starting transfers between devices: 11.5 us -> 0 us
  other arithmetic: 2.62 us -> 4.83 us
    pallas_call x0 -> x2, Pallas kernels: none -> 64 us  [exchange(): pl.pallas_call(functools.partial(exchange_kernel, n_head), out_shape=jax....]
    all_to_all x1 -> x0, blocking collectives: 23.2 us -> none  [per_device(): lax.all_to_all(prompt_parts.astype(jnp.bfloat16).reshape(devices, rows_he...]
    all_to_all x1 -> x0, waiting for transfers between devices: 17.6 us -> none  [per_device(): lax.all_to_all(outgoing, ('resp', 'head'), split_axis=0, concat_axis=0, t...]
    all_to_all x1 -> x0, starting transfers between devices: 11.5 us -> none  [per_device(): lax.all_to_all(outgoing, ('resp', 'head'), split_axis=0, concat_axis=0, t...]
    reduce_sum x1, other arithmetic: 0.16 us -> 1.39 us  [per_device(): arrived.astype(jnp.float32)]
  transfers between devices with their start and end apart: 1 -> 0, of which waited for: 1 -> 0; matrix products, arithmetic and copies ran while one was open for 1% -> 0% of each run, Pallas kernels for 0% -> 0%
where the time goes in v7:
time: 113 us
  Pallas kernels  103 us (91%)
  other arithmetic  4.83 us (4%)
  local copies, waits for them, and re-layouts  3.27 us (3%)
  between operations  1.3 us (1%)
    pallas_call x2, Pallas kernels, exchange(): pl.pallas_call(functools.partial(exchange_kernel, n_head), out_shape=jax....  64 us
    pallas_call x1, Pallas kernels, attend(): pl.pallas_call(attention_kernel, out_shape=(jax.ShapeDtypeStruct((steps,...  39.1 us
    reshape x1, other arithmetic, per_device(): prompt_parts.astype(jnp.bfloat16).reshape(devices, rows_here, 2 * kv_width)  2.71 us

profile of v7, /device:TPU:1, one launch (start us, length us, event | category | flops | bytes accessed | tf_op | source)
XLA Modules:
  0.0 112.5 jit_solution(6656236686344566472)
XLA Ops:
  1.3 0.7 maximum_bitcast_fusion
  2.0 1.6 %copy.14.keep_col_ref = s32[512,1]{1,0:T(8,128)} copy(s32[512,1]{0,1:T(1,128)} %bitcast.35) | data formatting | bytes 4096 | tf_op jit(solution)/shard_map/reshape | solution.py:228
  3.6 1.1 broadcast_in_dim.2
  4.7 32.3 %shard_map.127 = bf16[128,8,512]{2,1,0:T(8,128)(2,1)} custom-call(bf16[128,8,512]{2,1,0:T(8,128)(2,1)} %bitcast.24), custom_call_target="tpu_custom_call" | custom-call | tf_op jit(solution)/shard_map/pallas_call | solution.py:192
  37.0 39.1 %shard_map.128 = (bf16[512,1280]{1,0:T(8,128)(2,1)}, bf16[512,1280]{1,0:T(8,128)(2,1)}, bf16[512,256]{1,0:T(8,128)(2,1)}, bf16[512,256]{1,0:T(8,128)(2,1)}, f32[1024,512]{1,0:T(8,128)}) custom-call(s32[1]{0:T(128)S(6)} %copy.15.length_ref, bf16[512,1280]{1,0:T(8,128)(2,1)} %bitcast.26, bf16[512,1280]{1,0:T(8,128)(2,1)} %bitcast.27, ...), custom_call_target="tpu_custom_call" | custom-call | tf_op jit(solution)/shard_map/pallas_call | solution.py:97
  76.1 2.7 %convert_bitcast_fusion.x_ref = bf16[128,8,512]{2,1,0:T(8,128)(2,1)} fusion(f32[1024,512]{1,0:T(8,128)} %get-tuple-element.15), kind=kLoop, calls=%fused_computation.1 | loop fusion | flops 524288 | bytes 3145728 | tf_op jit(solution)/shard_map/reshape | solution.py:232
  78.9 31.6 %shard_map.129 = bf16[128,8,512]{2,1,0:T(8,128)(2,1)} custom-call(bf16[128,8,512]{2,1,0:T(8,128)(2,1)} %convert_bitcast_fusion.x_ref), custom_call_target="tpu_custom_call" | custom-call | tf_op jit(solution)/shard_map/pallas_call | solution.py:192
  110.5 1.4 %convert_reduce_fusion = f32[4,8,512]{2,1,0:T(8,128)S(1)} fusion(bf16[32,4,8,512]{3,2,1,0:T(8,128)(2,1)} %bitcast.25), kind=kLoop, calls=%fused_computation | loop fusion | flops 1032192 | bytes 1114112 | tf_op jit(solution)/shard_map/reduce_sum | solution.py:234
  111.9 0.6 fusion

commit v8 on v7

--- a/solution.py
+++ b/solution.py
@@ -131,13 +131,18 @@
     )(length, queries, out_grad, prompt_kv, prompt_kv, keys, values, keep)
 
 
-def exchange_kernel(n_head, x_ref, o_ref, send_sem, recv_sem):
-    count = x_ref.shape[0]
-    me = lax.axis_index("resp") * n_head + lax.axis_index("head")
+def exchange_kernel(axis, same, x_ref, o_ref, send_sem, recv_sem):
+    count = o_ref.shape[0]
+    axes = ("resp", "head")
+    me = lax.axis_index(axes[axis])
+    here = tuple(lax.axis_index(a) for a in axes)
     barrier = pltpu.get_barrier_semaphore()
 
     def where(d):
-        return (d // n_head, d % n_head)
+        return here[:axis] + (d,) + here[axis + 1 :]
+
+    def block(d):
+        return x_ref if same else x_ref.at[d]
 
     def greet(d, carry):
         @pl.when(d != me)
@@ -151,7 +156,7 @@
 
     def send(d):
         return pltpu.make_async_remote_copy(
-            src_ref=x_ref.at[d],
+            src_ref=block(d),
             dst_ref=o_ref.at[me],
             send_sem=send_sem.at[d],
             recv_sem=recv_sem.at[me],
@@ -167,14 +172,14 @@
         return carry
 
     lax.fori_loop(0, count, start, 0)
-    o_ref[me] = x_ref[me]
+    o_ref[me] = block(me)[...]
 
     def finish(d, carry):
         @pl.when(d != me)
         def _():
             send(d).wait_send()
             pltpu.make_async_remote_copy(
-                src_ref=x_ref.at[d],
+                src_ref=block(d),
                 dst_ref=o_ref.at[d],
                 send_sem=send_sem.at[d],
                 recv_sem=recv_sem.at[d],
@@ -187,11 +192,11 @@
     lax.fori_loop(0, count, finish, 0)
 
 
-def exchange(x, n_head, collective_id):
-    count = x.shape[0]
+def exchange(x, axis, count, collective_id, same=False):
+    shape = ((count,) + x.shape) if same else x.shape
     return pl.pallas_call(
-        functools.partial(exchange_kernel, n_head),
-        out_shape=jax.ShapeDtypeStruct(x.shape, x.dtype),
+        functools.partial(exchange_kernel, axis, same),
+        out_shape=jax.ShapeDtypeStruct(shape, x.dtype),
         in_specs=[pl.BlockSpec(memory_space=pltpu.VMEM)],
         out_specs=pl.BlockSpec(memory_space=pltpu.VMEM),
         scratch_shapes=[pltpu.SemaphoreType.DMA((count,)), pltpu.SemaphoreType.DMA((count,))],
@@ -211,10 +216,9 @@
         [prompt_keys.reshape(rows_here, groups, kv_width), prompt_values.reshape(rows_here, groups, kv_width)],
         2,
     ).transpose(1, 0, 2)
-    outgoing = jnp.broadcast_to(both[None], (devices // groups,) + both.shape).reshape(
-        devices, rows_here, 2 * kv_width
-    )
-    gathered = exchange(outgoing, groups, 0)
+    responses = devices // groups
+    mine = exchange(both, 1, groups, 0)
+    gathered = exchange(mine, 0, responses, 1, same=True)
     prompt_kv = gathered.reshape(devices * rows_here, 2 * kv_width)
 
     steps = queries.shape[1]
@@ -229,9 +233,10 @@
         kv_count,
     )
     arrived = exchange(
-        prompt_parts.astype(jnp.bfloat16).reshape(devices, rows_here, 2 * kv_width), groups, 1
-    )
-    summed = arrived.astype(jnp.float32).reshape(devices // groups, groups, rows_here, 2 * kv_width).sum(0)
+        prompt_parts.astype(jnp.bfloat16).reshape(responses, groups * rows_here, 2 * kv_width), 0, responses, 2
+    )
+    partial = arrived.astype(jnp.float32).sum(0).astype(jnp.bfloat16)
+    summed = exchange(partial.reshape(groups, rows_here, 2 * kv_width), 1, groups, 3).astype(jnp.float32)
     summed = summed.transpose(1, 0, 2)
     prompt_key_grad = summed[:, :, :kv_width].reshape(rows_here, groups * kv_width)
     prompt_value_grad = summed[:, :, kv_width:].reshape(rows_here, groups * kv_width)

time: 113 us -> 111 us (0.982)
  Pallas kernels: 103 us -> 100 us
  other arithmetic: 4.83 us -> 6.83 us
    pallas_call x2 -> x4, Pallas kernels: 64 us -> 61 us  [exchange(): pl.pallas_call(functools.partial(exchange_kernel, axis, same), out_shape=...]
    convert_element_type x0 -> x1, other arithmetic: none -> 2.71 us  [per_device(): prompt_parts.astype(jnp.bfloat16)]
    reshape x1 -> x0, other arithmetic: 2.71 us -> none  [per_device(): prompt_parts.astype(jnp.bfloat16).reshape(devices, rows_here, 2 * kv_width)]
where the time goes in v8:
time: 111 us
  Pallas kernels  100 us (90%)
  other arithmetic  6.83 us (6%)
  local copies, waits for them, and re-layouts  2.18 us (2%)
  between operations  1.32 us (1%)
    pallas_call x4, Pallas kernels, exchange(): pl.pallas_call(functools.partial(exchange_kernel, axis, same), out_shape=...  61 us
    pallas_call x1, Pallas kernels, attend(): pl.pallas_call(attention_kernel, out_shape=(jax.ShapeDtypeStruct((steps,...  39.1 us
    convert_element_type x1, other arithmetic, per_device(): prompt_parts.astype(jnp.bfloat16)  2.71 us

profile of v8, /device:TPU:1, one launch (start us, length us, event | category | flops | bytes accessed | tf_op | source)
XLA Modules:
  0.0 110.5 jit_solution(18154835424880381833)
XLA Ops:
  1.3 1.4 %maximum_bitcast_fusion.x_ref = bf16[4,8,512]{2,1,0:T(8,128)(2,1)} fusion(bf16[8,4,256]{2,0,1:T(8,128)(2,1)} %bitcast.30, bf16[8,4,256]{2,0,1:T(8,128)(2,1)} %bitcast.31), kind=kLoop, calls=%fused_computation.1 | loop fusion | flops 65536 | bytes 65536 | tf_op jit(solution)/shard_map/transpose | solution.py:218
  2.6 7.6 %shard_map.127.x_ref = bf16[4,8,512]{2,1,0:T(8,128)(2,1)} custom-call(bf16[4,8,512]{2,1,0:T(8,128)(2,1)} %maximum_bitcast_fusion.x_ref), custom_call_target="tpu_custom_call" | custom-call | tf_op jit(solution)/shard_map/pallas_call | solution.py:197
  10.3 1.6 %copy.14.keep_col_ref = s32[512,1]{1,0:T(8,128)} copy(s32[512,1]{0,1:T(1,128)} %bitcast.32) | data formatting | bytes 4096 | tf_op jit(solution)/shard_map/reshape | solution.py:232
  11.8 24.1 %shard_map.128 = bf16[32,4,8,512]{3,2,1,0:T(8,128)(2,1)} custom-call(bf16[4,8,512]{2,1,0:T(8,128)(2,1)} %shard_map.127.x_ref), custom_call_target="tpu_custom_call" | custom-call | tf_op jit(solution)/shard_map/pallas_call | solution.py:197
  35.9 39.1 %shard_map.129 = (bf16[512,1280]{1,0:T(8,128)(2,1)}, bf16[512,1280]{1,0:T(8,128)(2,1)}, bf16[512,256]{1,0:T(8,128)(2,1)}, bf16[512,256]{1,0:T(8,128)(2,1)}, f32[1024,512]{1,0:T(8,128)}) custom-call(s32[1]{0:T(128)S(6)} %copy.15.length_ref, bf16[512,1280]{1,0:T(8,128)(2,1)} %bitcast.23, bf16[512,1280]{1,0:T(8,128)(2,1)} %bitcast.24, ...), custom_call_target="tpu_custom_call" | custom-call | tf_op jit(solution)/shard_map/pallas_call | solution.py:97
  75.1 2.7 %convert_element_type.2 = bf16[1024,512]{1,0:T(8,128)(2,1)} convert(f32[1024,512]{1,0:T(8,128)} %get-tuple-element.15) | non-fusion elementwise | flops 524288 | bytes 3145728 | tf_op jit(solution)/shard_map/convert_element_type | solution.py:236
  77.8 20.9 %shard_map.130 = bf16[32,32,512]{2,1,0:T(8,128)(2,1)} custom-call(bf16[32,32,512]{2,1,0:T(8,128)(2,1)} %bitcast.22), custom_call_target="tpu_custom_call" | custom-call | tf_op jit(solution)/shard_map/pallas_call | solution.py:197
  98.7 2.0 %reduce_sum.12 = bf16[32,512]{1,0:T(8,128)(2,1)} reduce(bf16[32,32,512]{2,1,0:T(8,128)(2,1)} %shard_map.130, bf16[]{:T(256)} %constant.2.clone.1), dimensions={0}, to_apply=%region_0.0 | reduce | flops 507904 | bytes 1081346 | tf_op jit(solution)/shard_map/reduce_sum | solution.py:238
  100.7 8.5 %shard_map.131 = bf16[4,8,512]{2,1,0:T(8,128)(2,1)} custom-call(bf16[4,8,512]{2,1,0:T(8,128)(2,1)} %bitcast.27), custom_call_target="tpu_custom_call" | custom-call | tf_op jit(solution)/shard_map/pallas_call | solution.py:197
  109.1 0.8 convert_bitcast_fusion
  109.9 0.6 fusion

commit v9 on v6

--- a/solution.py
+++ b/solution.py
@@ -13,8 +13,8 @@
 
 
 def attention_kernel(
-    length_ref, q_ref, do_ref, kp_ref, vp_ref, ko_ref, vo_ref, keep_col_ref,
-    att_ref, dq_ref, dko_ref, dvo_ref, pg_ref, dko_acc, dvo_acc,
+    n_head, length_ref, q_ref, do_ref, kp_ref, vp_ref, ko_ref, vo_ref, keep_col_ref,
+    att_ref, dq_ref, dko_ref, dvo_ref, recv_ref, dko_acc, dvo_acc, pg_ref, sbuf, rbuf, ssem, rsem,
 ):
     f32, bf16 = jnp.float32, jnp.bfloat16
     k = pl.program_id(0)
@@ -64,30 +64,97 @@
     dko = jnp.dot(dso, q, preferred_element_type=f32) * scale
     dvo = jnp.dot(wo, do, preferred_element_type=f32)
     width = HEAD_DIM
-    kcol = pl.ds(pl.multiple_of(k * width, width), width)
-    vcol = pl.ds(pl.multiple_of((k + pl.num_programs(0)) * width, width), width)
+    last_g = g == pl.num_programs(1) - 1
+    count = sbuf.shape[1]
+    me = lax.axis_index("resp") * n_head + lax.axis_index("head")
+
+    def where(d):
+        return (d // n_head, d % n_head)
+
+    @pl.when((k == 0) & (g == 0))
+    def _():
+        barrier = pltpu.get_barrier_semaphore()
+
+        def greet(d, carry):
+            @pl.when(d != me)
+            def _():
+                pl.semaphore_signal(barrier, 1, device_id=where(d), device_id_type=pl.DeviceIdType.MESH)
+
+            return carry
+
+        lax.fori_loop(0, count, greet, 0)
+        pl.semaphore_wait(barrier, count - 1)
 
     @pl.when(g == 0)
     def _():
         dko_acc[...] = dko
         dvo_acc[...] = dvo
-        pg_ref[:, kcol] = dkp
-        pg_ref[:, vcol] = dvp
+        pg_ref[:, :width] = dkp
+        pg_ref[:, width:] = dvp
 
     @pl.when(g > 0)
     def _():
         dko_acc[...] += dko
         dvo_acc[...] += dvo
-        pg_ref[:, kcol] += dkp
-        pg_ref[:, vcol] += dvp
-
-    @pl.when(g == pl.num_programs(1) - 1)
+        pg_ref[:, :width] += dkp
+        pg_ref[:, width:] += dvp
+
+    def send(kk, d):
+        return pltpu.make_async_remote_copy(
+            src_ref=sbuf.at[kk, d],
+            dst_ref=rbuf.at[kk, me],
+            send_sem=ssem.at[kk, d],
+            recv_sem=rsem.at[kk, me],
+            device_id=where(d),
+            device_id_type=pl.DeviceIdType.MESH,
+        )
+
+    @pl.when(last_g)
     def _():
         dko_ref[...] = dko_acc[...].astype(bf16)
         dvo_ref[...] = dvo_acc[...].astype(bf16)
-
-
-def attend(length, queries, out_grad, prompt_kv, keys, values, keep, kv_count):
+        rows = sbuf.shape[2]
+
+        def stage(d, carry):
+            sbuf[k, d] = pg_ref[pl.ds(pl.multiple_of(d * rows, rows), rows), :].astype(bf16)
+            return carry
+
+        lax.fori_loop(0, count, stage, 0)
+
+        def start(d, carry):
+            @pl.when(d != me)
+            def _():
+                send(k, d).start()
+
+            return carry
+
+        lax.fori_loop(0, count, start, 0)
+        rbuf[k, me] = sbuf[k, me]
+
+    @pl.when(last_g & (k == pl.num_programs(0) - 1))
+    def _():
+        for kk in range(sbuf.shape[0]):
+
+            def finish(d, carry):
+                @pl.when(d != me)
+                def _():
+                    send(kk, d).wait_send()
+                    pltpu.make_async_remote_copy(
+                        src_ref=sbuf.at[kk, d],
+                        dst_ref=rbuf.at[kk, d],
+                        send_sem=ssem.at[kk, d],
+                        recv_sem=rsem.at[kk, d],
+                        device_id=where(d),
+                        device_id_type=pl.DeviceIdType.MESH,
+                    ).wait_recv()
+
+                return carry
+
+            lax.fori_loop(0, count, finish, 0)
+        recv_ref[...] = rbuf[...]
+
+
+def attend(length, queries, out_grad, prompt_kv, keys, values, keep, kv_count, n_head, devices):
     steps, width = queries.shape
     group_size = width // (kv_count * HEAD_DIM)
     prompt_rows = prompt_kv.shape[0]
@@ -95,13 +162,13 @@
     kv_block = lambda k, g, n: (0, k)
     bf16, f32 = jnp.bfloat16, jnp.float32
     return pl.pallas_call(
-        attention_kernel,
+        functools.partial(attention_kernel, n_head),
         out_shape=(
             jax.ShapeDtypeStruct((steps, width), bf16),
             jax.ShapeDtypeStruct((steps, width), bf16),
             jax.ShapeDtypeStruct(keys.shape, bf16),
             jax.ShapeDtypeStruct(keys.shape, bf16),
-            jax.ShapeDtypeStruct((prompt_rows, 2 * kv_count * HEAD_DIM), f32),
+            jax.ShapeDtypeStruct((kv_count, devices, prompt_rows // devices, 2 * HEAD_DIM), bf16),
         ),
         grid_spec=pltpu.PrefetchScalarGridSpec(
             num_scalar_prefetch=1,
@@ -120,13 +187,20 @@
                 pl.BlockSpec((steps, HEAD_DIM), head_block),
                 pl.BlockSpec((steps, HEAD_DIM), kv_block),
                 pl.BlockSpec((steps, HEAD_DIM), kv_block),
-                pl.BlockSpec((prompt_rows, 2 * kv_count * HEAD_DIM), lambda k, g, n: (0, 0)),
+                pl.BlockSpec(
+                    (kv_count, devices, prompt_rows // devices, 2 * HEAD_DIM), lambda k, g, n: (0, 0, 0, 0)
+                ),
             ],
-            scratch_shapes=[pltpu.VMEM((steps, HEAD_DIM), f32)] * 2,
+            scratch_shapes=[pltpu.VMEM((steps, HEAD_DIM), f32)] * 2
+            + [pltpu.VMEM((prompt_rows, 2 * HEAD_DIM), f32)]
+            + [pltpu.VMEM((kv_count, devices, prompt_rows // devices, 2 * HEAD_DIM), bf16)] * 2
+            + [pltpu.SemaphoreType.DMA((kv_count, devices))] * 2,
         ),
         compiler_params=pltpu.CompilerParams(
             dimension_semantics=("arbitrary", "arbitrary"),
             vmem_limit_bytes=60 * 1024 * 1024,
+            collective_id=0,
+            has_side_effects=True,
         ),
     )(length, queries, out_grad, prompt_kv, prompt_kv, keys, values, keep)
 
@@ -150,7 +224,7 @@
     prompt_kv = gathered.reshape(devices * rows_here, 2 * kv_width)
 
     steps = queries.shape[1]
-    att, dq, dk, dv, prompt_parts = attend(
+    att, dq, dk, dv, arrived = attend(
         lengths,
         queries.reshape(steps, -1),
         out_grad.reshape(steps, -1),
@@ -159,18 +233,13 @@
         resp_values.reshape(steps, kv_width),
         loss_mask.reshape(steps, 1),
         kv_count,
-    )
-    arrived = lax.all_to_all(
-        prompt_parts.astype(jnp.bfloat16).reshape(devices, rows_here, 2 * kv_width),
-        ("resp", "head"),
-        split_axis=0,
-        concat_axis=0,
-        tiled=True,
-    )
-    summed = arrived.astype(jnp.float32).reshape(devices // groups, groups, rows_here, 2 * kv_width).sum(0)
-    summed = summed.transpose(1, 0, 2)
-    prompt_key_grad = summed[:, :, :kv_width].reshape(rows_here, groups * kv_width)
-    prompt_value_grad = summed[:, :, kv_width:].reshape(rows_here, groups * kv_width)
+        groups,
+        devices,
+    )
+    summed = arrived.astype(jnp.float32).reshape(kv_count, devices // groups, groups, rows_here, 2, HEAD_DIM)
+    summed = summed.sum(1).transpose(3, 2, 1, 0, 4)
+    prompt_key_grad = summed[0].reshape(rows_here, groups * kv_width)
+    prompt_value_grad = summed[1].reshape(rows_here, groups * kv_width)
     return (
         att.reshape(queries.shape),
         dq.reshape(queries.shape),

time: 99.2 us -> 103 us (1.038)
  blocking collectives: 23.2 us -> 0 us
  Pallas kernels: 39.1 us -> 61.5 us
  local copies, waits for them, and re-layouts: 3.57 us -> 8.45 us
    all_to_all x1 -> x0, blocking collectives: 23.2 us -> none  [per_device(): lax.all_to_all(prompt_parts.astype(jnp.bfloat16).reshape(devices, rows_he...]
    pallas_call x1, Pallas kernels: 39.1 us -> 61.5 us  [attend(): pl.pallas_call(functools.partial(attention_kernel, n_head), out_shape=(ja...]
    unnamed x4 -> x16, local copies, waits for them, and re-layouts: 1 us -> 5.26 us
    reshape x1 -> x0, other arithmetic: 1.73 us -> none  [per_device(): prompt_parts.astype(jnp.bfloat16).reshape(devices, rows_here, 2 * kv_width)]
    reduce_sum x1, other arithmetic: 0.16 us -> 1.48 us  [per_device(): summed = summed.sum(1).transpose(3, 2, 1, 0, 4)]
where the time goes in v9:
time: 103 us
  Pallas kernels  61.5 us (60%)
  waiting for transfers between devices  17.6 us (17%)
  starting transfers between devices  11.5 us (11%)
  local copies, waits for them, and re-layouts  8.45 us (8%)
  other arithmetic  2.22 us (2%)
  between operations  1.33 us (1%)
    pallas_call x1, Pallas kernels, attend(): pl.pallas_call(functools.partial(attention_kernel, n_head), out_shape=(ja...  61.5 us
    all_to_all x1, waiting for transfers between devices, per_device(): lax.all_to_all(outgoing, ('resp', 'head'), split_axis=0, concat_axis=0, t...  17.6 us
    all_to_all x1, starting transfers between devices, per_device(): lax.all_to_all(outgoing, ('resp', 'head'), split_axis=0, concat_axis=0, t...  11.5 us
    unnamed x16, local copies, waits for them, and re-layouts  5.26 us
  transfers between devices with their start and end apart: 1, of which 1 were waited for; matrix products, arithmetic and copies ran while one was open for 1% of the time, Pallas kernels for 0%

profile of v9, /device:TPU:1, one launch (start us, length us, event | category | flops | bytes accessed | tf_op | source)
XLA Modules:
  0.0 102.5 jit_solution(1441476709803642045)
XLA Ops:
  0.6 0.7 maximum_bitcast_fusion
  1.4 1.1 %broadcast_in_dim.2 = bf16[32,4,8,512]{3,2,1,0:T(8,128)(2,1)} broadcast(bf16[4,8,512]{2,1,0:T(8,128)(2,1)S(1)} %maximum_bitcast_fusion), dimensions={1,2,3} | broadcast | bytes 1081344 | tf_op jit(solution)/shard_map/broadcast_in_dim | solution.py:220
  2.5 0.0 copy-start.5
  2.5 11.5 %all-to-all-start = ((bf16[128,8,512]{2,1,0:T(8,128)(2,1)}), bf16[128,8,512]{2,1,0:T(8,128)(2,1)S(1)}, u32[]{:S(2)}, u32[]{:S(2)}) async-start(bf16[128,8,512]{2,1,0:T(8,128)(2,1)} %bitcast.5), calls=%async_computation | async-start | bytes 2097152 | tf_op jit(solution)/shard_map/all_to_all | solution.py:223
  14.6 0.0 copy-done.5
  14.6 0.9 copy.16.keep_col_ref
  15.5 17.6 %all-to-all-done = bf16[128,8,512]{2,1,0:T(8,128)(2,1)S(1)} async-done(((bf16[128,8,512]{2,1,0:T(8,128)(2,1)}), bf16[128,8,512]{2,1,0:T(8,128)(2,1)S(1)}, u32[]{:S(2)}, u32[]{:S(2)}) %all-to-all-start) | async-done | bytes 1048608 | tf_op jit(solution)/shard_map/all_to_all | solution.py:223
  33.0 0.0 copy-start
  33.0 1.0 copy-done
  34.0 61.5 %shard_map.127 = (bf16[512,1280]{1,0:T(8,128)(2,1)}, bf16[512,1280]{1,0:T(8,128)(2,1)}, bf16[512,256]{1,0:T(8,128)(2,1)}, bf16[512,256]{1,0:T(8,128)(2,1)}, bf16[2,128,8,256]{3,2,1,0:T(8,128)(2,1)}) custom-call(s32[1]{0:T(128)S(6)} %copy.23.length_ref, bf16[512,1280]{1,0:T(8,128)(2,1)} %bitcast.24, bf16[512,1280]{1,0:T(8,128)(2,1)} %bitcast.25, ...), custom_call_target="tpu_custom_call" | custom-call | tf_op jit(solution)/shard_map/pallas_call | solution.py:164
  95.5 0.0 copy-start.2
  95.5 1.5 %convert_reduce_fusion = f32[2,4,8,2,128]{4,2,3,1,0:T(8,128)S(1)} fusion(bf16[2,32,4,8,2,128]{5,3,4,2,1,0:T(8,128)(2,1)} %bitcast.26), kind=kLoop, calls=%fused_computation | loop fusion | flops 1032192 | bytes 1114112 | tf_op jit(solution)/shard_map/reduce_sum | solution.py:240
  97.0 0.6 copy.18
  97.6 0.6 copy.17
  98.3 0.0 copy-done.2
  98.3 0.0 copy-start.1
  98.3 1.1 %copy.24 = bf16[1,512,1280]{2,1,0:T(8,128)(2,1)} copy(bf16[1,512,1280]{2,1,0:T(8,128)(2,1)S(1)} %bitcast.23) | data formatting | bytes 2621440
  99.3 0.7 copy-done.1
  100.0 0.0 copy-start.4
  100.1 0.0 copy-start.3
  100.1 1.1 %copy.25 = bf16[1,512,1280]{2,1,0:T(8,128)(2,1)} copy(bf16[1,512,1280]{2,1,0:T(8,128)(2,1)S(1)} %bitcast.22) | data formatting | bytes 2621440
  101.1 0.0 copy-done.4
  101.1 0.7 copy.26
  101.8 0.0 copy-done.3
  101.8 0.7 copy.27
  (1 shorter events, 0.0 us)
Async XLA Ops:
  2.5 12.2 %copy-start.5 = (s32[1,512]{1,0:T(1,128)S(1)}, s32[1,512]{1,0:T(1,128)}, u32[]{:S(2)}) copy-start(s32[1,512]{1,0:T(1,128)} %param.14) | copy-start | bytes 6148
  2.5 30.6 %all-to-all-start = ((bf16[128,8,512]{2,1,0:T(8,128)(2,1)}), bf16[128,8,512]{2,1,0:T(8,128)(2,1)S(1)}, u32[]{:S(2)}, u32[]{:S(2)}) async-start(bf16[128,8,512]{2,1,0:T(8,128)(2,1)} %bitcast.5), calls=%async_computation | async-start | bytes 2097152 | tf_op jit(solution)/shard_map/all_to_all | solution.py:223
  33.0 1.0 copy-start
  95.5 2.7 %copy-start.2 = (bf16[512,1280]{1,0:T(8,128)(2,1)S(1)}, bf16[512,1280]{1,0:T(8,128)(2,1)}, u32[]{:S(2)}) copy-start(bf16[512,1280]{1,0:T(8,128)(2,1)} %get-tuple-element.11) | copy-start | bytes 3932164
  98.3 1.8 %copy-start.1 = (bf16[512,1280]{1,0:T(8,128)(2,1)S(1)}, bf16[512,1280]{1,0:T(8,128)(2,1)}, u32[]{:S(2)}) copy-start(bf16[512,1280]{1,0:T(8,128)(2,1)} %get-tuple-element.12) | copy-start | bytes 3932164
  100.0 1.1 %copy-start.4 = (bf16[512,256]{1,0:T(8,128)(2,1)S(1)}, bf16[512,256]{1,0:T(8,128)(2,1)}, u32[]{:S(2)}) copy-start(bf16[512,256]{1,0:T(8,128)(2,1)} %get-tuple-element.13) | copy-start | bytes 786436
  100.1 1.8 %copy-start.3 = (bf16[512,256]{1,0:T(8,128)(2,1)S(1)}, bf16[512,256]{1,0:T(8,128)(2,1)}, u32[]{:S(2)}) copy-start(bf16[512,256]{1,0:T(8,128)(2,1)} %get-tuple-element.14) | copy-start | bytes 786436

commit v10 on v3

v10 whole, which is shorter than its diff:
```python
import functools

import jax
import jax.numpy as jnp
from jax import lax
from jax.experimental import pallas as pl
from jax.experimental.pallas import tpu as pltpu
from jax.sharding import PartitionSpec as P

HEAD_DIM = 128
NT = (((1,), (1,)), ((), ()))
TN = (((0,), (0,)), ((), ()))


def attention_kernel(
    length_ref, q_ref, do_ref, kp_ref, vp_ref, ko_ref, vo_ref, keep_col_ref,
    att_ref, dq_ref, dko_ref, dvo_ref, pg_ref, dko_acc, dvo_acc,
):
    f32, bf16 = jnp.float32, jnp.bfloat16
    k = pl.program_id(0)
    g = pl.program_id(1)
    part = pl.program_id(2)
    parts = pl.num_programs(2)
    scale = HEAD_DIM ** (-0.5)
    length = length_ref[0]
    rows = q_ref.shape[0]
    width = HEAD_DIM
    kcol = pl.ds(pl.multiple_of(k * width, width), width)
    vcol = pl.ds(pl.multiple_of((k + pl.num_programs(0)) * width, width), width)

    @pl.when((g == 0) & (part == 0))
    def _():
        dko_acc[...] = jnp.zeros_like(dko_acc)
        dvo_acc[...] = jnp.zeros_like(dvo_acc)
        pg_ref[:, kcol] = jnp.zeros((pg_ref.shape[0], width), f32)
        pg_ref[:, vcol] = jnp.zeros((pg_ref.shape[0], width), f32)

    def compute(first):
        own = first + rows
        q = q_ref[...]
        kp = kp_ref[...]
        ko = ko_ref[:own, :]
        vp = vp_ref[...]
        vo = vo_ref[:own, :]
        sp = lax.dot_general(kp, q, NT, preferred_element_type=f32) * scale
        so = lax.dot_general(ko, q, NT, preferred_element_type=f32) * scale
        j = lax.broadcasted_iota(jnp.int32, (own, 1), 0)
        t = first + lax.broadcasted_iota(jnp.int32, (1, rows), 1)
        allowed = (j <= t) & (j < length)
        so = jnp.where(allowed, so, -jnp.inf)
        top = jnp.maximum(sp.max(0, keepdims=True), so.max(0, keepdims=True))
        ep = jnp.exp(sp - top)
        eo = jnp.exp(so - top)
        inverse = 1.0 / (ep.sum(0, keepdims=True) + eo.sum(0, keepdims=True))
        pp = ep * inverse
        po = eo * inverse
        wp = pp.astype(bf16)
        wo = po.astype(bf16)
        live = t < length
        out = lax.dot_general(vp, wp, TN, preferred_element_type=f32) + lax.dot_general(
            vo, wo, TN, preferred_element_type=f32
        )
        att = jnp.where(live, out, 0.0).astype(bf16).astype(f32)
        att_ref[...] = att.T.astype(bf16)
        live_col = first + lax.broadcasted_iota(jnp.int32, (rows, 1), 0) < length
        factor = (keep_col_ref[...] * live_col.astype(jnp.int32)).astype(bf16)
        do = do_ref[...] * factor
        delta = (do.astype(f32).T * att).sum(0, keepdims=True)
        dpp = lax.dot_general(vp, do, NT, preferred_element_type=f32)
        dpo = lax.dot_general(vo, do, NT, preferred_element_type=f32)
        dsp = (pp * (dpp - delta)).astype(bf16)
        dso = (po * (dpo - delta)).astype(bf16)
        dq = lax.dot_general(kp, dsp, TN, preferred_element_type=f32) + lax.dot_general(
            ko, dso, TN, preferred_element_type=f32
        )
        dq_ref[...] = (dq * scale).T.astype(bf16)
        pg_ref[:, kcol] += jnp.dot(dsp, q, preferred_element_type=f32) * scale
        pg_ref[:, vcol] += jnp.dot(wp, do, preferred_element_type=f32)
        dko_acc[:own, :] += jnp.dot(dso, q, preferred_element_type=f32) * scale
        dvo_acc[:own, :] += jnp.dot(wo, do, preferred_element_type=f32)

    for index in range(ko_ref.shape[0] // rows):

        @pl.when(part == index)
        def _():
            compute(index * rows)

    @pl.when((g == pl.num_programs(1) - 1) & (part == parts - 1))
    def _():
        dko_ref[...] = dko_acc[...].astype(bf16)
        dvo_ref[...] = dvo_acc[...].astype(bf16)


def attend(length, queries, out_grad, prompt_kv, keys, values, keep, kv_count):
    steps, width = queries.shape
    group_size = width // (kv_count * HEAD_DIM)
    prompt_rows = prompt_kv.shape[0]
    parts = 2
    rows = steps // parts
    head_block = lambda k, g, i, n: (i, k * group_size + g)
    kv_block = lambda k, g, i, n: (0, k)
    bf16, f32 = jnp.bfloat16, jnp.float32
    return pl.pallas_call(
        attention_kernel,
        out_shape=(
            jax.ShapeDtypeStruct((steps, width), bf16),
            jax.ShapeDtypeStruct((steps, width), bf16),
            jax.ShapeDtypeStruct(keys.shape, bf16),
            jax.ShapeDtypeStruct(keys.shape, bf16),
            jax.ShapeDtypeStruct((prompt_rows, 2 * kv_count * HEAD_DIM), f32),
        ),
        grid_spec=pltpu.PrefetchScalarGridSpec(
            num_scalar_prefetch=1,
            grid=(kv_count, group_size, parts),
            in_specs=[
                pl.BlockSpec((rows, HEAD_DIM), head_block),
                pl.BlockSpec((rows, HEAD_DIM), head_block),
                pl.BlockSpec((prompt_rows, HEAD_DIM), kv_block),
                pl.BlockSpec((prompt_rows, HEAD_DIM), lambda k, g, i, n: (0, k + kv_count)),
                pl.BlockSpec((steps, HEAD_DIM), kv_block),
                pl.BlockSpec((steps, HEAD_DIM), kv_block),
                pl.BlockSpec((rows, 1), lambda k, g, i, n: (i, 0)),
            ],
            out_specs=[
                pl.BlockSpec((rows, HEAD_DIM), head_block),
                pl.BlockSpec((rows, HEAD_DIM), head_block),
                pl.BlockSpec((steps, HEAD_DIM), kv_block),
                pl.BlockSpec((steps, HEAD_DIM), kv_block),
                pl.BlockSpec((prompt_rows, 2 * kv_count * HEAD_DIM), lambda k, g, i, n: (0, 0)),
            ],
            scratch_shapes=[pltpu.VMEM((steps, HEAD_DIM), f32)] * 2,
        ),
        compiler_params=pltpu.CompilerParams(
            dimension_semantics=("arbitrary", "arbitrary", "arbitrary"),
            vmem_limit_bytes=60 * 1024 * 1024,
        ),
    )(length, queries, out_grad, prompt_kv, prompt_kv, keys, values, keep)


def per_device(
    queries, resp_keys, resp_values, prompt_keys, prompt_values, lengths, loss_mask, out_grad
):
    kv_width = resp_keys.shape[2]
    kv_count = kv_width // HEAD_DIM
    rows_here = prompt_keys.shape[0]
    groups = lax.axis_size("head")
    devices = lax.axis_size("resp") * groups
    both = jnp.concatenate(
        [prompt_keys.reshape(rows_here, groups, kv_width), prompt_values.reshape(rows_here, groups, kv_width)],
        2,
    ).transpose(1, 0, 2)
    outgoing = jnp.broadcast_to(both[None], (devices // groups,) + both.shape).reshape(
        devices, rows_here, 2 * kv_width
    )
    gathered = lax.all_to_all(outgoing, ("resp", "head"), split_axis=0, concat_axis=0, tiled=True)
    prompt_kv = gathered.reshape(devices * rows_here, 2 * kv_width)

    steps = queries.shape[1]
    att, dq, dk, dv, prompt_parts = attend(
        lengths,
        queries.reshape(steps, -1),
        out_grad.reshape(steps, -1),
        prompt_kv,
        resp_keys.reshape(steps, kv_width),
        resp_values.reshape(steps, kv_width),
        loss_mask.reshape(steps, 1),
        kv_count,
    )
    arrived = lax.all_to_all(
        prompt_parts.astype(jnp.bfloat16).reshape(devices, rows_here, 2 * kv_width),
        ("resp", "head"),
        split_axis=0,
        concat_axis=0,
        tiled=True,
    )
    summed = arrived.astype(jnp.float32).reshape(devices // groups, groups, rows_here, 2 * kv_width).sum(0)
    summed = summed.transpose(1, 0, 2)
    prompt_key_grad = summed[:, :, :kv_width].reshape(rows_here, groups * kv_width)
    prompt_value_grad = summed[:, :, kv_width:].reshape(rows_here, groups * kv_width)
    return (
        att.reshape(queries.shape),
        dq.reshape(queries.shape),
        dk.reshape(resp_keys.shape),
        dv.reshape(resp_keys.shape),
        prompt_key_grad,
        prompt_value_grad,
    )


def solution(mesh):
    placed = (
        P("resp", None, "head"),
        P("resp", None, "head"),
        P("resp", None, "head"),
        P(("resp", "head"), None),
        P(("resp", "head"), None),
        P("resp"),
        P("resp", None),
        P("resp", None, "head"),
    )
    return jax.shard_map(
        per_device,
        mesh=mesh,
        in_specs=placed,
        out_specs=(
            P("resp", None, "head"),
            P("resp", None, "head"),
            P("resp", None, "head"),
            P("resp", None, "head"),
            P(("resp", "head"), None),
            P(("resp", "head"), None),
        ),
        check_vma=False,
    )
```

time: 103 us -> 105 us (1.019)
  Pallas kernels: 42.5 us -> 44.7 us
    pallas_call x1, Pallas kernels: 42.5 us -> 44.7 us  [attend(): pl.pallas_call(attention_kernel, out_shape=(jax.ShapeDtypeStruct((steps,...]
where the time goes in v10:
time: 105 us; the launch traced here: 104 us
  Pallas kernels  44.7 us (43%)
  blocking collectives  23.2 us (22%)
  waiting for transfers between devices  17.6 us (17%)
  starting transfers between devices  11.5 us (11%)
  local copies, waits for them, and re-layouts  3.57 us (3%)
  other arithmetic  2.62 us (2%)
  between operations  1.31 us (1%)
    pallas_call x1, Pallas kernels, attend(): pl.pallas_call(attention_kernel, out_shape=(jax.ShapeDtypeStruct((steps,...  44.7 us
    all_to_all x1, blocking collectives, per_device(): lax.all_to_all(prompt_parts.astype(jnp.bfloat16).reshape(devices, rows_he...  23.2 us
    all_to_all x1, waiting for transfers between devices, per_device(): lax.all_to_all(outgoing, ('resp', 'head'), split_axis=0, concat_axis=0, t...  17.6 us
    all_to_all x1, starting transfers between devices, per_device(): lax.all_to_all(outgoing, ('resp', 'head'), split_axis=0, concat_axis=0, t...  11.5 us
  transfers between devices with their start and end apart: 1, of which 1 were waited for; matrix products, arithmetic and copies ran while one was open for 1% of the time, Pallas kernels for 0%

profile of v10, /device:TPU:1, one launch (start us, length us, event | category | flops | bytes accessed | tf_op | source)
XLA Modules:
  0.0 104.5 jit_solution(13656783073898724527)
XLA Ops:
  0.6 0.7 maximum_bitcast_fusion
  1.4 1.1 %broadcast_in_dim.2 = bf16[32,4,8,512]{3,2,1,0:T(8,128)(2,1)} broadcast(bf16[4,8,512]{2,1,0:T(8,128)(2,1)S(1)} %maximum_bitcast_fusion), dimensions={1,2,3} | broadcast | bytes 1081344 | tf_op jit(solution)/shard_map/broadcast_in_dim | solution.py:152
  2.5 0.0 copy-start.1
  2.5 11.5 %all-to-all-start = ((bf16[128,8,512]{2,1,0:T(8,128)(2,1)}), bf16[128,8,512]{2,1,0:T(8,128)(2,1)S(1)}, u32[]{:S(2)}, u32[]{:S(2)}) async-start(bf16[128,8,512]{2,1,0:T(8,128)(2,1)} %bitcast.5), calls=%async_computation | async-start | bytes 2097152 | tf_op jit(solution)/shard_map/all_to_all | solution.py:155
  14.6 0.0 copy-done.1
  14.6 0.8 copy.14.keep_col_ref
  15.5 17.6 %all-to-all-done = bf16[128,8,512]{2,1,0:T(8,128)(2,1)S(1)} async-done(((bf16[128,8,512]{2,1,0:T(8,128)(2,1)}), bf16[128,8,512]{2,1,0:T(8,128)(2,1)S(1)}, u32[]{:S(2)}, u32[]{:S(2)}) %all-to-all-start) | async-done | bytes 1048608 | tf_op jit(solution)/shard_map/all_to_all | solution.py:155
  33.0 0.0 copy-start
  33.0 1.0 copy-done
  34.0 44.7 %shard_map.127 = (bf16[512,1280]{1,0:T(8,128)(2,1)}, bf16[512,1280]{1,0:T(8,128)(2,1)}, bf16[512,256]{1,0:T(8,128)(2,1)}, bf16[512,256]{1,0:T(8,128)(2,1)}, f32[1024,512]{1,0:T(8,128)}) custom-call(s32[1]{0:T(128)S(6)} %copy.15.length_ref, bf16[512,1280]{1,0:T(8,128)(2,1)} %bitcast.25, bf16[512,1280]{1,0:T(8,128)(2,1)} %bitcast.26, ...), custom_call_target="tpu_custom_call" | custom-call | tf_op jit(solution)/shard_map/pallas_call | solution.py:103
  78.7 1.7 %convert_bitcast_fusion = bf16[128,8,512]{2,1,0:T(8,128)(2,1)S(1)} fusion(f32[1024,512]{1,0:T(8,128)} %get-tuple-element.15), kind=kLoop, calls=%fused_computation.1 | loop fusion | flops 524288 | bytes 3145728 | tf_op jit(solution)/shard_map/reshape | solution.py:170
  80.5 23.2 %all_to_all.10 = bf16[128,8,512]{2,1,0:T(8,128)(2,1)S(1)} all-to-all(bf16[128,8,512]{2,1,0:T(8,128)(2,1)S(1)} %convert_bitcast_fusion), channel_id=1, replica_groups=mesh['resp'=32,'head'=4] {'resp','head'}, dimensions={0} | all-to-all | bytes 2097152 | tf_op jit(solution)/shard_map/all_to_all | solution.py:169
  103.7 0.2 convert_reduce_fusion
  103.8 0.6 fusion
Async XLA Ops:
  2.5 12.2 %copy-start.1 = (s32[1,512]{1,0:T(1,128)S(1)}, s32[1,512]{1,0:T(1,128)}, u32[]{:S(2)}) copy-start(s32[1,512]{1,0:T(1,128)} %param.14) | copy-start | bytes 6148
  2.5 30.6 %all-to-all-start = ((bf16[128,8,512]{2,1,0:T(8,128)(2,1)}), bf16[128,8,512]{2,1,0:T(8,128)(2,1)S(1)}, u32[]{:S(2)}, u32[]{:S(2)}) async-start(bf16[128,8,512]{2,1,0:T(8,128)(2,1)} %bitcast.5), calls=%async_computation | async-start | bytes 2097152 | tf_op jit(solution)/shard_map/all_to_all | solution.py:155
  33.0 1.0 copy-start

commit v11 on v6

--- a/solution.py
+++ b/solution.py
@@ -13,7 +13,8 @@
 
 
 def attention_kernel(
-    length_ref, q_ref, do_ref, kp_ref, vp_ref, ko_ref, vo_ref, keep_col_ref,
+    length_ref, q_ref, qt_ref, do_ref, dot_ref, kp_ref, kpt_ref, vp_ref, vpt_ref,
+    ko_ref, kot_ref, vo_ref, vot_ref, keep_col_ref, keep_row_ref,
     att_ref, dq_ref, dko_ref, dvo_ref, pg_ref, dko_acc, dvo_acc,
 ):
     f32, bf16 = jnp.float32, jnp.bfloat16
@@ -23,12 +24,13 @@
     length = length_ref[0]
     steps = q_ref.shape[0]
     q = q_ref[...]
+    qt = qt_ref[...]
     kp = kp_ref[...]
     ko = ko_ref[...]
     vp = vp_ref[...]
     vo = vo_ref[...]
-    sp = lax.dot_general(kp, q, NT, preferred_element_type=f32) * scale
-    so = lax.dot_general(ko, q, NT, preferred_element_type=f32) * scale
+    sp = jnp.dot(kp, qt, preferred_element_type=f32) * scale
+    so = jnp.dot(ko, qt, preferred_element_type=f32) * scale
     j = lax.broadcasted_iota(jnp.int32, (steps, 1), 0)
     t = lax.broadcasted_iota(jnp.int32, (1, steps), 1)
     allowed = (j <= t) & (j < length)
@@ -42,21 +44,21 @@
     wp = pp.astype(bf16)
     wo = po.astype(bf16)
     live = t < length
-    out = lax.dot_general(vp, wp, TN, preferred_element_type=f32) + lax.dot_general(
-        vo, wo, TN, preferred_element_type=f32
+    out = jnp.dot(vpt_ref[...], wp, preferred_element_type=f32) + jnp.dot(
+        vot_ref[...], wo, preferred_element_type=f32
     )
     att = jnp.where(live, out, 0.0).astype(bf16).astype(f32)
     att_ref[...] = att.T.astype(bf16)
     live_col = lax.broadcasted_iota(jnp.int32, (steps, 1), 0) < length
-    factor = (keep_col_ref[...] * live_col.astype(jnp.int32)).astype(bf16)
-    do = do_ref[...] * factor
-    delta = (do.astype(f32).T * att).sum(0, keepdims=True)
-    dpp = lax.dot_general(vp, do, NT, preferred_element_type=f32)
-    dpo = lax.dot_general(vo, do, NT, preferred_element_type=f32)
+    do = do_ref[...] * (keep_col_ref[...] * live_col.astype(jnp.int32)).astype(bf16)
+    dot = dot_ref[...] * (keep_row_ref[...] * live.astype(jnp.int32)).astype(bf16)
+    delta = (dot.astype(f32) * att).sum(0, keepdims=True)
+    dpp = jnp.dot(vp, dot, preferred_element_type=f32)
+    dpo = jnp.dot(vo, dot, preferred_element_type=f32)
     dsp = (pp * (dpp - delta)).astype(bf16)
     dso = (po * (dpo - delta)).astype(bf16)
-    dq = lax.dot_general(kp, dsp, TN, preferred_element_type=f32) + lax.dot_general(
-        ko, dso, TN, preferred_element_type=f32
+    dq = jnp.dot(kpt_ref[...], dsp, preferred_element_type=f32) + jnp.dot(
+        kot_ref[...], dso, preferred_element_type=f32
     )
     dq_ref[...] = (dq * scale).T.astype(bf16)
     dkp = jnp.dot(dsp, q, preferred_element_type=f32) * scale
@@ -108,12 +110,19 @@
             grid=(kv_count, group_size),
             in_specs=[
                 pl.BlockSpec((steps, HEAD_DIM), head_block),
-                pl.BlockSpec((steps, HEAD_DIM), head_block),
+                pl.BlockSpec((HEAD_DIM, steps), lambda k, g, n: (k * group_size + g, 0)),
+                pl.BlockSpec((steps, HEAD_DIM), head_block),
+                pl.BlockSpec((HEAD_DIM, steps), lambda k, g, n: (k * group_size + g, 0)),
                 pl.BlockSpec((prompt_rows, HEAD_DIM), kv_block),
+                pl.BlockSpec((HEAD_DIM, prompt_rows), lambda k, g, n: (k, 0)),
                 pl.BlockSpec((prompt_rows, HEAD_DIM), lambda k, g, n: (0, k + kv_count)),
-                pl.BlockSpec((steps, HEAD_DIM), kv_block),
-                pl.BlockSpec((steps, HEAD_DIM), kv_block),
+                pl.BlockSpec((HEAD_DIM, prompt_rows), lambda k, g, n: (k + kv_count, 0)),
+                pl.BlockSpec((steps, HEAD_DIM), kv_block),
+                pl.BlockSpec((HEAD_DIM, steps), lambda k, g, n: (k, 0)),
+                pl.BlockSpec((steps, HEAD_DIM), kv_block),
+                pl.BlockSpec((HEAD_DIM, steps), lambda k, g, n: (k, 0)),
                 pl.BlockSpec((steps, 1), lambda k, g, n: (0, 0)),
+                pl.BlockSpec((1, steps), lambda k, g, n: (0, 0)),
             ],
             out_specs=[
                 pl.BlockSpec((steps, HEAD_DIM), head_block),
@@ -128,7 +137,23 @@
             dimension_semantics=("arbitrary", "arbitrary"),
             vmem_limit_bytes=60 * 1024 * 1024,
         ),
-    )(length, queries, out_grad, prompt_kv, prompt_kv, keys, values, keep)
+    )(
+        length,
+        queries,
+        queries.T,
+        out_grad,
+        out_grad.T,
+        prompt_kv,
+        prompt_kv.T,
+        prompt_kv,
+        prompt_kv.T,
+        keys,
+        keys.T,
+        values,
+        values.T,
+        keep,
+        keep.reshape(1, steps),
+    )
 
 
 def per_device(

time: 99.2 us -> 98.8 us (level)
  local copies, waits for them, and re-layouts: 3.57 us -> 9.58 us
  waiting for transfers between devices: 17.6 us -> 11.9 us
    all_to_all x1, waiting for transfers between devices: 17.6 us -> 11.9 us  [per_device(): lax.all_to_all(outgoing, ('resp', 'head'), split_axis=0, concat_axis=0, t...]
    unnamed x4 -> x14, local copies, waits for them, and re-layouts: 1 us -> 5.63 us
    reshape x0 -> x1, local copies, waits for them, and re-layouts: none -> 1.37 us  [per_device(): prompt_kv = gathered.reshape(devices * rows_here, 2 * kv_width)]
  transfers between devices with their start and end apart: 1 -> 1, of which waited for: 1 -> 1; matrix products, arithmetic and copies ran while one was open for 1% -> 7% of each run, Pallas kernels for 0% -> 0%
where the time goes in v11:
time: 98.8 us; the launch traced here: 98.4 us
  Pallas kernels  38.3 us (39%)
  blocking collectives  23.2 us (23%)
  waiting for transfers between devices  11.9 us (12%)
  starting transfers between devices  11.5 us (12%)
  local copies, waits for them, and re-layouts  9.58 us (10%)
  other arithmetic  2.62 us (3%)
  between operations  1.32 us (1%)
    pallas_call x1, Pallas kernels, attend(): pl.pallas_call(attention_kernel, out_shape=(jax.ShapeDtypeStruct((steps,...  38.3 us
    all_to_all x1, blocking collectives, per_device(): lax.all_to_all(prompt_parts.astype(jnp.bfloat16).reshape(devices, rows_he...  23.2 us
    all_to_all x1, waiting for transfers between devices, per_device(): lax.all_to_all(outgoing, ('resp', 'head'), split_axis=0, concat_axis=0, t...  11.9 us
    all_to_all x1, starting transfers between devices, per_device(): lax.all_to_all(outgoing, ('resp', 'head'), split_axis=0, concat_axis=0, t...  11.5 us
    unnamed x14, local copies, waits for them, and re-layouts  5.63 us
  transfers between devices with their start and end apart: 1, of which 1 were waited for; matrix products, arithmetic and copies ran while one was open for 7% of the time, Pallas kernels for 0%

profile of v11, /device:TPU:1, one launch (start us, length us, event | category | flops | bytes accessed | tf_op | source)
XLA Modules:
  0.0 98.4 jit_solution(401245235335318143)
XLA Ops:
  0.6 0.7 maximum_bitcast_fusion
  1.4 1.1 %broadcast_in_dim.2 = bf16[32,4,8,512]{3,2,1,0:T(8,128)(2,1)} broadcast(bf16[4,8,512]{2,1,0:T(8,128)(2,1)S(1)} %maximum_bitcast_fusion), dimensions={1,2,3} | broadcast | bytes 1081344 | tf_op jit(solution)/shard_map/broadcast_in_dim | solution.py:171
  2.5 0.0 copy-start.4
  2.5 0.0 copy-start.2
  2.5 0.0 copy-start.3
  2.5 0.0 copy-start.1
  2.5 11.5 %all-to-all-start = ((bf16[128,8,512]{2,1,0:T(8,128)(2,1)}), bf16[128,8,512]{2,1,0:T(8,128)(2,1)S(1)}, u32[]{:S(2)}, u32[]{:S(2)}) async-start(bf16[128,8,512]{2,1,0:T(8,128)(2,1)} %bitcast.9), calls=%async_computation | async-start | bytes 2097152 | tf_op jit(solution)/shard_map/all_to_all | solution.py:174
  14.6 0.0 copy-done.4
  14.6 0.9 copy.34.keep_col_ref
  15.5 0.0 copy-done.2
  15.5 0.8 copy.28
  16.3 0.0 copy-done.3
  16.3 0.9 copy.29
  17.2 0.0 copy-done.1
  17.2 1.5 %copy.25 = bf16[1,512,1280]{1,2,0:T(8,128)(2,1)} copy(bf16[1,512,1280]{2,1,0:T(8,128)(2,1)S(1)} %copy-done.1) | data formatting | bytes 2621440 | tf_op args[0]
  18.7 2.4 %copy.26 = bf16[1,512,1280]{1,2,0:T(8,128)(2,1)} copy(bf16[1,512,1280]{2,1,0:T(8,128)(2,1)} %param.15) | data formatting | bytes 2621440 | tf_op args[7]
  21.1 11.9 %all-to-all-done = bf16[128,8,512]{2,1,0:T(8,128)(2,1)S(1)} async-done(((bf16[128,8,512]{2,1,0:T(8,128)(2,1)}), bf16[128,8,512]{2,1,0:T(8,128)(2,1)S(1)}, u32[]{:S(2)}, u32[]{:S(2)}) %all-to-all-start) | async-done | bytes 1048608 | tf_op jit(solution)/shard_map/all_to_all | solution.py:174
  33.1 0.0 copy-start
  33.1 1.4 %copy.27 = bf16[1024,512]{0,1:T(8,128)(2,1)} copy(bf16[1024,512]{1,0:T(8,128)(2,1)S(1)} %bitcast.35) | data formatting | bytes 2097152 | tf_op jit(solution)/shard_map/reshape | solution.py:175
  34.4 0.0 copy-done
  34.4 38.3 %shard_map.127 = (bf16[512,1280]{1,0:T(8,128)(2,1)}, bf16[512,1280]{1,0:T(8,128)(2,1)}, bf16[512,256]{1,0:T(8,128)(2,1)}, bf16[512,256]{1,0:T(8,128)(2,1)}, f32[1024,512]{1,0:T(8,128)}) custom-call(s32[1]{0:T(128)S(6)} %copy.39.length_ref, bf16[512,1280]{1,0:T(8,128)(2,1)} %bitcast.40, bf16[1280,512]{1,0:T(8,128)(2,1)} %bitcast.42, ...), custom_call_target="tpu_custom_call" | custom-call | tf_op jit(solution)/shard_map/pallas_call | solution.py:99
  72.8 1.7 %convert_bitcast_fusion = bf16[128,8,512]{2,1,0:T(8,128)(2,1)S(1)} fusion(f32[1024,512]{1,0:T(8,128)} %get-tuple-element.15), kind=kLoop, calls=%fused_computation.1 | loop fusion | flops 524288 | bytes 3145728 | tf_op jit(solution)/shard_map/reshape | solution.py:189
  74.5 23.2 %all_to_all.10 = bf16[128,8,512]{2,1,0:T(8,128)(2,1)S(1)} all-to-all(bf16[128,8,512]{2,1,0:T(8,128)(2,1)S(1)} %convert_bitcast_fusion), channel_id=1, replica_groups=mesh['resp'=32,'head'=4] {'resp','head'}, dimensions={0} | all-to-all | bytes 2097152 | tf_op jit(solution)/shard_map/all_to_all | solution.py:188
  97.6 0.2 convert_reduce_fusion
  97.8 0.6 fusion
Async XLA Ops:
  2.5 12.2 %copy-start.4 = (s32[1,512]{1,0:T(1,128)S(1)}, s32[1,512]{1,0:T(1,128)}, u32[]{:S(2)}) copy-start(s32[1,512]{1,0:T(1,128)} %keep_row_ref.1) | copy-start | bytes 6148
  2.5 13.0 %copy-start.2 = (bf16[1,512,256]{2,1,0:T(8,128)(2,1)S(1)}, bf16[1,512,256]{2,1,0:T(8,128)(2,1)}, u32[]{:S(2)}) copy-start(bf16[1,512,256]{2,1,0:T(8,128)(2,1)} %param.9) | copy-start | bytes 786436
  2.5 13.9 %copy-start.3 = (bf16[1,512,256]{2,1,0:T(8,128)(2,1)S(1)}, bf16[1,512,256]{2,1,0:T(8,128)(2,1)}, u32[]{:S(2)}) copy-start(bf16[1,512,256]{2,1,0:T(8,128)(2,1)} %param.10) | copy-start | bytes 786436
  2.5 14.7 %copy-start.1 = (bf16[1,512,1280]{2,1,0:T(8,128)(2,1)S(1)}, bf16[1,512,1280]{2,1,0:T(8,128)(2,1)}, u32[]{:S(2)}) copy-start(bf16[1,512,1280]{2,1,0:T(8,128)(2,1)} %param.8) | copy-start | bytes 3932164
  2.5 30.6 %all-to-all-start = ((bf16[128,8,512]{2,1,0:T(8,128)(2,1)}), bf16[128,8,512]{2,1,0:T(8,128)(2,1)S(1)}, u32[]{:S(2)}, u32[]{:S(2)}) async-start(bf16[128,8,512]{2,1,0:T(8,128)(2,1)} %bitcast.9), calls=%async_computation | async-start | bytes 2097152 | tf_op jit(solution)/shard_map/all_to_all | solution.py:174
  33.1 1.4 %copy-start = (bf16[128,8,512]{2,1,0:T(8,128)(2,1)}, bf16[128,8,512]{2,1,0:T(8,128)(2,1)S(1)}, u32[]{:S(2)}) copy-start(bf16[128,8,512]{2,1,0:T(8,128)(2,1)S(1)} %all-to-all-done) | copy-start | bytes 3145732

commit v12 on v11

--- a/solution.py
+++ b/solution.py
@@ -15,7 +15,7 @@
 def attention_kernel(
     length_ref, q_ref, qt_ref, do_ref, dot_ref, kp_ref, kpt_ref, vp_ref, vpt_ref,
     ko_ref, kot_ref, vo_ref, vot_ref, keep_col_ref, keep_row_ref,
-    att_ref, dq_ref, dko_ref, dvo_ref, pg_ref, dko_acc, dvo_acc,
+    att_ref, dq_ref, dko_ref, dvo_ref, pg_out, dko_acc, dvo_acc, pg_ref,
 ):
     f32, bf16 = jnp.float32, jnp.bfloat16
     k = pl.program_id(0)
@@ -87,6 +87,8 @@
     def _():
         dko_ref[...] = dko_acc[...].astype(bf16)
         dvo_ref[...] = dvo_acc[...].astype(bf16)
+        pg_out[:, kcol] = pg_ref[:, kcol].astype(bf16)
+        pg_out[:, vcol] = pg_ref[:, vcol].astype(bf16)
 
 
 def attend(length, queries, out_grad, prompt_kv, keys, values, keep, kv_count):
@@ -103,7 +105,7 @@
             jax.ShapeDtypeStruct((steps, width), bf16),
             jax.ShapeDtypeStruct(keys.shape, bf16),
             jax.ShapeDtypeStruct(keys.shape, bf16),
-            jax.ShapeDtypeStruct((prompt_rows, 2 * kv_count * HEAD_DIM), f32),
+            jax.ShapeDtypeStruct((prompt_rows, 2 * kv_count * HEAD_DIM), bf16),
         ),
         grid_spec=pltpu.PrefetchScalarGridSpec(
             num_scalar_prefetch=1,
@@ -131,7 +133,8 @@
                 pl.BlockSpec((steps, HEAD_DIM), kv_block),
                 pl.BlockSpec((prompt_rows, 2 * kv_count * HEAD_DIM), lambda k, g, n: (0, 0)),
             ],
-            scratch_shapes=[pltpu.VMEM((steps, HEAD_DIM), f32)] * 2,
+            scratch_shapes=[pltpu.VMEM((steps, HEAD_DIM), f32)] * 2
+            + [pltpu.VMEM((prompt_rows, 2 * kv_count * HEAD_DIM), f32)],
         ),
         compiler_params=pltpu.CompilerParams(
             dimension_semantics=("arbitrary", "arbitrary"),
@@ -186,7 +189,7 @@
         kv_count,
     )
     arrived = lax.all_to_all(
-        prompt_parts.astype(jnp.bfloat16).reshape(devices, rows_here, 2 * kv_width),
+        prompt_parts.reshape(devices, rows_here, 2 * kv_width),
         ("resp", "head"),
         split_axis=0,
         concat_axis=0,

time: 98.8 us -> 98 us (level)
  other arithmetic: 2.62 us -> 0.9 us
    reshape x1 -> x0, other arithmetic: 1.73 us -> none  [per_device(): prompt_parts.astype(jnp.bfloat16).reshape(devices, rows_here, 2 * kv_width)]
where the time goes in v12:
time: 98 us; the launch traced here: 97.6 us
  Pallas kernels  38.3 us (39%)
  blocking collectives  24 us (24%)
  waiting for transfers between devices  12 us (12%)
  starting transfers between devices  11.5 us (12%)
  local copies, waits for them, and re-layouts  9.5 us (10%)
  between operations  1.31 us (1%)
    pallas_call x1, Pallas kernels, attend(): pl.pallas_call(attention_kernel, out_shape=(jax.ShapeDtypeStruct((steps,...  38.3 us
    all_to_all x1, blocking collectives, per_device(): lax.all_to_all(prompt_parts.reshape(devices, rows_here, 2 * kv_width), ('...  24 us
    all_to_all x1, waiting for transfers between devices, per_device(): lax.all_to_all(outgoing, ('resp', 'head'), split_axis=0, concat_axis=0, t...  12 us
    all_to_all x1, starting transfers between devices, per_device(): lax.all_to_all(outgoing, ('resp', 'head'), split_axis=0, concat_axis=0, t...  11.5 us
    unnamed x14, local copies, waits for them, and re-layouts  5.6 us
  transfers between devices with their start and end apart: 1, of which 1 were waited for; matrix products, arithmetic and copies ran while one was open for 7% of the time, Pallas kernels for 0%

profile of v12, /device:TPU:1, one launch (start us, length us, event | category | flops | bytes accessed | tf_op | source)
XLA Modules:
  0.0 97.6 jit_solution(1692256137966489354)
XLA Ops:
  0.6 0.7 maximum_bitcast_fusion
  1.4 1.1 %broadcast_in_dim.2 = bf16[32,4,8,512]{3,2,1,0:T(8,128)(2,1)} broadcast(bf16[4,8,512]{2,1,0:T(8,128)(2,1)S(1)} %maximum_bitcast_fusion), dimensions={1,2,3} | broadcast | bytes 1081344 | tf_op jit(solution)/shard_map/broadcast_in_dim | solution.py:174
  2.5 0.0 copy-start.4
  2.5 0.0 copy-start.2
  2.5 0.0 copy-start.3
  2.5 0.0 copy-start.1
  2.5 11.5 %all-to-all-start = ((bf16[128,8,512]{2,1,0:T(8,128)(2,1)}), bf16[128,8,512]{2,1,0:T(8,128)(2,1)S(1)}, u32[]{:S(2)}, u32[]{:S(2)}) async-start(bf16[128,8,512]{2,1,0:T(8,128)(2,1)} %bitcast.9), calls=%async_computation | async-start | bytes 2097152 | tf_op jit(solution)/shard_map/all_to_all | solution.py:177
  14.6 0.0 copy-done.4
  14.6 0.8 copy.34.keep_col_ref
  15.5 0.0 copy-done.2
  15.5 0.8 copy.28
  16.3 0.0 copy-done.3
  16.3 0.8 copy.29
  17.2 0.0 copy-done.1
  17.2 1.5 %copy.25 = bf16[1,512,1280]{1,2,0:T(8,128)(2,1)} copy(bf16[1,512,1280]{2,1,0:T(8,128)(2,1)S(1)} %copy-done.1) | data formatting | bytes 2621440 | tf_op args[0]
  18.6 2.4 %copy.26 = bf16[1,512,1280]{1,2,0:T(8,128)(2,1)} copy(bf16[1,512,1280]{2,1,0:T(8,128)(2,1)} %param.15) | data formatting | bytes 2621440 | tf_op args[7]
  21.1 12.0 %all-to-all-done = bf16[128,8,512]{2,1,0:T(8,128)(2,1)S(1)} async-done(((bf16[128,8,512]{2,1,0:T(8,128)(2,1)}), bf16[128,8,512]{2,1,0:T(8,128)(2,1)S(1)}, u32[]{:S(2)}, u32[]{:S(2)}) %all-to-all-start) | async-done | bytes 1048608 | tf_op jit(solution)/shard_map/all_to_all | solution.py:177
  33.1 0.0 copy-start
  33.1 1.3 %copy.27 = bf16[1024,512]{0,1:T(8,128)(2,1)} copy(bf16[1024,512]{1,0:T(8,128)(2,1)S(1)} %bitcast.34) | data formatting | bytes 2097152 | tf_op jit(solution)/shard_map/reshape | solution.py:178
  34.4 0.0 copy-done
  34.4 38.3 %shard_map.127 = (bf16[512,1280]{1,0:T(8,128)(2,1)}, bf16[512,1280]{1,0:T(8,128)(2,1)}, bf16[512,256]{1,0:T(8,128)(2,1)}, bf16[512,256]{1,0:T(8,128)(2,1)}, bf16[1024,512]{1,0:T(8,128)(2,1)}) custom-call(s32[1]{0:T(128)S(6)} %copy.39.length_ref, bf16[512,1280]{1,0:T(8,128)(2,1)} %bitcast.39, bf16[1280,512]{1,0:T(8,128)(2,1)} %bitcast.41, ...), custom_call_target="tpu_custom_call" | custom-call | tf_op jit(solution)/shard_map/pallas_call | solution.py:101
  72.7 24.0 %all_to_all.10 = bf16[128,8,512]{2,1,0:T(8,128)(2,1)S(1)} all-to-all(bf16[128,8,512]{2,1,0:T(8,128)(2,1)} %bitcast.48), channel_id=1, replica_groups=mesh['resp'=32,'head'=4] {'resp','head'}, dimensions={0} | all-to-all | bytes 2097152 | tf_op jit(solution)/shard_map/all_to_all | solution.py:191
  96.8 0.2 convert_reduce_fusion
  96.9 0.6 fusion
Async XLA Ops:
  2.5 12.2 %copy-start.4 = (s32[1,512]{1,0:T(1,128)S(1)}, s32[1,512]{1,0:T(1,128)}, u32[]{:S(2)}) copy-start(s32[1,512]{1,0:T(1,128)} %keep_row_ref.1) | copy-start | bytes 6148
  2.5 13.0 %copy-start.2 = (bf16[1,512,256]{2,1,0:T(8,128)(2,1)S(1)}, bf16[1,512,256]{2,1,0:T(8,128)(2,1)}, u32[]{:S(2)}) copy-start(bf16[1,512,256]{2,1,0:T(8,128)(2,1)} %param.9) | copy-start | bytes 786436
  2.5 13.9 %copy-start.3 = (bf16[1,512,256]{2,1,0:T(8,128)(2,1)S(1)}, bf16[1,512,256]{2,1,0:T(8,128)(2,1)}, u32[]{:S(2)}) copy-start(bf16[1,512,256]{2,1,0:T(8,128)(2,1)} %param.10) | copy-start | bytes 786436
  2.5 14.7 %copy-start.1 = (bf16[1,512,1280]{2,1,0:T(8,128)(2,1)S(1)}, bf16[1,512,1280]{2,1,0:T(8,128)(2,1)}, u32[]{:S(2)}) copy-start(bf16[1,512,1280]{2,1,0:T(8,128)(2,1)} %param.8) | copy-start | bytes 3932164
  2.5 30.6 %all-to-all-start = ((bf16[128,8,512]{2,1,0:T(8,128)(2,1)}), bf16[128,8,512]{2,1,0:T(8,128)(2,1)S(1)}, u32[]{:S(2)}, u32[]{:S(2)}) async-start(bf16[128,8,512]{2,1,0:T(8,128)(2,1)} %bitcast.9), calls=%async_computation | async-start | bytes 2097152 | tf_op jit(solution)/shard_map/all_to_all | solution.py:177
  33.1 1.3 %copy-start = (bf16[128,8,512]{2,1,0:T(8,128)(2,1)}, bf16[128,8,512]{2,1,0:T(8,128)(2,1)S(1)}, u32[]{:S(2)}) copy-start(bf16[128,8,512]{2,1,0:T(8,128)(2,1)S(1)} %all-to-all-done) | copy-start | bytes 3145732

commit v13 on v12

v13 whole, which is shorter than its diff:
```python
import functools

import jax
import jax.numpy as jnp
from jax import lax
from jax.experimental import pallas as pl
from jax.experimental.pallas import tpu as pltpu
from jax.sharding import PartitionSpec as P

HEAD_DIM = 128
NT = (((1,), (1,)), ((), ()))
TN = (((0,), (0,)), ((), ()))


def attention_kernel(
    length_ref, q_ref, qt_ref, do_ref, dot_ref, kp_ref, kpt_ref, vp_ref, vpt_ref,
    ko_ref, kot_ref, vo_ref, vot_ref, keep_col_ref, keep_row_ref,
    att_ref, dq_ref, dko_ref, dvo_ref, pg_out, dko_acc, dvo_acc, pg_ref,
):
    f32, bf16 = jnp.float32, jnp.bfloat16
    scale = HEAD_DIM ** (-0.5)
    length = length_ref[0]
    steps = q_ref.shape[0]
    width = HEAD_DIM
    group_size = q_ref.shape[1] // width
    j = lax.broadcasted_iota(jnp.int32, (steps, 1), 0)
    t = lax.broadcasted_iota(jnp.int32, (1, steps), 1)
    allowed = (j <= t) & (j < length)
    live = t < length
    live_col = j < length
    factor_col = (keep_col_ref[...] * live_col.astype(jnp.int32)).astype(bf16)
    factor_row = (keep_row_ref[...] * live.astype(jnp.int32)).astype(bf16)
    dko_acc[...] = jnp.zeros_like(dko_acc)
    dvo_acc[...] = jnp.zeros_like(dvo_acc)
    pg_ref[...] = jnp.zeros_like(pg_ref)

    def head(h, carry):
        cols = pl.ds(pl.multiple_of(h * width, width), width)
        q = q_ref[:, cols]
        qt = qt_ref[cols, :]
        kp = kp_ref[...]
        ko = ko_ref[...]
        vp = vp_ref[...]
        vo = vo_ref[...]
        sp = jnp.dot(kp, qt, preferred_element_type=f32) * scale
        so = jnp.dot(ko, qt, preferred_element_type=f32) * scale
        so = jnp.where(allowed, so, -jnp.inf)
        top = jnp.maximum(sp.max(0, keepdims=True), so.max(0, keepdims=True))
        ep = jnp.exp(sp - top)
        eo = jnp.exp(so - top)
        inverse = 1.0 / (ep.sum(0, keepdims=True) + eo.sum(0, keepdims=True))
        pp = ep * inverse
        po = eo * inverse
        wp = pp.astype(bf16)
        wo = po.astype(bf16)
        out = jnp.dot(vpt_ref[...], wp, preferred_element_type=f32) + jnp.dot(
            vot_ref[...], wo, preferred_element_type=f32
        )
        att = jnp.where(live, out, 0.0).astype(bf16).astype(f32)
        att_ref[:, cols] = att.T.astype(bf16)
        do = do_ref[:, cols] * factor_col
        dot = dot_ref[cols, :] * factor_row
        delta = (dot.astype(f32) * att).sum(0, keepdims=True)
        dpp = jnp.dot(vp, dot, preferred_element_type=f32)
        dpo = jnp.dot(vo, dot, preferred_element_type=f32)
        dsp = (pp * (dpp - delta)).astype(bf16)
        dso = (po * (dpo - delta)).astype(bf16)
        dq = jnp.dot(kpt_ref[...], dsp, preferred_element_type=f32) + jnp.dot(
            kot_ref[...], dso, preferred_element_type=f32
        )
        dq_ref[:, cols] = (dq * scale).T.astype(bf16)
        pg_ref[:, :width] += jnp.dot(dsp, q, preferred_element_type=f32) * scale
        pg_ref[:, width:] += jnp.dot(wp, do, preferred_element_type=f32)
        dko_acc[...] += jnp.dot(dso, q, preferred_element_type=f32) * scale
        dvo_acc[...] += jnp.dot(wo, do, preferred_element_type=f32)
        return carry

    lax.fori_loop(0, group_size, head, 0)
    dko_ref[...] = dko_acc[...].astype(bf16)
    dvo_ref[...] = dvo_acc[...].astype(bf16)
    pg_out[:, :width] = pg_ref[:, :width].astype(bf16)
    pg_out[:, width:] = pg_ref[:, width:].astype(bf16)


def attend(length, queries, out_grad, prompt_kv, keys, values, keep, kv_count):
    steps, width = queries.shape
    group_size = width // (kv_count * HEAD_DIM)
    prompt_rows = prompt_kv.shape[0]
    heads = group_size * HEAD_DIM
    kv_block = lambda k, n: (0, k)
    kv_block_t = lambda k, n: (k, 0)
    bf16, f32 = jnp.bfloat16, jnp.float32
    return pl.pallas_call(
        attention_kernel,
        out_shape=(
            jax.ShapeDtypeStruct((steps, width), bf16),
            jax.ShapeDtypeStruct((steps, width), bf16),
            jax.ShapeDtypeStruct(keys.shape, bf16),
            jax.ShapeDtypeStruct(keys.shape, bf16),
            jax.ShapeDtypeStruct((prompt_rows, 2 * kv_count * HEAD_DIM), bf16),
        ),
        grid_spec=pltpu.PrefetchScalarGridSpec(
            num_scalar_prefetch=1,
            grid=(kv_count,),
            in_specs=[
                pl.BlockSpec((steps, heads), kv_block),
                pl.BlockSpec((heads, steps), kv_block_t),
                pl.BlockSpec((steps, heads), kv_block),
                pl.BlockSpec((heads, steps), kv_block_t),
                pl.BlockSpec((prompt_rows, HEAD_DIM), kv_block),
                pl.BlockSpec((HEAD_DIM, prompt_rows), kv_block_t),
                pl.BlockSpec((prompt_rows, HEAD_DIM), lambda k, n: (0, k + kv_count)),
                pl.BlockSpec((HEAD_DIM, prompt_rows), lambda k, n: (k + kv_count, 0)),
                pl.BlockSpec((steps, HEAD_DIM), kv_block),
                pl.BlockSpec((HEAD_DIM, steps), kv_block_t),
                pl.BlockSpec((steps, HEAD_DIM), kv_block),
                pl.BlockSpec((HEAD_DIM, steps), kv_block_t),
                pl.BlockSpec((steps, 1), lambda k, n: (0, 0)),
                pl.BlockSpec((1, steps), lambda k, n: (0, 0)),
            ],
            out_specs=[
                pl.BlockSpec((steps, heads), kv_block),
                pl.BlockSpec((steps, heads), kv_block),
                pl.BlockSpec((steps, HEAD_DIM), kv_block),
                pl.BlockSpec((steps, HEAD_DIM), kv_block),
                pl.BlockSpec((prompt_rows, 2 * HEAD_DIM), kv_block),
            ],
            scratch_shapes=[pltpu.VMEM((steps, HEAD_DIM), f32)] * 2
            + [pltpu.VMEM((prompt_rows, 2 * HEAD_DIM), f32)],
        ),
        compiler_params=pltpu.CompilerParams(
            dimension_semantics=("arbitrary",),
            vmem_limit_bytes=60 * 1024 * 1024,
        ),
    )(
        length,
        queries,
        queries.T,
        out_grad,
        out_grad.T,
        prompt_kv,
        prompt_kv.T,
        prompt_kv,
        prompt_kv.T,
        keys,
        keys.T,
        values,
        values.T,
        keep,
        keep.reshape(1, steps),
    )


def per_device(
    queries, resp_keys, resp_values, prompt_keys, prompt_values, lengths, loss_mask, out_grad
):
    kv_width = resp_keys.shape[2]
    kv_count = kv_width // HEAD_DIM
    rows_here = prompt_keys.shape[0]
    groups = lax.axis_size("head")
    devices = lax.axis_size("resp") * groups
    both = jnp.concatenate(
        [prompt_keys.reshape(rows_here, groups, kv_width), prompt_values.reshape(rows_here, groups, kv_width)],
        2,
    ).transpose(1, 0, 2)
    outgoing = jnp.broadcast_to(both[None], (devices // groups,) + both.shape).reshape(
        devices, rows_here, 2 * kv_width
    )
    gathered = lax.all_to_all(outgoing, ("resp", "head"), split_axis=0, concat_axis=0, tiled=True)
    prompt_kv = gathered.reshape(devices * rows_here, 2 * kv_width)

    steps = queries.shape[1]
    att, dq, dk, dv, prompt_parts = attend(
        lengths,
        queries.reshape(steps, -1),
        out_grad.reshape(steps, -1),
        prompt_kv,
        resp_keys.reshape(steps, kv_width),
        resp_values.reshape(steps, kv_width),
        loss_mask.reshape(steps, 1),
        kv_count,
    )
    arrived = lax.all_to_all(
        prompt_parts.reshape(devices, rows_here, 2 * kv_width),
        ("resp", "head"),
        split_axis=0,
        concat_axis=0,
        tiled=True,
    )
    summed = arrived.astype(jnp.float32).reshape(devices // groups, groups, rows_here, 2 * kv_width).sum(0)
    summed = summed.reshape(groups, rows_here, kv_count, 2, HEAD_DIM).transpose(3, 1, 0, 2, 4)
    prompt_key_grad = summed[0].reshape(rows_here, groups * kv_width)
    prompt_value_grad = summed[1].reshape(rows_here, groups * kv_width)
    return (
        att.reshape(queries.shape),
        dq.reshape(queries.shape),
        dk.reshape(resp_keys.shape),
        dv.reshape(resp_keys.shape),
        prompt_key_grad,
        prompt_value_grad,
    )


def solution(mesh):
    placed = (
        P("resp", None, "head"),
        P("resp", None, "head"),
        P("resp", None, "head"),
        P(("resp", "head"), None),
        P(("resp", "head"), None),
        P("resp"),
        P("resp", None),
        P("resp", None, "head"),
    )
    return jax.shard_map(
        per_device,
        mesh=mesh,
        in_specs=placed,
        out_specs=(
            P("resp", None, "head"),
            P("resp", None, "head"),
            P("resp", None, "head"),
            P("resp", None, "head"),
            P(("resp", "head"), None),
            P(("resp", "head"), None),
        ),
        check_vma=False,
    )
```

time: 98 us -> 95.7 us (0.977)
  Pallas kernels: 38.3 us -> 36 us
    pallas_call x1, Pallas kernels: 38.3 us -> 36 us  [attend(): pl.pallas_call(attention_kernel, out_shape=(jax.ShapeDtypeStruct((steps,...]
where the time goes in v13:
time: 95.7 us; the launch traced here: 95.2 us
  Pallas kernels  36 us (38%)
  blocking collectives  24 us (25%)
  waiting for transfers between devices  12 us (13%)
  starting transfers between devices  11.5 us (12%)
  local copies, waits for them, and re-layouts  9.5 us (10%)
  between operations  1.31 us (1%)
    pallas_call x1, Pallas kernels, attend(): pl.pallas_call(attention_kernel, out_shape=(jax.ShapeDtypeStruct((steps,...  36 us
    all_to_all x1, blocking collectives, per_device(): lax.all_to_all(prompt_parts.reshape(devices, rows_here, 2 * kv_width), ('...  24 us
    all_to_all x1, waiting for transfers between devices, per_device(): lax.all_to_all(outgoing, ('resp', 'head'), split_axis=0, concat_axis=0, t...  12 us
    all_to_all x1, starting transfers between devices, per_device(): lax.all_to_all(outgoing, ('resp', 'head'), split_axis=0, concat_axis=0, t...  11.5 us
    unnamed x14, local copies, waits for them, and re-layouts  5.6 us
  transfers between devices with their start and end apart: 1, of which 1 were waited for; matrix products, arithmetic and copies ran while one was open for 7% of the time, Pallas kernels for 0%

profile of v13, /device:TPU:1, one launch (start us, length us, event | category | flops | bytes accessed | tf_op | source)
XLA Modules:
  0.0 95.2 jit_solution(15241585211634714523)
XLA Ops:
  0.6 0.7 maximum_bitcast_fusion
  1.4 1.1 %broadcast_in_dim.2 = bf16[32,4,8,512]{3,2,1,0:T(8,128)(2,1)} broadcast(bf16[4,8,512]{2,1,0:T(8,128)(2,1)S(1)} %maximum_bitcast_fusion), dimensions={1,2,3} | broadcast | bytes 1081344 | tf_op jit(solution)/shard_map/broadcast_in_dim | solution.py:166
  2.5 0.0 copy-start.4
  2.5 0.0 copy-start.2
  2.5 0.0 copy-start.3
  2.5 0.0 copy-start.1
  2.5 11.5 %all-to-all-start = ((bf16[128,8,512]{2,1,0:T(8,128)(2,1)}), bf16[128,8,512]{2,1,0:T(8,128)(2,1)S(1)}, u32[]{:S(2)}, u32[]{:S(2)}) async-start(bf16[128,8,512]{2,1,0:T(8,128)(2,1)} %bitcast.9), calls=%async_computation | async-start | bytes 2097152 | tf_op jit(solution)/shard_map/all_to_all | solution.py:169
  14.6 0.0 copy-done.4
  14.6 0.8 copy.34.keep_col_ref
  15.5 0.0 copy-done.2
  15.5 0.8 copy.28
  16.3 0.0 copy-done.3
  16.3 0.8 copy.29
  17.2 0.0 copy-done.1
  17.2 1.5 %copy.25 = bf16[1,512,1280]{1,2,0:T(8,128)(2,1)} copy(bf16[1,512,1280]{2,1,0:T(8,128)(2,1)S(1)} %copy-done.1) | data formatting | bytes 2621440 | tf_op args[0]
  18.6 2.4 %copy.26 = bf16[1,512,1280]{1,2,0:T(8,128)(2,1)} copy(bf16[1,512,1280]{2,1,0:T(8,128)(2,1)} %param.15) | data formatting | bytes 2621440 | tf_op args[7]
  21.1 12.0 %all-to-all-done = bf16[128,8,512]{2,1,0:T(8,128)(2,1)S(1)} async-done(((bf16[128,8,512]{2,1,0:T(8,128)(2,1)}), bf16[128,8,512]{2,1,0:T(8,128)(2,1)S(1)}, u32[]{:S(2)}, u32[]{:S(2)}) %all-to-all-start) | async-done | bytes 1048608 | tf_op jit(solution)/shard_map/all_to_all | solution.py:169
  33.1 0.0 copy-start
  33.1 1.3 %copy.27 = bf16[1024,512]{0,1:T(8,128)(2,1)} copy(bf16[1024,512]{1,0:T(8,128)(2,1)S(1)} %bitcast.36) | data formatting | bytes 2097152 | tf_op jit(solution)/shard_map/reshape | solution.py:170
  34.4 0.0 copy-done
  34.4 36.0 %shard_map.127 = (bf16[512,1280]{1,0:T(8,128)(2,1)}, bf16[512,1280]{1,0:T(8,128)(2,1)}, bf16[512,256]{1,0:T(8,128)(2,1)}, bf16[512,256]{1,0:T(8,128)(2,1)}, bf16[1024,512]{1,0:T(8,128)(2,1)}) custom-call(s32[1]{0:T(128)S(6)} %copy.39.length_ref, bf16[512,1280]{1,0:T(8,128)(2,1)} %bitcast.41, bf16[1280,512]{1,0:T(8,128)(2,1)} %bitcast.43, ...), custom_call_target="tpu_custom_call" | custom-call | tf_op jit(solution)/shard_map/pallas_call | solution.py:93
  70.4 24.0 %all_to_all.10 = bf16[128,8,512]{2,1,0:T(8,128)(2,1)S(1)} all-to-all(bf16[128,8,512]{2,1,0:T(8,128)(2,1)} %bitcast.50), channel_id=1, replica_groups=mesh['resp'=32,'head'=4] {'resp','head'}, dimensions={0} | all-to-all | bytes 2097152 | tf_op jit(solution)/shard_map/all_to_all | solution.py:183
  94.4 0.2 convert_reduce_fusion
  94.6 0.6 fusion
Async XLA Ops:
  2.5 12.2 %copy-start.4 = (s32[1,512]{1,0:T(1,128)S(1)}, s32[1,512]{1,0:T(1,128)}, u32[]{:S(2)}) copy-start(s32[1,512]{1,0:T(1,128)} %keep_row_ref.1) | copy-start | bytes 6148
  2.5 13.0 %copy-start.2 = (bf16[1,512,256]{2,1,0:T(8,128)(2,1)S(1)}, bf16[1,512,256]{2,1,0:T(8,128)(2,1)}, u32[]{:S(2)}) copy-start(bf16[1,512,256]{2,1,0:T(8,128)(2,1)} %param.9) | copy-start | bytes 786436
  2.5 13.9 %copy-start.3 = (bf16[1,512,256]{2,1,0:T(8,128)(2,1)S(1)}, bf16[1,512,256]{2,1,0:T(8,128)(2,1)}, u32[]{:S(2)}) copy-start(bf16[1,512,256]{2,1,0:T(8,128)(2,1)} %param.10) | copy-start | bytes 786436
  2.5 14.7 %copy-start.1 = (bf16[1,512,1280]{2,1,0:T(8,128)(2,1)S(1)}, bf16[1,512,1280]{2,1,0:T(8,128)(2,1)}, u32[]{:S(2)}) copy-start(bf16[1,512,1280]{2,1,0:T(8,128)(2,1)} %param.8) | copy-start | bytes 3932164
  2.5 30.6 %all-to-all-start = ((bf16[128,8,512]{2,1,0:T(8,128)(2,1)}), bf16[128,8,512]{2,1,0:T(8,128)(2,1)S(1)}, u32[]{:S(2)}, u32[]{:S(2)}) async-start(bf16[128,8,512]{2,1,0:T(8,128)(2,1)} %bitcast.9), calls=%async_computation | async-start | bytes 2097152 | tf_op jit(solution)/shard_map/all_to_all | solution.py:169
  33.1 1.3 %copy-start = (bf16[128,8,512]{2,1,0:T(8,128)(2,1)}, bf16[128,8,512]{2,1,0:T(8,128)(2,1)S(1)}, u32[]{:S(2)}) copy-start(bf16[128,8,512]{2,1,0:T(8,128)(2,1)S(1)} %all-to-all-done) | copy-start | bytes 3145732

commit v14 on v13

--- a/solution.py
+++ b/solution.py
@@ -25,7 +25,9 @@
     group_size = q_ref.shape[1] // width
     j = lax.broadcasted_iota(jnp.int32, (steps, 1), 0)
     t = lax.broadcasted_iota(jnp.int32, (1, steps), 1)
-    allowed = (j <= t) & (j < length)
+    half = steps // 2
+    allowed1 = (j[:half] <= t[:, :half]) & (j[:half] < length)
+    allowed2 = (j <= t[:, half:]) & (j < length)
     live = t < length
     live_col = j < length
     factor_col = (keep_col_ref[...] * live_col.astype(jnp.int32)).astype(bf16)
@@ -43,18 +45,35 @@
         vp = vp_ref[...]
         vo = vo_ref[...]
         sp = jnp.dot(kp, qt, preferred_element_type=f32) * scale
-        so = jnp.dot(ko, qt, preferred_element_type=f32) * scale
-        so = jnp.where(allowed, so, -jnp.inf)
-        top = jnp.maximum(sp.max(0, keepdims=True), so.max(0, keepdims=True))
+        so1 = jnp.dot(ko[:half], qt[:, :half], preferred_element_type=f32) * scale
+        so2 = jnp.dot(ko, qt[:, half:], preferred_element_type=f32) * scale
+        so1 = jnp.where(allowed1, so1, -jnp.inf)
+        so2 = jnp.where(allowed2, so2, -jnp.inf)
+        top = jnp.maximum(
+            sp.max(0, keepdims=True),
+            jnp.concatenate([so1.max(0, keepdims=True), so2.max(0, keepdims=True)], 1),
+        )
         ep = jnp.exp(sp - top)
-        eo = jnp.exp(so - top)
-        inverse = 1.0 / (ep.sum(0, keepdims=True) + eo.sum(0, keepdims=True))
+        eo1 = jnp.exp(so1 - top[:, :half])
+        eo2 = jnp.exp(so2 - top[:, half:])
+        inverse = 1.0 / (
+            ep.sum(0, keepdims=True)
+            + jnp.concatenate([eo1.sum(0, keepdims=True), eo2.sum(0, keepdims=True)], 1)
+        )
         pp = ep * inverse
-        po = eo * inverse
+        po1 = eo1 * inverse[:, :half]
+        po2 = eo2 * inverse[:, half:]
         wp = pp.astype(bf16)
-        wo = po.astype(bf16)
-        out = jnp.dot(vpt_ref[...], wp, preferred_element_type=f32) + jnp.dot(
-            vot_ref[...], wo, preferred_element_type=f32
+        wo1 = po1.astype(bf16)
+        wo2 = po2.astype(bf16)
+        vot = vot_ref[...]
+        kot = kot_ref[...]
+        out = jnp.dot(vpt_ref[...], wp, preferred_element_type=f32) + jnp.concatenate(
+            [
+                jnp.dot(vot[:, :half], wo1, preferred_element_type=f32),
+                jnp.dot(vot, wo2, preferred_element_type=f32),
+            ],
+            1,
         )
         att = jnp.where(live, out, 0.0).astype(bf16).astype(f32)
         att_ref[:, cols] = att.T.astype(bf16)
@@ -62,17 +81,25 @@
         dot = dot_ref[cols, :] * factor_row
         delta = (dot.astype(f32) * att).sum(0, keepdims=True)
         dpp = jnp.dot(vp, dot, preferred_element_type=f32)
-        dpo = jnp.dot(vo, dot, preferred_element_type=f32)
+        dpo1 = jnp.dot(vo[:half], dot[:, :half], preferred_element_type=f32)
+        dpo2 = jnp.dot(vo, dot[:, half:], preferred_element_type=f32)
         dsp = (pp * (dpp - delta)).astype(bf16)
-        dso = (po * (dpo - delta)).astype(bf16)
-        dq = jnp.dot(kpt_ref[...], dsp, preferred_element_type=f32) + jnp.dot(
-            kot_ref[...], dso, preferred_element_type=f32
+        dso1 = (po1 * (dpo1 - delta[:, :half])).astype(bf16)
+        dso2 = (po2 * (dpo2 - delta[:, half:])).astype(bf16)
+        dq = jnp.dot(kpt_ref[...], dsp, preferred_element_type=f32) + jnp.concatenate(
+            [
+                jnp.dot(kot[:, :half], dso1, preferred_element_type=f32),
+                jnp.dot(kot, dso2, preferred_element_type=f32),
+            ],
+            1,
         )
         dq_ref[:, cols] = (dq * scale).T.astype(bf16)
         pg_ref[:, :width] += jnp.dot(dsp, q, preferred_element_type=f32) * scale
         pg_ref[:, width:] += jnp.dot(wp, do, preferred_element_type=f32)
-        dko_acc[...] += jnp.dot(dso, q, preferred_element_type=f32) * scale
-        dvo_acc[...] += jnp.dot(wo, do, preferred_element_type=f32)
+        dko_acc[:half, :] += jnp.dot(dso1, q[:half], preferred_element_type=f32) * scale
+        dko_acc[...] += jnp.dot(dso2, q[half:], preferred_element_type=f32) * scale
+        dvo_acc[:half, :] += jnp.dot(wo1, do[:half], preferred_element_type=f32)
+        dvo_acc[...] += jnp.dot(wo2, do[half:], preferred_element_type=f32)
         return carry
 
     lax.fori_loop(0, group_size, head, 0)

time: 95.7 us -> 94.6 us (0.989)
  Pallas kernels: 36 us -> 34.9 us
    pallas_call x1, Pallas kernels: 36 us -> 34.9 us  [attend(): pl.pallas_call(attention_kernel, out_shape=(jax.ShapeDtypeStruct((steps,...]
where the time goes in v14:
time: 94.6 us; the launch traced here: 94.2 us
  Pallas kernels  34.9 us (37%)
  blocking collectives  24 us (25%)
  waiting for transfers between devices  12 us (13%)
  starting transfers between devices  11.5 us (12%)
  local copies, waits for them, and re-layouts  9.5 us (10%)
  between operations  1.31 us (1%)
    pallas_call x1, Pallas kernels, attend(): pl.pallas_call(attention_kernel, out_shape=(jax.ShapeDtypeStruct((steps,...  34.9 us
    all_to_all x1, blocking collectives, per_device(): lax.all_to_all(prompt_parts.reshape(devices, rows_here, 2 * kv_width), ('...  24 us
    all_to_all x1, waiting for transfers between devices, per_device(): lax.all_to_all(outgoing, ('resp', 'head'), split_axis=0, concat_axis=0, t...  12 us
    all_to_all x1, starting transfers between devices, per_device(): lax.all_to_all(outgoing, ('resp', 'head'), split_axis=0, concat_axis=0, t...  11.5 us
    unnamed x14, local copies, waits for them, and re-layouts  5.6 us
  transfers between devices with their start and end apart: 1, of which 1 were waited for; matrix products, arithmetic and copies ran while one was open for 7% of the time, Pallas kernels for 0%

profile of v14, /device:TPU:1, one launch (start us, length us, event | category | flops | bytes accessed | tf_op | source)
XLA Modules:
  0.0 94.2 jit_solution(271705695572228216)
XLA Ops:
  0.6 0.7 maximum_bitcast_fusion
  1.4 1.1 %broadcast_in_dim.2 = bf16[32,4,8,512]{3,2,1,0:T(8,128)(2,1)} broadcast(bf16[4,8,512]{2,1,0:T(8,128)(2,1)S(1)} %maximum_bitcast_fusion), dimensions={1,2,3} | broadcast | bytes 1081344 | tf_op jit(solution)/shard_map/broadcast_in_dim | solution.py:193
  2.5 0.0 copy-start.4
  2.5 0.0 copy-start.2
  2.5 0.0 copy-start.3
  2.5 0.0 copy-start.1
  2.5 11.5 %all-to-all-start = ((bf16[128,8,512]{2,1,0:T(8,128)(2,1)}), bf16[128,8,512]{2,1,0:T(8,128)(2,1)S(1)}, u32[]{:S(2)}, u32[]{:S(2)}) async-start(bf16[128,8,512]{2,1,0:T(8,128)(2,1)} %bitcast.9), calls=%async_computation | async-start | bytes 2097152 | tf_op jit(solution)/shard_map/all_to_all | solution.py:196
  14.6 0.0 copy-done.4
  14.6 0.8 copy.34.keep_col_ref
  15.5 0.0 copy-done.2
  15.5 0.8 copy.28
  16.3 0.0 copy-done.3
  16.3 0.8 copy.29
  17.2 0.0 copy-done.1
  17.2 1.5 %copy.25 = bf16[1,512,1280]{1,2,0:T(8,128)(2,1)} copy(bf16[1,512,1280]{2,1,0:T(8,128)(2,1)S(1)} %copy-done.1) | data formatting | bytes 2621440 | tf_op args[0]
  18.6 2.4 %copy.26 = bf16[1,512,1280]{1,2,0:T(8,128)(2,1)} copy(bf16[1,512,1280]{2,1,0:T(8,128)(2,1)} %param.15) | data formatting | bytes 2621440 | tf_op args[7]
  21.1 12.0 %all-to-all-done = bf16[128,8,512]{2,1,0:T(8,128)(2,1)S(1)} async-done(((bf16[128,8,512]{2,1,0:T(8,128)(2,1)}), bf16[128,8,512]{2,1,0:T(8,128)(2,1)S(1)}, u32[]{:S(2)}, u32[]{:S(2)}) %all-to-all-start) | async-done | bytes 1048608 | tf_op jit(solution)/shard_map/all_to_all | solution.py:196
  33.1 0.0 copy-start
  33.1 1.3 %copy.27 = bf16[1024,512]{0,1:T(8,128)(2,1)} copy(bf16[1024,512]{1,0:T(8,128)(2,1)S(1)} %bitcast.36) | data formatting | bytes 2097152 | tf_op jit(solution)/shard_map/reshape | solution.py:197
  34.4 0.0 copy-done
  34.4 34.9 %shard_map.127 = (bf16[512,1280]{1,0:T(8,128)(2,1)}, bf16[512,1280]{1,0:T(8,128)(2,1)}, bf16[512,256]{1,0:T(8,128)(2,1)}, bf16[512,256]{1,0:T(8,128)(2,1)}, bf16[1024,512]{1,0:T(8,128)(2,1)}) custom-call(s32[1]{0:T(128)S(6)} %copy.39.length_ref, bf16[512,1280]{1,0:T(8,128)(2,1)} %bitcast.41, bf16[1280,512]{1,0:T(8,128)(2,1)} %bitcast.43, ...), custom_call_target="tpu_custom_call" | custom-call | tf_op jit(solution)/shard_map/pallas_call | solution.py:120
  69.3 24.0 %all_to_all.10 = bf16[128,8,512]{2,1,0:T(8,128)(2,1)S(1)} all-to-all(bf16[128,8,512]{2,1,0:T(8,128)(2,1)} %bitcast.50), channel_id=1, replica_groups=mesh['resp'=32,'head'=4] {'resp','head'}, dimensions={0} | all-to-all | bytes 2097152 | tf_op jit(solution)/shard_map/all_to_all | solution.py:210
  93.4 0.2 convert_reduce_fusion
  93.5 0.6 fusion
Async XLA Ops:
  2.5 12.2 %copy-start.4 = (s32[1,512]{1,0:T(1,128)S(1)}, s32[1,512]{1,0:T(1,128)}, u32[]{:S(2)}) copy-start(s32[1,512]{1,0:T(1,128)} %keep_row_ref.1) | copy-start | bytes 6148
  2.5 13.0 %copy-start.2 = (bf16[1,512,256]{2,1,0:T(8,128)(2,1)S(1)}, bf16[1,512,256]{2,1,0:T(8,128)(2,1)}, u32[]{:S(2)}) copy-start(bf16[1,512,256]{2,1,0:T(8,128)(2,1)} %param.9) | copy-start | bytes 786436
  2.5 13.9 %copy-start.3 = (bf16[1,512,256]{2,1,0:T(8,128)(2,1)S(1)}, bf16[1,512,256]{2,1,0:T(8,128)(2,1)}, u32[]{:S(2)}) copy-start(bf16[1,512,256]{2,1,0:T(8,128)(2,1)} %param.10) | copy-start | bytes 786436
  2.5 14.7 %copy-start.1 = (bf16[1,512,1280]{2,1,0:T(8,128)(2,1)S(1)}, bf16[1,512,1280]{2,1,0:T(8,128)(2,1)}, u32[]{:S(2)}) copy-start(bf16[1,512,1280]{2,1,0:T(8,128)(2,1)} %param.8) | copy-start | bytes 3932164
  2.5 30.6 %all-to-all-start = ((bf16[128,8,512]{2,1,0:T(8,128)(2,1)}), bf16[128,8,512]{2,1,0:T(8,128)(2,1)S(1)}, u32[]{:S(2)}, u32[]{:S(2)}) async-start(bf16[128,8,512]{2,1,0:T(8,128)(2,1)} %bitcast.9), calls=%async_computation | async-start | bytes 2097152 | tf_op jit(solution)/shard_map/all_to_all | solution.py:196
  33.1 1.3 %copy-start = (bf16[128,8,512]{2,1,0:T(8,128)(2,1)}, bf16[128,8,512]{2,1,0:T(8,128)(2,1)S(1)}, u32[]{:S(2)}) copy-start(bf16[128,8,512]{2,1,0:T(8,128)(2,1)S(1)} %all-to-all-done) | copy-start | bytes 3145732

commit v15 on v14

--- a/solution.py
+++ b/solution.py
@@ -13,9 +13,9 @@
 
 
 def attention_kernel(
-    length_ref, q_ref, qt_ref, do_ref, dot_ref, kp_ref, kpt_ref, vp_ref, vpt_ref,
+    length_ref, q_ref, qt_ref, do_ref, dot_ref, kp_ref, vp_ref,
     ko_ref, kot_ref, vo_ref, vot_ref, keep_col_ref, keep_row_ref,
-    att_ref, dq_ref, dko_ref, dvo_ref, pg_out, dko_acc, dvo_acc, pg_ref,
+    att_ref, dq_ref, dko_ref, dvo_ref, pg_out, dko_acc, dvo_acc, pg_ref, kpt_ref, vpt_ref,
 ):
     f32, bf16 = jnp.float32, jnp.bfloat16
     scale = HEAD_DIM ** (-0.5)
@@ -32,6 +32,8 @@
     live_col = j < length
     factor_col = (keep_col_ref[...] * live_col.astype(jnp.int32)).astype(bf16)
     factor_row = (keep_row_ref[...] * live.astype(jnp.int32)).astype(bf16)
+    kpt_ref[...] = kp_ref[...].astype(f32).T.astype(bf16)
+    vpt_ref[...] = vp_ref[...].astype(f32).T.astype(bf16)
     dko_acc[...] = jnp.zeros_like(dko_acc)
     dvo_acc[...] = jnp.zeros_like(dvo_acc)
     pg_ref[...] = jnp.zeros_like(pg_ref)
@@ -135,9 +137,7 @@
                 pl.BlockSpec((steps, heads), kv_block),
                 pl.BlockSpec((heads, steps), kv_block_t),
                 pl.BlockSpec((prompt_rows, HEAD_DIM), kv_block),
-                pl.BlockSpec((HEAD_DIM, prompt_rows), kv_block_t),
                 pl.BlockSpec((prompt_rows, HEAD_DIM), lambda k, n: (0, k + kv_count)),
-                pl.BlockSpec((HEAD_DIM, prompt_rows), lambda k, n: (k + kv_count, 0)),
                 pl.BlockSpec((steps, HEAD_DIM), kv_block),
                 pl.BlockSpec((HEAD_DIM, steps), kv_block_t),
                 pl.BlockSpec((steps, HEAD_DIM), kv_block),
@@ -153,7 +153,8 @@
                 pl.BlockSpec((prompt_rows, 2 * HEAD_DIM), kv_block),
             ],
             scratch_shapes=[pltpu.VMEM((steps, HEAD_DIM), f32)] * 2
-            + [pltpu.VMEM((prompt_rows, 2 * HEAD_DIM), f32)],
+            + [pltpu.VMEM((prompt_rows, 2 * HEAD_DIM), f32)]
+            + [pltpu.VMEM((HEAD_DIM, prompt_rows), bf16)] * 2,
         ),
         compiler_params=pltpu.CompilerParams(
             dimension_semantics=("arbitrary",),
@@ -166,9 +167,7 @@
         out_grad,
         out_grad.T,
         prompt_kv,
-        prompt_kv.T,
         prompt_kv,
-        prompt_kv.T,
         keys,
         keys.T,
         values,

time: 94.6 us -> 94.5 us (level)
    reshape x1 -> x0, local copies, waits for them, and re-layouts: 1.33 us -> none  [per_device(): prompt_kv = gathered.reshape(devices * rows_here, 2 * kv_width)]
    unnamed x14, local copies, waits for them, and re-layouts: 5.6 us -> 6.64 us
where the time goes in v15:
time: 94.5 us; the launch traced here: 94 us
  Pallas kernels  35.1 us (37%)
  blocking collectives  24 us (25%)
  waiting for transfers between devices  11.9 us (13%)
  starting transfers between devices  11.5 us (12%)
  local copies, waits for them, and re-layouts  9.23 us (10%)
  between operations  1.31 us (1%)
    pallas_call x1, Pallas kernels, attend(): pl.pallas_call(attention_kernel, out_shape=(jax.ShapeDtypeStruct((steps,...  35.1 us
    all_to_all x1, blocking collectives, per_device(): lax.all_to_all(prompt_parts.reshape(devices, rows_here, 2 * kv_width), ('...  24 us
    all_to_all x1, waiting for transfers between devices, per_device(): lax.all_to_all(outgoing, ('resp', 'head'), split_axis=0, concat_axis=0, t...  11.9 us
    all_to_all x1, starting transfers between devices, per_device(): lax.all_to_all(outgoing, ('resp', 'head'), split_axis=0, concat_axis=0, t...  11.5 us
    unnamed x14, local copies, waits for them, and re-layouts  6.64 us
  transfers between devices with their start and end apart: 1, of which 1 were waited for; matrix products, arithmetic and copies ran while one was open for 7% of the time, Pallas kernels for 0%

profile of v15, /device:TPU:1, one launch (start us, length us, event | category | flops | bytes accessed | tf_op | source)
XLA Modules:
  0.0 94.0 jit_solution(2730754453201909535)
XLA Ops:
  0.6 0.7 maximum_bitcast_fusion
  1.4 1.1 %broadcast_in_dim.2 = bf16[32,4,8,512]{3,2,1,0:T(8,128)(2,1)} broadcast(bf16[4,8,512]{2,1,0:T(8,128)(2,1)S(1)} %maximum_bitcast_fusion), dimensions={1,2,3} | broadcast | bytes 1081344 | tf_op jit(solution)/shard_map/broadcast_in_dim | solution.py:192
  2.5 0.0 copy-start.4
  2.5 0.0 copy-start.2
  2.5 0.0 copy-start.3
  2.5 0.0 copy-start.1
  2.5 11.5 %all-to-all-start = ((bf16[128,8,512]{2,1,0:T(8,128)(2,1)}), bf16[128,8,512]{2,1,0:T(8,128)(2,1)S(1)}, u32[]{:S(2)}, u32[]{:S(2)}) async-start(bf16[128,8,512]{2,1,0:T(8,128)(2,1)} %bitcast.9), calls=%async_computation | async-start | bytes 2097152 | tf_op jit(solution)/shard_map/all_to_all | solution.py:195
  14.6 0.0 copy-done.4
  14.6 0.9 copy.30.keep_col_ref
  15.5 0.0 copy-done.2
  15.5 0.9 copy.24
  16.4 0.0 copy-done.3
  16.4 0.9 copy.25
  17.2 0.0 copy-done.1
  17.2 1.5 %copy.22 = bf16[1,512,1280]{1,2,0:T(8,128)(2,1)} copy(bf16[1,512,1280]{2,1,0:T(8,128)(2,1)S(1)} %copy-done.1) | data formatting | bytes 2621440 | tf_op args[0]
  18.7 2.4 %copy.23 = bf16[1,512,1280]{1,2,0:T(8,128)(2,1)} copy(bf16[1,512,1280]{2,1,0:T(8,128)(2,1)} %param.15) | data formatting | bytes 2621440 | tf_op args[7]
  21.2 11.9 %all-to-all-done = bf16[128,8,512]{2,1,0:T(8,128)(2,1)S(1)} async-done(((bf16[128,8,512]{2,1,0:T(8,128)(2,1)}), bf16[128,8,512]{2,1,0:T(8,128)(2,1)S(1)}, u32[]{:S(2)}, u32[]{:S(2)}) %all-to-all-start) | async-done | bytes 1048608 | tf_op jit(solution)/shard_map/all_to_all | solution.py:195
  33.1 0.0 copy-start
  33.1 1.0 %copy-done = bf16[128,8,512]{2,1,0:T(8,128)(2,1)} copy-done((bf16[128,8,512]{2,1,0:T(8,128)(2,1)}, bf16[128,8,512]{2,1,0:T(8,128)(2,1)S(1)}, u32[]{:S(2)}) %copy-start) | copy-done | bytes 1048600
  34.0 35.1 %shard_map.127 = (bf16[512,1280]{1,0:T(8,128)(2,1)}, bf16[512,1280]{1,0:T(8,128)(2,1)}, bf16[512,256]{1,0:T(8,128)(2,1)}, bf16[512,256]{1,0:T(8,128)(2,1)}, bf16[1024,512]{1,0:T(8,128)(2,1)}) custom-call(s32[1]{0:T(128)S(6)} %copy.35.length_ref, bf16[512,1280]{1,0:T(8,128)(2,1)} %bitcast.37, bf16[1280,512]{1,0:T(8,128)(2,1)} %bitcast.39, ...), custom_call_target="tpu_custom_call" | custom-call | tf_op jit(solution)/shard_map/pallas_call | solution.py:122
  69.2 24.0 %all_to_all.10 = bf16[128,8,512]{2,1,0:T(8,128)(2,1)S(1)} all-to-all(bf16[128,8,512]{2,1,0:T(8,128)(2,1)} %bitcast.46), channel_id=1, replica_groups=mesh['resp'=32,'head'=4] {'resp','head'}, dimensions={0} | all-to-all | bytes 2097152 | tf_op jit(solution)/shard_map/all_to_all | solution.py:209
  93.2 0.2 convert_reduce_fusion
  93.4 0.6 fusion
Async XLA Ops:
  2.5 12.2 %copy-start.4 = (s32[1,512]{1,0:T(1,128)S(1)}, s32[1,512]{1,0:T(1,128)}, u32[]{:S(2)}) copy-start(s32[1,512]{1,0:T(1,128)} %keep_row_ref.1) | copy-start | bytes 6148
  2.5 13.0 %copy-start.2 = (bf16[1,512,256]{2,1,0:T(8,128)(2,1)S(1)}, bf16[1,512,256]{2,1,0:T(8,128)(2,1)}, u32[]{:S(2)}) copy-start(bf16[1,512,256]{2,1,0:T(8,128)(2,1)} %param.9) | copy-start | bytes 786436
  2.5 13.9 %copy-start.3 = (bf16[1,512,256]{2,1,0:T(8,128)(2,1)S(1)}, bf16[1,512,256]{2,1,0:T(8,128)(2,1)}, u32[]{:S(2)}) copy-start(bf16[1,512,256]{2,1,0:T(8,128)(2,1)} %param.10) | copy-start | bytes 786436
  2.5 14.8 %copy-start.1 = (bf16[1,512,1280]{2,1,0:T(8,128)(2,1)S(1)}, bf16[1,512,1280]{2,1,0:T(8,128)(2,1)}, u32[]{:S(2)}) copy-start(bf16[1,512,1280]{2,1,0:T(8,128)(2,1)} %param.8) | copy-start | bytes 3932164
  2.5 30.6 %all-to-all-start = ((bf16[128,8,512]{2,1,0:T(8,128)(2,1)}), bf16[128,8,512]{2,1,0:T(8,128)(2,1)S(1)}, u32[]{:S(2)}, u32[]{:S(2)}) async-start(bf16[128,8,512]{2,1,0:T(8,128)(2,1)} %bitcast.9), calls=%async_computation | async-start | bytes 2097152 | tf_op jit(solution)/shard_map/all_to_all | solution.py:195
  33.1 1.0 %copy-start = (bf16[128,8,512]{2,1,0:T(8,128)(2,1)}, bf16[128,8,512]{2,1,0:T(8,128)(2,1)S(1)}, u32[]{:S(2)}) copy-start(bf16[128,8,512]{2,1,0:T(8,128)(2,1)S(1)} %all-to-all-done) | copy-start | bytes 3145732

commit v16 on v14

--- a/solution.py
+++ b/solution.py
@@ -68,32 +68,32 @@
         wo2 = po2.astype(bf16)
         vot = vot_ref[...]
         kot = kot_ref[...]
-        out = jnp.dot(vpt_ref[...], wp, preferred_element_type=f32) + jnp.concatenate(
+        out = lax.dot_general(wp, vp, TN, preferred_element_type=f32) + jnp.concatenate(
             [
-                jnp.dot(vot[:, :half], wo1, preferred_element_type=f32),
-                jnp.dot(vot, wo2, preferred_element_type=f32),
-            ],
-            1,
-        )
-        att = jnp.where(live, out, 0.0).astype(bf16).astype(f32)
-        att_ref[:, cols] = att.T.astype(bf16)
+                lax.dot_general(wo1, vo[:half], TN, preferred_element_type=f32),
+                lax.dot_general(wo2, vo, TN, preferred_element_type=f32),
+            ],
+            0,
+        )
+        att = jnp.where(live_col, out, 0.0).astype(bf16)
+        att_ref[:, cols] = att
         do = do_ref[:, cols] * factor_col
         dot = dot_ref[cols, :] * factor_row
-        delta = (dot.astype(f32) * att).sum(0, keepdims=True)
+        delta = (dot.astype(f32) * att.astype(f32).T).sum(0, keepdims=True)
         dpp = jnp.dot(vp, dot, preferred_element_type=f32)
         dpo1 = jnp.dot(vo[:half], dot[:, :half], preferred_element_type=f32)
         dpo2 = jnp.dot(vo, dot[:, half:], preferred_element_type=f32)
         dsp = (pp * (dpp - delta)).astype(bf16)
         dso1 = (po1 * (dpo1 - delta[:, :half])).astype(bf16)
         dso2 = (po2 * (dpo2 - delta[:, half:])).astype(bf16)
-        dq = jnp.dot(kpt_ref[...], dsp, preferred_element_type=f32) + jnp.concatenate(
+        dq = lax.dot_general(dsp, kp, TN, preferred_element_type=f32) + jnp.concatenate(
             [
-                jnp.dot(kot[:, :half], dso1, preferred_element_type=f32),
-                jnp.dot(kot, dso2, preferred_element_type=f32),
-            ],
-            1,
-        )
-        dq_ref[:, cols] = (dq * scale).T.astype(bf16)
+                lax.dot_general(dso1, ko[:half], TN, preferred_element_type=f32),
+                lax.dot_general(dso2, ko, TN, preferred_element_type=f32),
+            ],
+            0,
+        )
+        dq_ref[:, cols] = (dq * scale).astype(bf16)
         pg_ref[:, :width] += jnp.dot(dsp, q, preferred_element_type=f32) * scale
         pg_ref[:, width:] += jnp.dot(wp, do, preferred_element_type=f32)
         dko_acc[:half, :] += jnp.dot(dso1, q[:half], preferred_element_type=f32) * scale

time: 94.6 us -> 101 us (1.068)
  Pallas kernels: 34.9 us -> 41.5 us
    pallas_call x1, Pallas kernels: 34.9 us -> 41.5 us  [attend(): pl.pallas_call(attention_kernel, out_shape=(jax.ShapeDtypeStruct((steps,...]
  transfers between devices with their start and end apart: 1 -> 1, of which waited for: 1 -> 1; matrix products, arithmetic and copies ran while one was open for 7% -> 6% of each run, Pallas kernels for 0% -> 0%
where the time goes in v16:
time: 101 us
  Pallas kernels  41.5 us (41%)
  blocking collectives  24.1 us (24%)
  waiting for transfers between devices  12 us (12%)
  starting transfers between devices  11.5 us (11%)
  local copies, waits for them, and re-layouts  9.5 us (9%)
  between operations  1.31 us (1%)
    pallas_call x1, Pallas kernels, attend(): pl.pallas_call(attention_kernel, out_shape=(jax.ShapeDtypeStruct((steps,...  41.5 us
    all_to_all x1, blocking collectives, per_device(): lax.all_to_all(prompt_parts.reshape(devices, rows_here, 2 * kv_width), ('...  24.1 us
    all_to_all x1, waiting for transfers between devices, per_device(): lax.all_to_all(outgoing, ('resp', 'head'), split_axis=0, concat_axis=0, t...  12 us
    all_to_all x1, starting transfers between devices, per_device(): lax.all_to_all(outgoing, ('resp', 'head'), split_axis=0, concat_axis=0, t...  11.5 us
    unnamed x14, local copies, waits for them, and re-layouts  5.6 us
  transfers between devices with their start and end apart: 1, of which 1 were waited for; matrix products, arithmetic and copies ran while one was open for 6% of the time, Pallas kernels for 0%

profile of v16, /device:TPU:1, one launch (start us, length us, event | category | flops | bytes accessed | tf_op | source)
XLA Modules:
  0.0 100.7 jit_solution(13062500480254075197)
XLA Ops:
  0.6 0.7 maximum_bitcast_fusion
  1.4 1.1 %broadcast_in_dim.2 = bf16[32,4,8,512]{3,2,1,0:T(8,128)(2,1)} broadcast(bf16[4,8,512]{2,1,0:T(8,128)(2,1)S(1)} %maximum_bitcast_fusion), dimensions={1,2,3} | broadcast | bytes 1081344 | tf_op jit(solution)/shard_map/broadcast_in_dim | solution.py:193
  2.5 0.0 copy-start.4
  2.5 0.0 copy-start.2
  2.5 0.0 copy-start.3
  2.5 0.0 copy-start.1
  2.5 11.5 %all-to-all-start = ((bf16[128,8,512]{2,1,0:T(8,128)(2,1)}), bf16[128,8,512]{2,1,0:T(8,128)(2,1)S(1)}, u32[]{:S(2)}, u32[]{:S(2)}) async-start(bf16[128,8,512]{2,1,0:T(8,128)(2,1)} %bitcast.9), calls=%async_computation | async-start | bytes 2097152 | tf_op jit(solution)/shard_map/all_to_all | solution.py:196
  14.6 0.0 copy-done.4
  14.6 0.8 copy.34.keep_col_ref
  15.5 0.0 copy-done.2
  15.5 0.8 copy.28
  16.3 0.0 copy-done.3
  16.3 0.8 copy.29
  17.2 0.0 copy-done.1
  17.2 1.5 %copy.25 = bf16[1,512,1280]{1,2,0:T(8,128)(2,1)} copy(bf16[1,512,1280]{2,1,0:T(8,128)(2,1)S(1)} %copy-done.1) | data formatting | bytes 2621440 | tf_op args[0]
  18.6 2.4 %copy.26 = bf16[1,512,1280]{1,2,0:T(8,128)(2,1)} copy(bf16[1,512,1280]{2,1,0:T(8,128)(2,1)} %param.15) | data formatting | bytes 2621440 | tf_op args[7]
  21.1 12.0 %all-to-all-done = bf16[128,8,512]{2,1,0:T(8,128)(2,1)S(1)} async-done(((bf16[128,8,512]{2,1,0:T(8,128)(2,1)}), bf16[128,8,512]{2,1,0:T(8,128)(2,1)S(1)}, u32[]{:S(2)}, u32[]{:S(2)}) %all-to-all-start) | async-done | bytes 1048608 | tf_op jit(solution)/shard_map/all_to_all | solution.py:196
  33.1 0.0 copy-start
  33.1 1.3 %copy.27 = bf16[1024,512]{0,1:T(8,128)(2,1)} copy(bf16[1024,512]{1,0:T(8,128)(2,1)S(1)} %bitcast.36) | data formatting | bytes 2097152 | tf_op jit(solution)/shard_map/reshape | solution.py:197
  34.4 0.0 copy-done
  34.4 41.5 %shard_map.127 = (bf16[512,1280]{1,0:T(8,128)(2,1)}, bf16[512,1280]{1,0:T(8,128)(2,1)}, bf16[512,256]{1,0:T(8,128)(2,1)}, bf16[512,256]{1,0:T(8,128)(2,1)}, bf16[1024,512]{1,0:T(8,128)(2,1)}) custom-call(s32[1]{0:T(128)S(6)} %copy.39.length_ref, bf16[512,1280]{1,0:T(8,128)(2,1)} %bitcast.41, bf16[1280,512]{1,0:T(8,128)(2,1)} %bitcast.43, ...), custom_call_target="tpu_custom_call" | custom-call | tf_op jit(solution)/shard_map/pallas_call | solution.py:120
  75.9 24.1 %all_to_all.10 = bf16[128,8,512]{2,1,0:T(8,128)(2,1)S(1)} all-to-all(bf16[128,8,512]{2,1,0:T(8,128)(2,1)} %bitcast.50), channel_id=1, replica_groups=mesh['resp'=32,'head'=4] {'resp','head'}, dimensions={0} | all-to-all | bytes 2097152 | tf_op jit(solution)/shard_map/all_to_all | solution.py:210
  100.0 0.2 convert_reduce_fusion
  100.1 0.6 fusion
Async XLA Ops:
  2.5 12.2 %copy-start.4 = (s32[1,512]{1,0:T(1,128)S(1)}, s32[1,512]{1,0:T(1,128)}, u32[]{:S(2)}) copy-start(s32[1,512]{1,0:T(1,128)} %keep_row_ref.1) | copy-start | bytes 6148
  2.5 13.0 %copy-start.2 = (bf16[1,512,256]{2,1,0:T(8,128)(2,1)S(1)}, bf16[1,512,256]{2,1,0:T(8,128)(2,1)}, u32[]{:S(2)}) copy-start(bf16[1,512,256]{2,1,0:T(8,128)(2,1)} %param.9) | copy-start | bytes 786436
  2.5 13.9 %copy-start.3 = (bf16[1,512,256]{2,1,0:T(8,128)(2,1)S(1)}, bf16[1,512,256]{2,1,0:T(8,128)(2,1)}, u32[]{:S(2)}) copy-start(bf16[1,512,256]{2,1,0:T(8,128)(2,1)} %param.10) | copy-start | bytes 786436
  2.5 14.7 %copy-start.1 = (bf16[1,512,1280]{2,1,0:T(8,128)(2,1)S(1)}, bf16[1,512,1280]{2,1,0:T(8,128)(2,1)}, u32[]{:S(2)}) copy-start(bf16[1,512,1280]{2,1,0:T(8,128)(2,1)} %param.8) | copy-start | bytes 3932164
  2.5 30.6 %all-to-all-start = ((bf16[128,8,512]{2,1,0:T(8,128)(2,1)}), bf16[128,8,512]{2,1,0:T(8,128)(2,1)S(1)}, u32[]{:S(2)}, u32[]{:S(2)}) async-start(bf16[128,8,512]{2,1,0:T(8,128)(2,1)} %bitcast.9), calls=%async_computation | async-start | bytes 2097152 | tf_op jit(solution)/shard_map/all_to_all | solution.py:196
  33.1 1.3 %copy-start = (bf16[128,8,512]{2,1,0:T(8,128)(2,1)}, bf16[128,8,512]{2,1,0:T(8,128)(2,1)S(1)}, u32[]{:S(2)}) copy-start(bf16[128,8,512]{2,1,0:T(8,128)(2,1)S(1)} %all-to-all-done) | copy-start | bytes 3145732

commit v17 on v14

--- a/solution.py
+++ b/solution.py
@@ -15,7 +15,7 @@
 def attention_kernel(
     length_ref, q_ref, qt_ref, do_ref, dot_ref, kp_ref, kpt_ref, vp_ref, vpt_ref,
     ko_ref, kot_ref, vo_ref, vot_ref, keep_col_ref, keep_row_ref,
-    att_ref, dq_ref, dko_ref, dvo_ref, pg_out, dko_acc, dvo_acc, pg_ref,
+    att_ref, dq_ref, dko_ref, dvo_ref, pg_out, dko_acc, dvo_acc, pg_ref, e_scr, dp_scr, w_scr, ds_scr,
 ):
     f32, bf16 = jnp.float32, jnp.bfloat16
     scale = HEAD_DIM ** (-0.5)
@@ -26,6 +26,8 @@
     j = lax.broadcasted_iota(jnp.int32, (steps, 1), 0)
     t = lax.broadcasted_iota(jnp.int32, (1, steps), 1)
     half = steps // 2
+    chunk = 64
+    chunks = kp_ref.shape[0] // chunk
     allowed1 = (j[:half] <= t[:, :half]) & (j[:half] < length)
     allowed2 = (j <= t[:, half:]) & (j < length)
     live = t < length
@@ -44,31 +46,43 @@
         ko = ko_ref[...]
         vp = vp_ref[...]
         vo = vo_ref[...]
-        sp = jnp.dot(kp, qt, preferred_element_type=f32) * scale
+        e_scr[...] = jnp.dot(kp, qt, preferred_element_type=f32)
         so1 = jnp.dot(ko[:half], qt[:, :half], preferred_element_type=f32) * scale
         so2 = jnp.dot(ko, qt[:, half:], preferred_element_type=f32) * scale
         so1 = jnp.where(allowed1, so1, -jnp.inf)
         so2 = jnp.where(allowed2, so2, -jnp.inf)
         top = jnp.maximum(
-            sp.max(0, keepdims=True),
+            e_scr[...].max(0, keepdims=True) * scale,
             jnp.concatenate([so1.max(0, keepdims=True), so2.max(0, keepdims=True)], 1),
         )
-        ep = jnp.exp(sp - top)
+
+        def exps(c, total):
+            rows = pl.ds(pl.multiple_of(c * chunk, chunk), chunk)
+            e = jnp.exp(e_scr[rows, :] * scale - top)
+            e_scr[rows, :] = e
+            return total + e.sum(0, keepdims=True)
+
+        prompt_total = lax.fori_loop(0, chunks, exps, jnp.zeros((1, steps), f32))
         eo1 = jnp.exp(so1 - top[:, :half])
         eo2 = jnp.exp(so2 - top[:, half:])
         inverse = 1.0 / (
-            ep.sum(0, keepdims=True)
+            prompt_total
             + jnp.concatenate([eo1.sum(0, keepdims=True), eo2.sum(0, keepdims=True)], 1)
         )
-        pp = ep * inverse
+
+        def weights(c, carry):
+            rows = pl.ds(pl.multiple_of(c * chunk, chunk), chunk)
+            w_scr[rows, :] = (e_scr[rows, :] * inverse).astype(bf16)
+            return carry
+
+        lax.fori_loop(0, chunks, weights, 0)
         po1 = eo1 * inverse[:, :half]
         po2 = eo2 * inverse[:, half:]
-        wp = pp.astype(bf16)
         wo1 = po1.astype(bf16)
         wo2 = po2.astype(bf16)
         vot = vot_ref[...]
         kot = kot_ref[...]
-        out = jnp.dot(vpt_ref[...], wp, preferred_element_type=f32) + jnp.concatenate(
+        out = jnp.dot(vpt_ref[...], w_scr[...], preferred_element_type=f32) + jnp.concatenate(
             [
                 jnp.dot(vot[:, :half], wo1, preferred_element_type=f32),
                 jnp.dot(vot, wo2, preferred_element_type=f32),
@@ -80,13 +94,19 @@
         do = do_ref[:, cols] * factor_col
         dot = dot_ref[cols, :] * factor_row
         delta = (dot.astype(f32) * att).sum(0, keepdims=True)
-        dpp = jnp.dot(vp, dot, preferred_element_type=f32)
+        dp_scr[...] = jnp.dot(vp, dot, preferred_element_type=f32)
         dpo1 = jnp.dot(vo[:half], dot[:, :half], preferred_element_type=f32)
         dpo2 = jnp.dot(vo, dot[:, half:], preferred_element_type=f32)
-        dsp = (pp * (dpp - delta)).astype(bf16)
+
+        def grads(c, carry):
+            rows = pl.ds(pl.multiple_of(c * chunk, chunk), chunk)
+            ds_scr[rows, :] = (e_scr[rows, :] * inverse * (dp_scr[rows, :] - delta)).astype(bf16)
+            return carry
+
+        lax.fori_loop(0, chunks, grads, 0)
         dso1 = (po1 * (dpo1 - delta[:, :half])).astype(bf16)
         dso2 = (po2 * (dpo2 - delta[:, half:])).astype(bf16)
-        dq = jnp.dot(kpt_ref[...], dsp, preferred_element_type=f32) + jnp.concatenate(
+        dq = jnp.dot(kpt_ref[...], ds_scr[...], preferred_element_type=f32) + jnp.concatenate(
             [
                 jnp.dot(kot[:, :half], dso1, preferred_element_type=f32),
                 jnp.dot(kot, dso2, preferred_element_type=f32),
@@ -94,8 +114,8 @@
             1,
         )
         dq_ref[:, cols] = (dq * scale).T.astype(bf16)
-        pg_ref[:, :width] += jnp.dot(dsp, q, preferred_element_type=f32) * scale
-        pg_ref[:, width:] += jnp.dot(wp, do, preferred_element_type=f32)
+        pg_ref[:, :width] += jnp.dot(ds_scr[...], q, preferred_element_type=f32) * scale
+        pg_ref[:, width:] += jnp.dot(w_scr[...], do, preferred_element_type=f32)
         dko_acc[:half, :] += jnp.dot(dso1, q[:half], preferred_element_type=f32) * scale
         dko_acc[...] += jnp.dot(dso2, q[half:], preferred_element_type=f32) * scale
         dvo_acc[:half, :] += jnp.dot(wo1, do[:half], preferred_element_type=f32)
@@ -153,7 +173,9 @@
                 pl.BlockSpec((prompt_rows, 2 * HEAD_DIM), kv_block),
             ],
             scratch_shapes=[pltpu.VMEM((steps, HEAD_DIM), f32)] * 2
-            + [pltpu.VMEM((prompt_rows, 2 * HEAD_DIM), f32)],
+            + [pltpu.VMEM((prompt_rows, 2 * HEAD_DIM), f32)]
+            + [pltpu.VMEM((prompt_rows, steps), f32)] * 2
+            + [pltpu.VMEM((prompt_rows, steps), bf16)] * 2,
         ),
         compiler_params=pltpu.CompilerParams(
             dimension_semantics=("arbitrary",),

time: 94.6 us -> 102 us (1.078)
  Pallas kernels: 34.9 us -> 42.4 us
    pallas_call x1, Pallas kernels: 34.9 us -> 42.4 us  [attend(): pl.pallas_call(attention_kernel, out_shape=(jax.ShapeDtypeStruct((steps,...]
  transfers between devices with their start and end apart: 1 -> 1, of which waited for: 1 -> 1; matrix products, arithmetic and copies ran while one was open for 7% -> 6% of each run, Pallas kernels for 0% -> 0%
where the time goes in v17:
time: 102 us
  Pallas kernels  42.4 us (42%)
  blocking collectives  24 us (24%)
  waiting for transfers between devices  12 us (12%)
  starting transfers between devices  11.5 us (11%)
  local copies, waits for them, and re-layouts  9.5 us (9%)
  between operations  1.31 us (1%)
    pallas_call x1, Pallas kernels, attend(): pl.pallas_call(attention_kernel, out_shape=(jax.ShapeDtypeStruct((steps,...  42.4 us
    all_to_all x1, blocking collectives, per_device(): lax.all_to_all(prompt_parts.reshape(devices, rows_here, 2 * kv_width), ('...  24 us
    all_to_all x1, waiting for transfers between devices, per_device(): lax.all_to_all(outgoing, ('resp', 'head'), split_axis=0, concat_axis=0, t...  12 us
    all_to_all x1, starting transfers between devices, per_device(): lax.all_to_all(outgoing, ('resp', 'head'), split_axis=0, concat_axis=0, t...  11.5 us
    unnamed x14, local copies, waits for them, and re-layouts  5.6 us
  transfers between devices with their start and end apart: 1, of which 1 were waited for; matrix products, arithmetic and copies ran while one was open for 6% of the time, Pallas kernels for 0%

profile of v17, /device:TPU:1, one launch (start us, length us, event | category | flops | bytes accessed | tf_op | source)
XLA Modules:
  0.0 101.6 jit_solution(9650313954321179137)
XLA Ops:
  0.6 0.7 maximum_bitcast_fusion
  1.4 1.1 %broadcast_in_dim.2 = bf16[32,4,8,512]{3,2,1,0:T(8,128)(2,1)} broadcast(bf16[4,8,512]{2,1,0:T(8,128)(2,1)S(1)} %maximum_bitcast_fusion), dimensions={1,2,3} | broadcast | bytes 1081344 | tf_op jit(solution)/shard_map/broadcast_in_dim | solution.py:215
  2.5 0.0 copy-start.4
  2.5 0.0 copy-start.2
  2.5 0.0 copy-start.3
  2.5 0.0 copy-start.1
  2.5 11.5 %all-to-all-start = ((bf16[128,8,512]{2,1,0:T(8,128)(2,1)}), bf16[128,8,512]{2,1,0:T(8,128)(2,1)S(1)}, u32[]{:S(2)}, u32[]{:S(2)}) async-start(bf16[128,8,512]{2,1,0:T(8,128)(2,1)} %bitcast.9), calls=%async_computation | async-start | bytes 2097152 | tf_op jit(solution)/shard_map/all_to_all | solution.py:218
  14.6 0.0 copy-done.4
  14.6 0.8 copy.34.keep_col_ref
  15.5 0.0 copy-done.2
  15.5 0.8 copy.28
  16.3 0.0 copy-done.3
  16.3 0.8 copy.29
  17.2 0.0 copy-done.1
  17.2 1.5 %copy.25 = bf16[1,512,1280]{1,2,0:T(8,128)(2,1)} copy(bf16[1,512,1280]{2,1,0:T(8,128)(2,1)S(1)} %copy-done.1) | data formatting | bytes 2621440 | tf_op args[0]
  18.6 2.4 %copy.26 = bf16[1,512,1280]{1,2,0:T(8,128)(2,1)} copy(bf16[1,512,1280]{2,1,0:T(8,128)(2,1)} %param.15) | data formatting | bytes 2621440 | tf_op args[7]
  21.1 12.0 %all-to-all-done = bf16[128,8,512]{2,1,0:T(8,128)(2,1)S(1)} async-done(((bf16[128,8,512]{2,1,0:T(8,128)(2,1)}), bf16[128,8,512]{2,1,0:T(8,128)(2,1)S(1)}, u32[]{:S(2)}, u32[]{:S(2)}) %all-to-all-start) | async-done | bytes 1048608 | tf_op jit(solution)/shard_map/all_to_all | solution.py:218
  33.1 0.0 copy-start
  33.1 1.3 %copy.27 = bf16[1024,512]{0,1:T(8,128)(2,1)} copy(bf16[1024,512]{1,0:T(8,128)(2,1)S(1)} %bitcast.36) | data formatting | bytes 2097152 | tf_op jit(solution)/shard_map/reshape | solution.py:219
  34.4 0.0 copy-done
  34.4 42.4 %shard_map.127 = (bf16[512,1280]{1,0:T(8,128)(2,1)}, bf16[512,1280]{1,0:T(8,128)(2,1)}, bf16[512,256]{1,0:T(8,128)(2,1)}, bf16[512,256]{1,0:T(8,128)(2,1)}, bf16[1024,512]{1,0:T(8,128)(2,1)}) custom-call(s32[1]{0:T(128)S(6)} %copy.39.length_ref, bf16[512,1280]{1,0:T(8,128)(2,1)} %bitcast.41, bf16[1280,512]{1,0:T(8,128)(2,1)} %bitcast.43, ...), custom_call_target="tpu_custom_call" | custom-call | tf_op jit(solution)/shard_map/pallas_call | solution.py:140
  76.8 24.0 %all_to_all.10 = bf16[128,8,512]{2,1,0:T(8,128)(2,1)S(1)} all-to-all(bf16[128,8,512]{2,1,0:T(8,128)(2,1)} %bitcast.50), channel_id=1, replica_groups=mesh['resp'=32,'head'=4] {'resp','head'}, dimensions={0} | all-to-all | bytes 2097152 | tf_op jit(solution)/shard_map/all_to_all | solution.py:232
  100.8 0.2 convert_reduce_fusion
  101.0 0.6 fusion
Async XLA Ops:
  2.5 12.2 %copy-start.4 = (s32[1,512]{1,0:T(1,128)S(1)}, s32[1,512]{1,0:T(1,128)}, u32[]{:S(2)}) copy-start(s32[1,512]{1,0:T(1,128)} %keep_row_ref.1) | copy-start | bytes 6148
  2.5 13.0 %copy-start.2 = (bf16[1,512,256]{2,1,0:T(8,128)(2,1)S(1)}, bf16[1,512,256]{2,1,0:T(8,128)(2,1)}, u32[]{:S(2)}) copy-start(bf16[1,512,256]{2,1,0:T(8,128)(2,1)} %param.9) | copy-start | bytes 786436
  2.5 13.9 %copy-start.3 = (bf16[1,512,256]{2,1,0:T(8,128)(2,1)S(1)}, bf16[1,512,256]{2,1,0:T(8,128)(2,1)}, u32[]{:S(2)}) copy-start(bf16[1,512,256]{2,1,0:T(8,128)(2,1)} %param.10) | copy-start | bytes 786436
  2.5 14.7 %copy-start.1 = (bf16[1,512,1280]{2,1,0:T(8,128)(2,1)S(1)}, bf16[1,512,1280]{2,1,0:T(8,128)(2,1)}, u32[]{:S(2)}) copy-start(bf16[1,512,1280]{2,1,0:T(8,128)(2,1)} %param.8) | copy-start | bytes 3932164
  2.5 30.6 %all-to-all-start = ((bf16[128,8,512]{2,1,0:T(8,128)(2,1)}), bf16[128,8,512]{2,1,0:T(8,128)(2,1)S(1)}, u32[]{:S(2)}, u32[]{:S(2)}) async-start(bf16[128,8,512]{2,1,0:T(8,128)(2,1)} %bitcast.9), calls=%async_computation | async-start | bytes 2097152 | tf_op jit(solution)/shard_map/all_to_all | solution.py:218
  33.1 1.3 %copy-start = (bf16[128,8,512]{2,1,0:T(8,128)(2,1)}, bf16[128,8,512]{2,1,0:T(8,128)(2,1)S(1)}, u32[]{:S(2)}) copy-start(bf16[128,8,512]{2,1,0:T(8,128)(2,1)S(1)} %all-to-all-done) | copy-start | bytes 3145732

commit v18 on v14

--- a/solution.py
+++ b/solution.py
@@ -60,12 +60,9 @@
             ep.sum(0, keepdims=True)
             + jnp.concatenate([eo1.sum(0, keepdims=True), eo2.sum(0, keepdims=True)], 1)
         )
-        pp = ep * inverse
-        po1 = eo1 * inverse[:, :half]
-        po2 = eo2 * inverse[:, half:]
-        wp = pp.astype(bf16)
-        wo1 = po1.astype(bf16)
-        wo2 = po2.astype(bf16)
+        wp = (ep * inverse).astype(bf16)
+        wo1 = (eo1 * inverse[:, :half]).astype(bf16)
+        wo2 = (eo2 * inverse[:, half:]).astype(bf16)
         vot = vot_ref[...]
         kot = kot_ref[...]
         out = jnp.dot(vpt_ref[...], wp, preferred_element_type=f32) + jnp.concatenate(
@@ -83,9 +80,9 @@
         dpp = jnp.dot(vp, dot, preferred_element_type=f32)
         dpo1 = jnp.dot(vo[:half], dot[:, :half], preferred_element_type=f32)
         dpo2 = jnp.dot(vo, dot[:, half:], preferred_element_type=f32)
-        dsp = (pp * (dpp - delta)).astype(bf16)
-        dso1 = (po1 * (dpo1 - delta[:, :half])).astype(bf16)
-        dso2 = (po2 * (dpo2 - delta[:, half:])).astype(bf16)
+        dsp = (ep * inverse * (dpp - delta)).astype(bf16)
+        dso1 = (eo1 * inverse[:, :half] * (dpo1 - delta[:, :half])).astype(bf16)
+        dso2 = (eo2 * inverse[:, half:] * (dpo2 - delta[:, half:])).astype(bf16)
         dq = jnp.dot(kpt_ref[...], dsp, preferred_element_type=f32) + jnp.concatenate(
             [
                 jnp.dot(kot[:, :half], dso1, preferred_element_type=f32),

time: 94.6 us -> 94.6 us (level)
  no operation moved by 1% of the time
where the time goes in v18:
time: 94.6 us; the launch traced here: 94.2 us
  Pallas kernels  34.9 us (37%)
  blocking collectives  24 us (25%)
  waiting for transfers between devices  12 us (13%)
  starting transfers between devices  11.5 us (12%)
  local copies, waits for them, and re-layouts  9.5 us (10%)
  between operations  1.31 us (1%)
    pallas_call x1, Pallas kernels, attend(): pl.pallas_call(attention_kernel, out_shape=(jax.ShapeDtypeStruct((steps,...  34.9 us
    all_to_all x1, blocking collectives, per_device(): lax.all_to_all(prompt_parts.reshape(devices, rows_here, 2 * kv_width), ('...  24 us
    all_to_all x1, waiting for transfers between devices, per_device(): lax.all_to_all(outgoing, ('resp', 'head'), split_axis=0, concat_axis=0, t...  12 us
    all_to_all x1, starting transfers between devices, per_device(): lax.all_to_all(outgoing, ('resp', 'head'), split_axis=0, concat_axis=0, t...  11.5 us
    unnamed x14, local copies, waits for them, and re-layouts  5.6 us
  transfers between devices with their start and end apart: 1, of which 1 were waited for; matrix products, arithmetic and copies ran while one was open for 7% of the time, Pallas kernels for 0%

profile of v18, /device:TPU:1, one launch (start us, length us, event | category | flops | bytes accessed | tf_op | source)
XLA Modules:
  0.0 94.2 jit_solution(271705695572228216)
XLA Ops:
  0.6 0.7 maximum_bitcast_fusion
  1.4 1.1 %broadcast_in_dim.2 = bf16[32,4,8,512]{3,2,1,0:T(8,128)(2,1)} broadcast(bf16[4,8,512]{2,1,0:T(8,128)(2,1)S(1)} %maximum_bitcast_fusion), dimensions={1,2,3} | broadcast | bytes 1081344 | tf_op jit(solution)/shard_map/broadcast_in_dim | solution.py:190
  2.5 0.0 copy-start.4
  2.5 0.0 copy-start.2
  2.5 0.0 copy-start.3
  2.5 0.0 copy-start.1
  2.5 11.5 %all-to-all-start = ((bf16[128,8,512]{2,1,0:T(8,128)(2,1)}), bf16[128,8,512]{2,1,0:T(8,128)(2,1)S(1)}, u32[]{:S(2)}, u32[]{:S(2)}) async-start(bf16[128,8,512]{2,1,0:T(8,128)(2,1)} %bitcast.9), calls=%async_computation | async-start | bytes 2097152 | tf_op jit(solution)/shard_map/all_to_all | solution.py:193
  14.6 0.0 copy-done.4
  14.6 0.8 copy.34.keep_col_ref
  15.5 0.0 copy-done.2
  15.5 0.8 copy.28
  16.3 0.0 copy-done.3
  16.3 0.8 copy.29
  17.2 0.0 copy-done.1
  17.2 1.5 %copy.25 = bf16[1,512,1280]{1,2,0:T(8,128)(2,1)} copy(bf16[1,512,1280]{2,1,0:T(8,128)(2,1)S(1)} %copy-done.1) | data formatting | bytes 2621440 | tf_op args[0]
  18.6 2.4 %copy.26 = bf16[1,512,1280]{1,2,0:T(8,128)(2,1)} copy(bf16[1,512,1280]{2,1,0:T(8,128)(2,1)} %param.15) | data formatting | bytes 2621440 | tf_op args[7]
  21.1 12.0 %all-to-all-done = bf16[128,8,512]{2,1,0:T(8,128)(2,1)S(1)} async-done(((bf16[128,8,512]{2,1,0:T(8,128)(2,1)}), bf16[128,8,512]{2,1,0:T(8,128)(2,1)S(1)}, u32[]{:S(2)}, u32[]{:S(2)}) %all-to-all-start) | async-done | bytes 1048608 | tf_op jit(solution)/shard_map/all_to_all | solution.py:193
  33.1 0.0 copy-start
  33.1 1.3 %copy.27 = bf16[1024,512]{0,1:T(8,128)(2,1)} copy(bf16[1024,512]{1,0:T(8,128)(2,1)S(1)} %bitcast.36) | data formatting | bytes 2097152 | tf_op jit(solution)/shard_map/reshape | solution.py:194
  34.4 0.0 copy-done
  34.4 34.9 %shard_map.127 = (bf16[512,1280]{1,0:T(8,128)(2,1)}, bf16[512,1280]{1,0:T(8,128)(2,1)}, bf16[512,256]{1,0:T(8,128)(2,1)}, bf16[512,256]{1,0:T(8,128)(2,1)}, bf16[1024,512]{1,0:T(8,128)(2,1)}) custom-call(s32[1]{0:T(128)S(6)} %copy.39.length_ref, bf16[512,1280]{1,0:T(8,128)(2,1)} %bitcast.41, bf16[1280,512]{1,0:T(8,128)(2,1)} %bitcast.43, ...), custom_call_target="tpu_custom_call" | custom-call | tf_op jit(solution)/shard_map/pallas_call | solution.py:117
  69.3 24.0 %all_to_all.10 = bf16[128,8,512]{2,1,0:T(8,128)(2,1)S(1)} all-to-all(bf16[128,8,512]{2,1,0:T(8,128)(2,1)} %bitcast.50), channel_id=1, replica_groups=mesh['resp'=32,'head'=4] {'resp','head'}, dimensions={0} | all-to-all | bytes 2097152 | tf_op jit(solution)/shard_map/all_to_all | solution.py:207
  93.4 0.2 convert_reduce_fusion
  93.5 0.6 fusion
Async XLA Ops:
  2.5 12.2 %copy-start.4 = (s32[1,512]{1,0:T(1,128)S(1)}, s32[1,512]{1,0:T(1,128)}, u32[]{:S(2)}) copy-start(s32[1,512]{1,0:T(1,128)} %keep_row_ref.1) | copy-start | bytes 6148
  2.5 13.0 %copy-start.2 = (bf16[1,512,256]{2,1,0:T(8,128)(2,1)S(1)}, bf16[1,512,256]{2,1,0:T(8,128)(2,1)}, u32[]{:S(2)}) copy-start(bf16[1,512,256]{2,1,0:T(8,128)(2,1)} %param.9) | copy-start | bytes 786436
  2.5 13.9 %copy-start.3 = (bf16[1,512,256]{2,1,0:T(8,128)(2,1)S(1)}, bf16[1,512,256]{2,1,0:T(8,128)(2,1)}, u32[]{:S(2)}) copy-start(bf16[1,512,256]{2,1,0:T(8,128)(2,1)} %param.10) | copy-start | bytes 786436
  2.5 14.7 %copy-start.1 = (bf16[1,512,1280]{2,1,0:T(8,128)(2,1)S(1)}, bf16[1,512,1280]{2,1,0:T(8,128)(2,1)}, u32[]{:S(2)}) copy-start(bf16[1,512,1280]{2,1,0:T(8,128)(2,1)} %param.8) | copy-start | bytes 3932164
  2.5 30.6 %all-to-all-start = ((bf16[128,8,512]{2,1,0:T(8,128)(2,1)}), bf16[128,8,512]{2,1,0:T(8,128)(2,1)S(1)}, u32[]{:S(2)}, u32[]{:S(2)}) async-start(bf16[128,8,512]{2,1,0:T(8,128)(2,1)} %bitcast.9), calls=%async_computation | async-start | bytes 2097152 | tf_op jit(solution)/shard_map/all_to_all | solution.py:193
  33.1 1.3 %copy-start = (bf16[128,8,512]{2,1,0:T(8,128)(2,1)}, bf16[128,8,512]{2,1,0:T(8,128)(2,1)S(1)}, u32[]{:S(2)}) copy-start(bf16[128,8,512]{2,1,0:T(8,128)(2,1)S(1)} %all-to-all-done) | copy-start | bytes 3145732

commit v19 on v13

--- a/solution.py
+++ b/solution.py
@@ -25,7 +25,12 @@
     group_size = q_ref.shape[1] // width
     j = lax.broadcasted_iota(jnp.int32, (steps, 1), 0)
     t = lax.broadcasted_iota(jnp.int32, (1, steps), 1)
-    allowed = (j <= t) & (j < length)
+    blocks = 4
+    part = steps // blocks
+    allowed = [
+        (j[: (b + 1) * part] <= t[:, b * part : (b + 1) * part]) & (j[: (b + 1) * part] < length)
+        for b in range(blocks)
+    ]
     live = t < length
     live_col = j < length
     factor_col = (keep_col_ref[...] * live_col.astype(jnp.int32)).astype(bf16)
@@ -43,18 +48,31 @@
         vp = vp_ref[...]
         vo = vo_ref[...]
         sp = jnp.dot(kp, qt, preferred_element_type=f32) * scale
-        so = jnp.dot(ko, qt, preferred_element_type=f32) * scale
-        so = jnp.where(allowed, so, -jnp.inf)
-        top = jnp.maximum(sp.max(0, keepdims=True), so.max(0, keepdims=True))
+        so = [
+            jnp.where(
+                allowed[b],
+                jnp.dot(ko[: (b + 1) * part], qt[:, b * part : (b + 1) * part], preferred_element_type=f32)
+                * scale,
+                -jnp.inf,
+            )
+            for b in range(blocks)
+        ]
+        top = jnp.maximum(
+            sp.max(0, keepdims=True), jnp.concatenate([s.max(0, keepdims=True) for s in so], 1)
+        )
         ep = jnp.exp(sp - top)
-        eo = jnp.exp(so - top)
-        inverse = 1.0 / (ep.sum(0, keepdims=True) + eo.sum(0, keepdims=True))
+        eo = [jnp.exp(s - top[:, b * part : (b + 1) * part]) for b, s in enumerate(so)]
+        inverse = 1.0 / (
+            ep.sum(0, keepdims=True) + jnp.concatenate([e.sum(0, keepdims=True) for e in eo], 1)
+        )
         pp = ep * inverse
-        po = eo * inverse
+        po = [e * inverse[:, b * part : (b + 1) * part] for b, e in enumerate(eo)]
         wp = pp.astype(bf16)
-        wo = po.astype(bf16)
-        out = jnp.dot(vpt_ref[...], wp, preferred_element_type=f32) + jnp.dot(
-            vot_ref[...], wo, preferred_element_type=f32
+        wo = [p.astype(bf16) for p in po]
+        vot = vot_ref[...]
+        kot = kot_ref[...]
+        out = jnp.dot(vpt_ref[...], wp, preferred_element_type=f32) + jnp.concatenate(
+            [jnp.dot(vot[:, : (b + 1) * part], w, preferred_element_type=f32) for b, w in enumerate(wo)], 1
         )
         att = jnp.where(live, out, 0.0).astype(bf16).astype(f32)
         att_ref[:, cols] = att.T.astype(bf16)
@@ -62,17 +80,28 @@
         dot = dot_ref[cols, :] * factor_row
         delta = (dot.astype(f32) * att).sum(0, keepdims=True)
         dpp = jnp.dot(vp, dot, preferred_element_type=f32)
-        dpo = jnp.dot(vo, dot, preferred_element_type=f32)
         dsp = (pp * (dpp - delta)).astype(bf16)
-        dso = (po * (dpo - delta)).astype(bf16)
-        dq = jnp.dot(kpt_ref[...], dsp, preferred_element_type=f32) + jnp.dot(
-            kot_ref[...], dso, preferred_element_type=f32
+        dso = [
+            (
+                p
+                * (
+                    jnp.dot(vo[: (b + 1) * part], dot[:, b * part : (b + 1) * part], preferred_element_type=f32)
+                    - delta[:, b * part : (b + 1) * part]
+                )
+            ).astype(bf16)
+            for b, p in enumerate(po)
+        ]
+        dq = jnp.dot(kpt_ref[...], dsp, preferred_element_type=f32) + jnp.concatenate(
+            [jnp.dot(kot[:, : (b + 1) * part], d, preferred_element_type=f32) for b, d in enumerate(dso)], 1
         )
         dq_ref[:, cols] = (dq * scale).T.astype(bf16)
         pg_ref[:, :width] += jnp.dot(dsp, q, preferred_element_type=f32) * scale
         pg_ref[:, width:] += jnp.dot(wp, do, preferred_element_type=f32)
-        dko_acc[...] += jnp.dot(dso, q, preferred_element_type=f32) * scale
-        dvo_acc[...] += jnp.dot(wo, do, preferred_element_type=f32)
+        for b in range(blocks):
+            rows = slice(0, (b + 1) * part)
+            tb = slice(b * part, (b + 1) * part)
+            dko_acc[rows, :] += jnp.dot(dso[b], q[tb], preferred_element_type=f32) * scale
+            dvo_acc[rows, :] += jnp.dot(wo[b], do[tb], preferred_element_type=f32)
         return carry
 
     lax.fori_loop(0, group_size, head, 0)

time: 95.7 us -> 94.8 us (level)
  no operation moved by 1% of the time
where the time goes in v19:
time: 94.8 us; the launch traced here: 94.4 us
  Pallas kernels  35.2 us (37%)
  blocking collectives  24 us (25%)
  waiting for transfers between devices  12 us (13%)
  starting transfers between devices  11.5 us (12%)
  local copies, waits for them, and re-layouts  9.5 us (10%)
  between operations  1.31 us (1%)
    pallas_call x1, Pallas kernels, attend(): pl.pallas_call(attention_kernel, out_shape=(jax.ShapeDtypeStruct((steps,...  35.2 us
    all_to_all x1, blocking collectives, per_device(): lax.all_to_all(prompt_parts.reshape(devices, rows_here, 2 * kv_width), ('...  24 us
    all_to_all x1, waiting for transfers between devices, per_device(): lax.all_to_all(outgoing, ('resp', 'head'), split_axis=0, concat_axis=0, t...  12 us
    all_to_all x1, starting transfers between devices, per_device(): lax.all_to_all(outgoing, ('resp', 'head'), split_axis=0, concat_axis=0, t...  11.5 us
    unnamed x14, local copies, waits for them, and re-layouts  5.6 us
  transfers between devices with their start and end apart: 1, of which 1 were waited for; matrix products, arithmetic and copies ran while one was open for 7% of the time, Pallas kernels for 0%

profile of v19, /device:TPU:1, one launch (start us, length us, event | category | flops | bytes accessed | tf_op | source)
XLA Modules:
  0.0 94.4 jit_solution(13427832474796240908)
XLA Ops:
  0.6 0.7 maximum_bitcast_fusion
  1.4 1.1 %broadcast_in_dim.2 = bf16[32,4,8,512]{3,2,1,0:T(8,128)(2,1)} broadcast(bf16[4,8,512]{2,1,0:T(8,128)(2,1)S(1)} %maximum_bitcast_fusion), dimensions={1,2,3} | broadcast | bytes 1081344 | tf_op jit(solution)/shard_map/broadcast_in_dim | solution.py:195
  2.5 0.0 copy-start.4
  2.5 0.0 copy-start.2
  2.5 0.0 copy-start.3
  2.5 0.0 copy-start.1
  2.5 11.5 %all-to-all-start = ((bf16[128,8,512]{2,1,0:T(8,128)(2,1)}), bf16[128,8,512]{2,1,0:T(8,128)(2,1)S(1)}, u32[]{:S(2)}, u32[]{:S(2)}) async-start(bf16[128,8,512]{2,1,0:T(8,128)(2,1)} %bitcast.9), calls=%async_computation | async-start | bytes 2097152 | tf_op jit(solution)/shard_map/all_to_all | solution.py:198
  14.6 0.0 copy-done.4
  14.6 0.8 copy.34.keep_col_ref
  15.5 0.0 copy-done.2
  15.5 0.8 copy.28
  16.3 0.0 copy-done.3
  16.3 0.8 copy.29
  17.2 0.0 copy-done.1
  17.2 1.5 %copy.25 = bf16[1,512,1280]{1,2,0:T(8,128)(2,1)} copy(bf16[1,512,1280]{2,1,0:T(8,128)(2,1)S(1)} %copy-done.1) | data formatting | bytes 2621440 | tf_op args[0]
  18.6 2.4 %copy.26 = bf16[1,512,1280]{1,2,0:T(8,128)(2,1)} copy(bf16[1,512,1280]{2,1,0:T(8,128)(2,1)} %param.15) | data formatting | bytes 2621440 | tf_op args[7]
  21.1 12.0 %all-to-all-done = bf16[128,8,512]{2,1,0:T(8,128)(2,1)S(1)} async-done(((bf16[128,8,512]{2,1,0:T(8,128)(2,1)}), bf16[128,8,512]{2,1,0:T(8,128)(2,1)S(1)}, u32[]{:S(2)}, u32[]{:S(2)}) %all-to-all-start) | async-done | bytes 1048608 | tf_op jit(solution)/shard_map/all_to_all | solution.py:198
  33.1 0.0 copy-start
  33.1 1.3 %copy.27 = bf16[1024,512]{0,1:T(8,128)(2,1)} copy(bf16[1024,512]{1,0:T(8,128)(2,1)S(1)} %bitcast.36) | data formatting | bytes 2097152 | tf_op jit(solution)/shard_map/reshape | solution.py:199
  34.4 0.0 copy-done
  34.4 35.2 %shard_map.127 = (bf16[512,1280]{1,0:T(8,128)(2,1)}, bf16[512,1280]{1,0:T(8,128)(2,1)}, bf16[512,256]{1,0:T(8,128)(2,1)}, bf16[512,256]{1,0:T(8,128)(2,1)}, bf16[1024,512]{1,0:T(8,128)(2,1)}) custom-call(s32[1]{0:T(128)S(6)} %copy.39.length_ref, bf16[512,1280]{1,0:T(8,128)(2,1)} %bitcast.41, bf16[1280,512]{1,0:T(8,128)(2,1)} %bitcast.43, ...), custom_call_target="tpu_custom_call" | custom-call | tf_op jit(solution)/shard_map/pallas_call | solution.py:122
  69.6 24.0 %all_to_all.10 = bf16[128,8,512]{2,1,0:T(8,128)(2,1)S(1)} all-to-all(bf16[128,8,512]{2,1,0:T(8,128)(2,1)} %bitcast.50), channel_id=1, replica_groups=mesh['resp'=32,'head'=4] {'resp','head'}, dimensions={0} | all-to-all | bytes 2097152 | tf_op jit(solution)/shard_map/all_to_all | solution.py:212
  93.6 0.2 convert_reduce_fusion
  93.7 0.6 fusion
Async XLA Ops:
  2.5 12.2 %copy-start.4 = (s32[1,512]{1,0:T(1,128)S(1)}, s32[1,512]{1,0:T(1,128)}, u32[]{:S(2)}) copy-start(s32[1,512]{1,0:T(1,128)} %keep_row_ref.1) | copy-start | bytes 6148
  2.5 13.0 %copy-start.2 = (bf16[1,512,256]{2,1,0:T(8,128)(2,1)S(1)}, bf16[1,512,256]{2,1,0:T(8,128)(2,1)}, u32[]{:S(2)}) copy-start(bf16[1,512,256]{2,1,0:T(8,128)(2,1)} %param.9) | copy-start | bytes 786436
  2.5 13.9 %copy-start.3 = (bf16[1,512,256]{2,1,0:T(8,128)(2,1)S(1)}, bf16[1,512,256]{2,1,0:T(8,128)(2,1)}, u32[]{:S(2)}) copy-start(bf16[1,512,256]{2,1,0:T(8,128)(2,1)} %param.10) | copy-start | bytes 786436
  2.5 14.7 %copy-start.1 = (bf16[1,512,1280]{2,1,0:T(8,128)(2,1)S(1)}, bf16[1,512,1280]{2,1,0:T(8,128)(2,1)}, u32[]{:S(2)}) copy-start(bf16[1,512,1280]{2,1,0:T(8,128)(2,1)} %param.8) | copy-start | bytes 3932164
  2.5 30.6 %all-to-all-start = ((bf16[128,8,512]{2,1,0:T(8,128)(2,1)}), bf16[128,8,512]{2,1,0:T(8,128)(2,1)S(1)}, u32[]{:S(2)}, u32[]{:S(2)}) async-start(bf16[128,8,512]{2,1,0:T(8,128)(2,1)} %bitcast.9), calls=%async_computation | async-start | bytes 2097152 | tf_op jit(solution)/shard_map/all_to_all | solution.py:198
  33.1 1.3 %copy-start = (bf16[128,8,512]{2,1,0:T(8,128)(2,1)}, bf16[128,8,512]{2,1,0:T(8,128)(2,1)S(1)}, u32[]{:S(2)}) copy-start(bf16[128,8,512]{2,1,0:T(8,128)(2,1)S(1)} %all-to-all-done) | copy-start | bytes 3145732

commit v20 on v15

--- a/solution.py
+++ b/solution.py
@@ -13,7 +13,7 @@
 
 
 def attention_kernel(
-    length_ref, q_ref, qt_ref, do_ref, dot_ref, kp_ref, vp_ref,
+    length_ref, q_ref, qt_ref, do_ref, dot_ref, pkv_ref,
     ko_ref, kot_ref, vo_ref, vot_ref, keep_col_ref, keep_row_ref,
     att_ref, dq_ref, dko_ref, dvo_ref, pg_out, dko_acc, dvo_acc, pg_ref, kpt_ref, vpt_ref,
 ):
@@ -32,6 +32,9 @@
     live_col = j < length
     factor_col = (keep_col_ref[...] * live_col.astype(jnp.int32)).astype(bf16)
     factor_row = (keep_row_ref[...] * live.astype(jnp.int32)).astype(bf16)
+    k = pl.program_id(0)
+    kp_ref = pkv_ref.at[:, pl.ds(pl.multiple_of(k * width, width), width)]
+    vp_ref = pkv_ref.at[:, pl.ds(pl.multiple_of((k + pl.num_programs(0)) * width, width), width)]
     kpt_ref[...] = kp_ref[...].astype(f32).T.astype(bf16)
     vpt_ref[...] = vp_ref[...].astype(f32).T.astype(bf16)
     dko_acc[...] = jnp.zeros_like(dko_acc)
@@ -136,8 +139,7 @@
                 pl.BlockSpec((heads, steps), kv_block_t),
                 pl.BlockSpec((steps, heads), kv_block),
                 pl.BlockSpec((heads, steps), kv_block_t),
-                pl.BlockSpec((prompt_rows, HEAD_DIM), kv_block),
-                pl.BlockSpec((prompt_rows, HEAD_DIM), lambda k, n: (0, k + kv_count)),
+                pl.BlockSpec(memory_space=pltpu.VMEM),
                 pl.BlockSpec((steps, HEAD_DIM), kv_block),
                 pl.BlockSpec((HEAD_DIM, steps), kv_block_t),
                 pl.BlockSpec((steps, HEAD_DIM), kv_block),
@@ -166,7 +168,6 @@
         queries.T,
         out_grad,
         out_grad.T,
-        prompt_kv,
         prompt_kv,
         keys,
         keys.T,

time: 94.5 us -> 93.8 us (level)
  local copies, waits for them, and re-layouts: 9.23 us -> 7.29 us
    unnamed x14, local copies, waits for them, and re-layouts: 6.64 us -> 4.7 us
  transfers between devices with their start and end apart: 1 -> 1, of which waited for: 1 -> 1; matrix products, arithmetic and copies ran while one was open for 7% -> 6% of each run, Pallas kernels for 0% -> 0%
where the time goes in v20:
time: 93.8 us; the launch traced here: 93.4 us
  Pallas kernels  35.4 us (38%)
  blocking collectives  24 us (26%)
  waiting for transfers between devices  12.5 us (13%)
  starting transfers between devices  12 us (13%)
  local copies, waits for them, and re-layouts  7.29 us (8%)
  between operations  1.31 us (1%)
    pallas_call x1, Pallas kernels, attend(): pl.pallas_call(attention_kernel, out_shape=(jax.ShapeDtypeStruct((steps,...  35.4 us
    all_to_all x1, blocking collectives, per_device(): lax.all_to_all(prompt_parts.reshape(devices, rows_here, 2 * kv_width), ('...  24 us
    all_to_all x1, waiting for transfers between devices, per_device(): lax.all_to_all(outgoing, ('resp', 'head'), split_axis=0, concat_axis=0, t...  12.5 us
    all_to_all x1, starting transfers between devices, per_device(): lax.all_to_all(outgoing, ('resp', 'head'), split_axis=0, concat_axis=0, t...  12 us
    unnamed x14, local copies, waits for them, and re-layouts  4.7 us
  transfers between devices with their start and end apart: 1, of which 1 were waited for; matrix products, arithmetic and copies ran while one was open for 6% of the time, Pallas kernels for 0%

profile of v20, /device:TPU:1, one launch (start us, length us, event | category | flops | bytes accessed | tf_op | source)
XLA Modules:
  0.0 93.4 jit_solution(14626272971223584944)
XLA Ops:
  0.6 0.7 maximum_bitcast_fusion
  1.4 1.1 %broadcast_in_dim.2 = bf16[32,4,8,512]{3,2,1,0:T(8,128)(2,1)} broadcast(bf16[4,8,512]{2,1,0:T(8,128)(2,1)S(1)} %maximum_bitcast_fusion), dimensions={1,2,3} | broadcast | bytes 1081344 | tf_op jit(solution)/shard_map/broadcast_in_dim | solution.py:193
  2.5 0.0 copy-start.4
  2.5 0.0 copy-start.2
  2.5 0.0 copy-start.3
  2.5 0.0 copy-start
  2.5 12.0 %all-to-all-start = ((bf16[128,8,512]{2,1,0:T(8,128)(2,1)}), bf16[128,8,512]{2,1,0:T(8,128)(2,1)}, u32[]{:S(2)}, u32[]{:S(2)}) async-start(bf16[128,8,512]{2,1,0:T(8,128)(2,1)} %bitcast.9), calls=%async_computation | async-start | bytes 2097152 | tf_op jit(solution)/shard_map/all_to_all | solution.py:196
  15.1 0.0 copy-done.4
  15.1 0.9 copy.30.keep_col_ref
  16.0 0.0 copy-done.2
  16.0 0.9 copy.24
  16.8 0.0 copy-done.3
  16.8 0.9 copy.25
  17.7 0.0 copy-done
  17.7 0.0 copy-start.1
  17.7 1.5 %copy.22 = bf16[1,512,1280]{1,2,0:T(8,128)(2,1)} copy(bf16[1,512,1280]{2,1,0:T(8,128)(2,1)S(1)} %copy-done) | data formatting | bytes 2621440 | tf_op args[0]
  19.2 0.0 copy-done.1
  19.2 1.5 %copy.23 = bf16[1,512,1280]{1,2,0:T(8,128)(2,1)} copy(bf16[1,512,1280]{2,1,0:T(8,128)(2,1)S(1)} %copy-done.1) | data formatting | bytes 2621440 | tf_op args[7]
  20.7 12.5 %all-to-all-done = bf16[128,8,512]{2,1,0:T(8,128)(2,1)} async-done(((bf16[128,8,512]{2,1,0:T(8,128)(2,1)}), bf16[128,8,512]{2,1,0:T(8,128)(2,1)}, u32[]{:S(2)}, u32[]{:S(2)}) %all-to-all-start) | async-done | bytes 1048608 | tf_op jit(solution)/shard_map/all_to_all | solution.py:196
  33.2 35.4 %shard_map.127 = (bf16[512,1280]{1,0:T(8,128)(2,1)}, bf16[512,1280]{1,0:T(8,128)(2,1)}, bf16[512,256]{1,0:T(8,128)(2,1)}, bf16[512,256]{1,0:T(8,128)(2,1)}, bf16[1024,512]{1,0:T(8,128)(2,1)}) custom-call(s32[1]{0:T(128)S(6)} %copy.35.length_ref, bf16[512,1280]{1,0:T(8,128)(2,1)} %bitcast.35, bf16[1280,512]{1,0:T(8,128)(2,1)} %bitcast.37, ...), custom_call_target="tpu_custom_call" | custom-call | tf_op jit(solution)/shard_map/pallas_call | solution.py:125
  68.5 24.0 %all_to_all.10 = bf16[128,8,512]{2,1,0:T(8,128)(2,1)S(1)} all-to-all(bf16[128,8,512]{2,1,0:T(8,128)(2,1)} %bitcast.44), channel_id=1, replica_groups=mesh['resp'=32,'head'=4] {'resp','head'}, dimensions={0} | all-to-all | bytes 2097152 | tf_op jit(solution)/shard_map/all_to_all | solution.py:210
  92.6 0.2 convert_reduce_fusion
  92.7 0.6 fusion
Async XLA Ops:
  2.5 12.6 %copy-start.4 = (s32[1,512]{1,0:T(1,128)S(1)}, s32[1,512]{1,0:T(1,128)}, u32[]{:S(2)}) copy-start(s32[1,512]{1,0:T(1,128)} %keep_row_ref.1) | copy-start | bytes 6148
  2.5 13.5 %copy-start.2 = (bf16[1,512,256]{2,1,0:T(8,128)(2,1)S(1)}, bf16[1,512,256]{2,1,0:T(8,128)(2,1)}, u32[]{:S(2)}) copy-start(bf16[1,512,256]{2,1,0:T(8,128)(2,1)} %param.9) | copy-start | bytes 786436
  2.5 14.4 %copy-start.3 = (bf16[1,512,256]{2,1,0:T(8,128)(2,1)S(1)}, bf16[1,512,256]{2,1,0:T(8,128)(2,1)}, u32[]{:S(2)}) copy-start(bf16[1,512,256]{2,1,0:T(8,128)(2,1)} %param.10) | copy-start | bytes 786436
  2.5 15.2 %copy-start = (bf16[1,512,1280]{2,1,0:T(8,128)(2,1)S(1)}, bf16[1,512,1280]{2,1,0:T(8,128)(2,1)}, u32[]{:S(2)}) copy-start(bf16[1,512,1280]{2,1,0:T(8,128)(2,1)} %param.8) | copy-start | bytes 3932164
  2.5 30.7 %all-to-all-start = ((bf16[128,8,512]{2,1,0:T(8,128)(2,1)}), bf16[128,8,512]{2,1,0:T(8,128)(2,1)}, u32[]{:S(2)}, u32[]{:S(2)}) async-start(bf16[128,8,512]{2,1,0:T(8,128)(2,1)} %bitcast.9), calls=%async_computation | async-start | bytes 2097152 | tf_op jit(solution)/shard_map/all_to_all | solution.py:196
  17.7 1.5 %copy-start.1 = (bf16[1,512,1280]{2,1,0:T(8,128)(2,1)S(1)}, bf16[1,512,1280]{2,1,0:T(8,128)(2,1)}, u32[]{:S(2)}) copy-start(bf16[1,512,1280]{2,1,0:T(8,128)(2,1)} %param.15) | copy-start | bytes 3932164

commit v21 on v20

--- a/solution.py
+++ b/solution.py
@@ -13,16 +13,21 @@
 
 
 def attention_kernel(
-    length_ref, q_ref, qt_ref, do_ref, dot_ref, pkv_ref,
+    length_ref, q_all, qt_all, do_all, dot_all, pkv_ref,
     ko_ref, kot_ref, vo_ref, vot_ref, keep_col_ref, keep_row_ref,
     att_ref, dq_ref, dko_ref, dvo_ref, pg_out, dko_acc, dvo_acc, pg_ref, kpt_ref, vpt_ref,
 ):
     f32, bf16 = jnp.float32, jnp.bfloat16
     scale = HEAD_DIM ** (-0.5)
     length = length_ref[0]
-    steps = q_ref.shape[0]
+    steps = q_all.shape[0]
     width = HEAD_DIM
-    group_size = q_ref.shape[1] // width
+    group_size = att_ref.shape[1] // width
+    heads = pl.ds(pl.multiple_of(pl.program_id(0) * group_size * width, width), group_size * width)
+    q_ref = q_all.at[:, heads]
+    qt_ref = qt_all.at[heads, :]
+    do_ref = do_all.at[:, heads]
+    dot_ref = dot_all.at[heads, :]
     j = lax.broadcasted_iota(jnp.int32, (steps, 1), 0)
     t = lax.broadcasted_iota(jnp.int32, (1, steps), 1)
     half = steps // 2
@@ -135,10 +140,10 @@
             num_scalar_prefetch=1,
             grid=(kv_count,),
             in_specs=[
-                pl.BlockSpec((steps, heads), kv_block),
-                pl.BlockSpec((heads, steps), kv_block_t),
-                pl.BlockSpec((steps, heads), kv_block),
-                pl.BlockSpec((heads, steps), kv_block_t),
+                pl.BlockSpec(memory_space=pltpu.VMEM),
+                pl.BlockSpec(memory_space=pltpu.VMEM),
+                pl.BlockSpec(memory_space=pltpu.VMEM),
+                pl.BlockSpec(memory_space=pltpu.VMEM),
                 pl.BlockSpec(memory_space=pltpu.VMEM),
                 pl.BlockSpec((steps, HEAD_DIM), kv_block),
                 pl.BlockSpec((HEAD_DIM, steps), kv_block_t),

time: 93.8 us -> 94.3 us (level)
  no operation moved by 1% of the time
where the time goes in v21:
time: 94.3 us; the launch traced here: 93.9 us
  Pallas kernels  35.9 us (38%)
  blocking collectives  24 us (25%)
  waiting for transfers between devices  12.5 us (13%)
  starting transfers between devices  12 us (13%)
  local copies, waits for them, and re-layouts  7.29 us (8%)
  between operations  1.31 us (1%)
    pallas_call x1, Pallas kernels, attend(): pl.pallas_call(attention_kernel, out_shape=(jax.ShapeDtypeStruct((steps,...  35.9 us
    all_to_all x1, blocking collectives, per_device(): lax.all_to_all(prompt_parts.reshape(devices, rows_here, 2 * kv_width), ('...  24 us
    all_to_all x1, waiting for transfers between devices, per_device(): lax.all_to_all(outgoing, ('resp', 'head'), split_axis=0, concat_axis=0, t...  12.5 us
    all_to_all x1, starting transfers between devices, per_device(): lax.all_to_all(outgoing, ('resp', 'head'), split_axis=0, concat_axis=0, t...  12 us
    unnamed x14, local copies, waits for them, and re-layouts  4.7 us
  transfers between devices with their start and end apart: 1, of which 1 were waited for; matrix products, arithmetic and copies ran while one was open for 6% of the time, Pallas kernels for 0%

profile of v21, /device:TPU:1, one launch (start us, length us, event | category | flops | bytes accessed | tf_op | source)
XLA Modules:
  0.0 93.9 jit_solution(10519842519722960652)
XLA Ops:
  0.6 0.7 maximum_bitcast_fusion
  1.4 1.1 %broadcast_in_dim.2 = bf16[32,4,8,512]{3,2,1,0:T(8,128)(2,1)} broadcast(bf16[4,8,512]{2,1,0:T(8,128)(2,1)S(1)} %maximum_bitcast_fusion), dimensions={1,2,3} | broadcast | bytes 1081344 | tf_op jit(solution)/shard_map/broadcast_in_dim | solution.py:198
  2.5 0.0 copy-start.4
  2.5 0.0 copy-start.2
  2.5 0.0 copy-start.3
  2.5 0.0 copy-start
  2.5 12.0 %all-to-all-start = ((bf16[128,8,512]{2,1,0:T(8,128)(2,1)}), bf16[128,8,512]{2,1,0:T(8,128)(2,1)}, u32[]{:S(2)}, u32[]{:S(2)}) async-start(bf16[128,8,512]{2,1,0:T(8,128)(2,1)} %bitcast.9), calls=%async_computation | async-start | bytes 2097152 | tf_op jit(solution)/shard_map/all_to_all | solution.py:201
  15.1 0.0 copy-done.4
  15.1 0.9 copy.30.keep_col_ref
  16.0 0.0 copy-done.2
  16.0 0.9 copy.24
  16.8 0.0 copy-done.3
  16.8 0.9 copy.25
  17.7 0.0 copy-done
  17.7 0.0 copy-start.1
  17.7 1.5 %copy.22 = bf16[1,512,1280]{1,2,0:T(8,128)(2,1)} copy(bf16[1,512,1280]{2,1,0:T(8,128)(2,1)S(1)} %copy-done) | data formatting | bytes 2621440 | tf_op args[0]
  19.2 0.0 copy-done.1
  19.2 1.5 %copy.23 = bf16[1,512,1280]{1,2,0:T(8,128)(2,1)} copy(bf16[1,512,1280]{2,1,0:T(8,128)(2,1)S(1)} %copy-done.1) | data formatting | bytes 2621440 | tf_op args[7]
  20.7 12.5 %all-to-all-done = bf16[128,8,512]{2,1,0:T(8,128)(2,1)} async-done(((bf16[128,8,512]{2,1,0:T(8,128)(2,1)}), bf16[128,8,512]{2,1,0:T(8,128)(2,1)}, u32[]{:S(2)}, u32[]{:S(2)}) %all-to-all-start) | async-done | bytes 1048608 | tf_op jit(solution)/shard_map/all_to_all | solution.py:201
  33.2 35.9 %shard_map.127 = (bf16[512,1280]{1,0:T(8,128)(2,1)}, bf16[512,1280]{1,0:T(8,128)(2,1)}, bf16[512,256]{1,0:T(8,128)(2,1)}, bf16[512,256]{1,0:T(8,128)(2,1)}, bf16[1024,512]{1,0:T(8,128)(2,1)}) custom-call(s32[1]{0:T(128)S(6)} %copy.35.length_ref, bf16[512,1280]{1,0:T(8,128)(2,1)} %bitcast.35, bf16[1280,512]{1,0:T(8,128)(2,1)} %bitcast.37, ...), custom_call_target="tpu_custom_call" | custom-call | tf_op jit(solution)/shard_map/pallas_call | solution.py:130
  69.0 24.0 %all_to_all.10 = bf16[128,8,512]{2,1,0:T(8,128)(2,1)S(1)} all-to-all(bf16[128,8,512]{2,1,0:T(8,128)(2,1)} %bitcast.44), channel_id=1, replica_groups=mesh['resp'=32,'head'=4] {'resp','head'}, dimensions={0} | all-to-all | bytes 2097152 | tf_op jit(solution)/shard_map/all_to_all | solution.py:215
  93.1 0.2 convert_reduce_fusion
  93.3 0.6 fusion
Async XLA Ops:
  2.5 12.6 %copy-start.4 = (s32[1,512]{1,0:T(1,128)S(1)}, s32[1,512]{1,0:T(1,128)}, u32[]{:S(2)}) copy-start(s32[1,512]{1,0:T(1,128)} %keep_row_ref.1) | copy-start | bytes 6148
  2.5 13.5 %copy-start.2 = (bf16[1,512,256]{2,1,0:T(8,128)(2,1)S(1)}, bf16[1,512,256]{2,1,0:T(8,128)(2,1)}, u32[]{:S(2)}) copy-start(bf16[1,512,256]{2,1,0:T(8,128)(2,1)} %param.9) | copy-start | bytes 786436
  2.5 14.4 %copy-start.3 = (bf16[1,512,256]{2,1,0:T(8,128)(2,1)S(1)}, bf16[1,512,256]{2,1,0:T(8,128)(2,1)}, u32[]{:S(2)}) copy-start(bf16[1,512,256]{2,1,0:T(8,128)(2,1)} %param.10) | copy-start | bytes 786436
  2.5 15.2 %copy-start = (bf16[1,512,1280]{2,1,0:T(8,128)(2,1)S(1)}, bf16[1,512,1280]{2,1,0:T(8,128)(2,1)}, u32[]{:S(2)}) copy-start(bf16[1,512,1280]{2,1,0:T(8,128)(2,1)} %param.8) | copy-start | bytes 3932164
  2.5 30.7 %all-to-all-start = ((bf16[128,8,512]{2,1,0:T(8,128)(2,1)}), bf16[128,8,512]{2,1,0:T(8,128)(2,1)}, u32[]{:S(2)}, u32[]{:S(2)}) async-start(bf16[128,8,512]{2,1,0:T(8,128)(2,1)} %bitcast.9), calls=%async_computation | async-start | bytes 2097152 | tf_op jit(solution)/shard_map/all_to_all | solution.py:201
  17.7 1.5 %copy-start.1 = (bf16[1,512,1280]{2,1,0:T(8,128)(2,1)S(1)}, bf16[1,512,1280]{2,1,0:T(8,128)(2,1)}, u32[]{:S(2)}) copy-start(bf16[1,512,1280]{2,1,0:T(8,128)(2,1)} %param.15) | copy-start | bytes 3932164

commit v22 on v20

--- a/solution.py
+++ b/solution.py
@@ -110,8 +110,8 @@
     lax.fori_loop(0, group_size, head, 0)
     dko_ref[...] = dko_acc[...].astype(bf16)
     dvo_ref[...] = dvo_acc[...].astype(bf16)
-    pg_out[:, :width] = pg_ref[:, :width].astype(bf16)
-    pg_out[:, width:] = pg_ref[:, width:].astype(bf16)
+    window = pl.ds(pl.multiple_of(pl.program_id(0) * 2 * width, width), 2 * width)
+    pg_out[:, window] = pg_ref[...].astype(bf16)
 
 
 def attend(length, queries, out_grad, prompt_kv, keys, values, keep, kv_count):
@@ -152,7 +152,7 @@
                 pl.BlockSpec((steps, heads), kv_block),
                 pl.BlockSpec((steps, HEAD_DIM), kv_block),
                 pl.BlockSpec((steps, HEAD_DIM), kv_block),
-                pl.BlockSpec((prompt_rows, 2 * HEAD_DIM), kv_block),
+                pl.BlockSpec(memory_space=pltpu.VMEM),
             ],
             scratch_shapes=[pltpu.VMEM((steps, HEAD_DIM), f32)] * 2
             + [pltpu.VMEM((prompt_rows, 2 * HEAD_DIM), f32)]

time: 93.8 us -> 93.9 us (level)
  no operation moved by 1% of the time
where the time goes in v22:
time: 93.9 us; the launch traced here: 93.5 us
  Pallas kernels  35.5 us (38%)
  blocking collectives  24 us (26%)
  waiting for transfers between devices  12.5 us (13%)
  starting transfers between devices  12 us (13%)
  local copies, waits for them, and re-layouts  7.29 us (8%)
  between operations  1.32 us (1%)
    pallas_call x1, Pallas kernels, attend(): pl.pallas_call(attention_kernel, out_shape=(jax.ShapeDtypeStruct((steps,...  35.5 us
    all_to_all x1, blocking collectives, per_device(): lax.all_to_all(prompt_parts.reshape(devices, rows_here, 2 * kv_width), ('...  24 us
    all_to_all x1, waiting for transfers between devices, per_device(): lax.all_to_all(outgoing, ('resp', 'head'), split_axis=0, concat_axis=0, t...  12.5 us
    all_to_all x1, starting transfers between devices, per_device(): lax.all_to_all(outgoing, ('resp', 'head'), split_axis=0, concat_axis=0, t...  12 us
    unnamed x14, local copies, waits for them, and re-layouts  4.7 us
  transfers between devices with their start and end apart: 1, of which 1 were waited for; matrix products, arithmetic and copies ran while one was open for 6% of the time, Pallas kernels for 0%

profile of v22, /device:TPU:1, one launch (start us, length us, event | category | flops | bytes accessed | tf_op | source)
XLA Modules:
  0.0 93.5 jit_solution(5569373773956547819)
XLA Ops:
  0.6 0.7 maximum_bitcast_fusion
  1.4 1.1 %broadcast_in_dim.2 = bf16[32,4,8,512]{3,2,1,0:T(8,128)(2,1)} broadcast(bf16[4,8,512]{2,1,0:T(8,128)(2,1)S(1)} %maximum_bitcast_fusion), dimensions={1,2,3} | broadcast | bytes 1081344 | tf_op jit(solution)/shard_map/broadcast_in_dim | solution.py:193
  2.5 0.0 copy-start.4
  2.5 0.0 copy-start.2
  2.5 0.0 copy-start.3
  2.5 0.0 copy-start
  2.5 12.0 %all-to-all-start = ((bf16[128,8,512]{2,1,0:T(8,128)(2,1)}), bf16[128,8,512]{2,1,0:T(8,128)(2,1)}, u32[]{:S(2)}, u32[]{:S(2)}) async-start(bf16[128,8,512]{2,1,0:T(8,128)(2,1)} %bitcast.9), calls=%async_computation | async-start | bytes 2097152 | tf_op jit(solution)/shard_map/all_to_all | solution.py:196
  15.1 0.0 copy-done.4
  15.1 0.9 copy.30.keep_col_ref
  16.0 0.0 copy-done.2
  16.0 0.9 copy.24
  16.8 0.0 copy-done.3
  16.8 0.9 copy.25
  17.7 0.0 copy-done
  17.7 0.0 copy-start.1
  17.7 1.5 %copy.22 = bf16[1,512,1280]{1,2,0:T(8,128)(2,1)} copy(bf16[1,512,1280]{2,1,0:T(8,128)(2,1)S(1)} %copy-done) | data formatting | bytes 2621440 | tf_op args[0]
  19.2 0.0 copy-done.1
  19.2 1.5 %copy.23 = bf16[1,512,1280]{1,2,0:T(8,128)(2,1)} copy(bf16[1,512,1280]{2,1,0:T(8,128)(2,1)S(1)} %copy-done.1) | data formatting | bytes 2621440 | tf_op args[7]
  20.7 12.5 %all-to-all-done = bf16[128,8,512]{2,1,0:T(8,128)(2,1)} async-done(((bf16[128,8,512]{2,1,0:T(8,128)(2,1)}), bf16[128,8,512]{2,1,0:T(8,128)(2,1)}, u32[]{:S(2)}, u32[]{:S(2)}) %all-to-all-start) | async-done | bytes 1048608 | tf_op jit(solution)/shard_map/all_to_all | solution.py:196
  33.2 35.5 %shard_map.127 = (bf16[512,1280]{1,0:T(8,128)(2,1)}, bf16[512,1280]{1,0:T(8,128)(2,1)}, bf16[512,256]{1,0:T(8,128)(2,1)}, bf16[512,256]{1,0:T(8,128)(2,1)}, bf16[1024,512]{1,0:T(8,128)(2,1)}) custom-call(s32[1]{0:T(128)S(6)} %copy.35.length_ref, bf16[512,1280]{1,0:T(8,128)(2,1)} %bitcast.35, bf16[1280,512]{1,0:T(8,128)(2,1)} %bitcast.37, ...), custom_call_target="tpu_custom_call" | custom-call | tf_op jit(solution)/shard_map/pallas_call | solution.py:125
  68.7 24.0 %all_to_all.10 = bf16[128,8,512]{2,1,0:T(8,128)(2,1)S(1)} all-to-all(bf16[128,8,512]{2,1,0:T(8,128)(2,1)} %bitcast.44), channel_id=1, replica_groups=mesh['resp'=32,'head'=4] {'resp','head'}, dimensions={0} | all-to-all | bytes 2097152 | tf_op jit(solution)/shard_map/all_to_all | solution.py:210
  92.7 0.2 convert_reduce_fusion
  92.9 0.6 fusion
Async XLA Ops:
  2.5 12.6 %copy-start.4 = (s32[1,512]{1,0:T(1,128)S(1)}, s32[1,512]{1,0:T(1,128)}, u32[]{:S(2)}) copy-start(s32[1,512]{1,0:T(1,128)} %keep_row_ref.1) | copy-start | bytes 6148
  2.5 13.5 %copy-start.2 = (bf16[1,512,256]{2,1,0:T(8,128)(2,1)S(1)}, bf16[1,512,256]{2,1,0:T(8,128)(2,1)}, u32[]{:S(2)}) copy-start(bf16[1,512,256]{2,1,0:T(8,128)(2,1)} %param.9) | copy-start | bytes 786436
  2.5 14.4 %copy-start.3 = (bf16[1,512,256]{2,1,0:T(8,128)(2,1)S(1)}, bf16[1,512,256]{2,1,0:T(8,128)(2,1)}, u32[]{:S(2)}) copy-start(bf16[1,512,256]{2,1,0:T(8,128)(2,1)} %param.10) | copy-start | bytes 786436
  2.5 15.2 %copy-start = (bf16[1,512,1280]{2,1,0:T(8,128)(2,1)S(1)}, bf16[1,512,1280]{2,1,0:T(8,128)(2,1)}, u32[]{:S(2)}) copy-start(bf16[1,512,1280]{2,1,0:T(8,128)(2,1)} %param.8) | copy-start | bytes 3932164
  2.5 30.7 %all-to-all-start = ((bf16[128,8,512]{2,1,0:T(8,128)(2,1)}), bf16[128,8,512]{2,1,0:T(8,128)(2,1)}, u32[]{:S(2)}, u32[]{:S(2)}) async-start(bf16[128,8,512]{2,1,0:T(8,128)(2,1)} %bitcast.9), calls=%async_computation | async-start | bytes 2097152 | tf_op jit(solution)/shard_map/all_to_all | solution.py:196
  17.7 1.5 %copy-start.1 = (bf16[1,512,1280]{2,1,0:T(8,128)(2,1)S(1)}, bf16[1,512,1280]{2,1,0:T(8,128)(2,1)}, u32[]{:S(2)}) copy-start(bf16[1,512,1280]{2,1,0:T(8,128)(2,1)} %param.15) | copy-start | bytes 3932164

commit v23 on v20

--- a/solution.py
+++ b/solution.py
@@ -99,18 +99,18 @@
             1,
         )
         dq_ref[:, cols] = (dq * scale).T.astype(bf16)
-        pg_ref[:, :width] += jnp.dot(dsp, q, preferred_element_type=f32) * scale
+        pg_ref[:, :width] += jnp.dot(dsp, q, preferred_element_type=f32)
         pg_ref[:, width:] += jnp.dot(wp, do, preferred_element_type=f32)
-        dko_acc[:half, :] += jnp.dot(dso1, q[:half], preferred_element_type=f32) * scale
-        dko_acc[...] += jnp.dot(dso2, q[half:], preferred_element_type=f32) * scale
+        dko_acc[:half, :] += jnp.dot(dso1, q[:half], preferred_element_type=f32)
+        dko_acc[...] += jnp.dot(dso2, q[half:], preferred_element_type=f32)
         dvo_acc[:half, :] += jnp.dot(wo1, do[:half], preferred_element_type=f32)
         dvo_acc[...] += jnp.dot(wo2, do[half:], preferred_element_type=f32)
         return carry
 
     lax.fori_loop(0, group_size, head, 0)
-    dko_ref[...] = dko_acc[...].astype(bf16)
+    dko_ref[...] = (dko_acc[...] * scale).astype(bf16)
     dvo_ref[...] = dvo_acc[...].astype(bf16)
-    pg_out[:, :width] = pg_ref[:, :width].astype(bf16)
+    pg_out[:, :width] = (pg_ref[:, :width] * scale).astype(bf16)
     pg_out[:, width:] = pg_ref[:, width:].astype(bf16)
 
 

time: 93.8 us -> 94.8 us (1.011)
    pallas_call x1, Pallas kernels: 35.4 us -> 36.3 us  [attend(): pl.pallas_call(attention_kernel, out_shape=(jax.ShapeDtypeStruct((steps,...]
where the time goes in v23:
time: 94.8 us; the launch traced here: 94.3 us
  Pallas kernels  36.3 us (38%)
  blocking collectives  24 us (25%)
  waiting for transfers between devices  12.5 us (13%)
  starting transfers between devices  12 us (13%)
  local copies, waits for them, and re-layouts  7.29 us (8%)
  between operations  1.31 us (1%)
    pallas_call x1, Pallas kernels, attend(): pl.pallas_call(attention_kernel, out_shape=(jax.ShapeDtypeStruct((steps,...  36.3 us
    all_to_all x1, blocking collectives, per_device(): lax.all_to_all(prompt_parts.reshape(devices, rows_here, 2 * kv_width), ('...  24 us
    all_to_all x1, waiting for transfers between devices, per_device(): lax.all_to_all(outgoing, ('resp', 'head'), split_axis=0, concat_axis=0, t...  12.5 us
    all_to_all x1, starting transfers between devices, per_device(): lax.all_to_all(outgoing, ('resp', 'head'), split_axis=0, concat_axis=0, t...  12 us
    unnamed x14, local copies, waits for them, and re-layouts  4.7 us
  transfers between devices with their start and end apart: 1, of which 1 were waited for; matrix products, arithmetic and copies ran while one was open for 6% of the time, Pallas kernels for 0%

profile of v23, /device:TPU:1, one launch (start us, length us, event | category | flops | bytes accessed | tf_op | source)
XLA Modules:
  0.0 94.3 jit_solution(1941534500463635891)
XLA Ops:
  0.6 0.7 maximum_bitcast_fusion
  1.4 1.1 %broadcast_in_dim.2 = bf16[32,4,8,512]{3,2,1,0:T(8,128)(2,1)} broadcast(bf16[4,8,512]{2,1,0:T(8,128)(2,1)S(1)} %maximum_bitcast_fusion), dimensions={1,2,3} | broadcast | bytes 1081344 | tf_op jit(solution)/shard_map/broadcast_in_dim | solution.py:193
  2.5 0.0 copy-start.4
  2.5 0.0 copy-start.2
  2.5 0.0 copy-start.3
  2.5 0.0 copy-start
  2.5 12.0 %all-to-all-start = ((bf16[128,8,512]{2,1,0:T(8,128)(2,1)}), bf16[128,8,512]{2,1,0:T(8,128)(2,1)}, u32[]{:S(2)}, u32[]{:S(2)}) async-start(bf16[128,8,512]{2,1,0:T(8,128)(2,1)} %bitcast.9), calls=%async_computation | async-start | bytes 2097152 | tf_op jit(solution)/shard_map/all_to_all | solution.py:196
  15.1 0.0 copy-done.4
  15.1 0.9 copy.30.keep_col_ref
  16.0 0.0 copy-done.2
  16.0 0.9 copy.24
  16.8 0.0 copy-done.3
  16.8 0.9 copy.25
  17.7 0.0 copy-done
  17.7 0.0 copy-start.1
  17.7 1.5 %copy.22 = bf16[1,512,1280]{1,2,0:T(8,128)(2,1)} copy(bf16[1,512,1280]{2,1,0:T(8,128)(2,1)S(1)} %copy-done) | data formatting | bytes 2621440 | tf_op args[0]
  19.2 0.0 copy-done.1
  19.2 1.5 %copy.23 = bf16[1,512,1280]{1,2,0:T(8,128)(2,1)} copy(bf16[1,512,1280]{2,1,0:T(8,128)(2,1)S(1)} %copy-done.1) | data formatting | bytes 2621440 | tf_op args[7]
  20.7 12.5 %all-to-all-done = bf16[128,8,512]{2,1,0:T(8,128)(2,1)} async-done(((bf16[128,8,512]{2,1,0:T(8,128)(2,1)}), bf16[128,8,512]{2,1,0:T(8,128)(2,1)}, u32[]{:S(2)}, u32[]{:S(2)}) %all-to-all-start) | async-done | bytes 1048608 | tf_op jit(solution)/shard_map/all_to_all | solution.py:196
  33.2 36.3 %shard_map.127 = (bf16[512,1280]{1,0:T(8,128)(2,1)}, bf16[512,1280]{1,0:T(8,128)(2,1)}, bf16[512,256]{1,0:T(8,128)(2,1)}, bf16[512,256]{1,0:T(8,128)(2,1)}, bf16[1024,512]{1,0:T(8,128)(2,1)}) custom-call(s32[1]{0:T(128)S(6)} %copy.35.length_ref, bf16[512,1280]{1,0:T(8,128)(2,1)} %bitcast.35, bf16[1280,512]{1,0:T(8,128)(2,1)} %bitcast.37, ...), custom_call_target="tpu_custom_call" | custom-call | tf_op jit(solution)/shard_map/pallas_call | solution.py:125
  69.5 24.0 %all_to_all.10 = bf16[128,8,512]{2,1,0:T(8,128)(2,1)S(1)} all-to-all(bf16[128,8,512]{2,1,0:T(8,128)(2,1)} %bitcast.44), channel_id=1, replica_groups=mesh['resp'=32,'head'=4] {'resp','head'}, dimensions={0} | all-to-all | bytes 2097152 | tf_op jit(solution)/shard_map/all_to_all | solution.py:210
  93.5 0.2 convert_reduce_fusion
  93.7 0.6 fusion
Async XLA Ops:
  2.5 12.6 %copy-start.4 = (s32[1,512]{1,0:T(1,128)S(1)}, s32[1,512]{1,0:T(1,128)}, u32[]{:S(2)}) copy-start(s32[1,512]{1,0:T(1,128)} %keep_row_ref.1) | copy-start | bytes 6148
  2.5 13.5 %copy-start.2 = (bf16[1,512,256]{2,1,0:T(8,128)(2,1)S(1)}, bf16[1,512,256]{2,1,0:T(8,128)(2,1)}, u32[]{:S(2)}) copy-start(bf16[1,512,256]{2,1,0:T(8,128)(2,1)} %param.9) | copy-start | bytes 786436
  2.5 14.4 %copy-start.3 = (bf16[1,512,256]{2,1,0:T(8,128)(2,1)S(1)}, bf16[1,512,256]{2,1,0:T(8,128)(2,1)}, u32[]{:S(2)}) copy-start(bf16[1,512,256]{2,1,0:T(8,128)(2,1)} %param.10) | copy-start | bytes 786436
  2.5 15.2 %copy-start = (bf16[1,512,1280]{2,1,0:T(8,128)(2,1)S(1)}, bf16[1,512,1280]{2,1,0:T(8,128)(2,1)}, u32[]{:S(2)}) copy-start(bf16[1,512,1280]{2,1,0:T(8,128)(2,1)} %param.8) | copy-start | bytes 3932164
  2.5 30.7 %all-to-all-start = ((bf16[128,8,512]{2,1,0:T(8,128)(2,1)}), bf16[128,8,512]{2,1,0:T(8,128)(2,1)}, u32[]{:S(2)}, u32[]{:S(2)}) async-start(bf16[128,8,512]{2,1,0:T(8,128)(2,1)} %bitcast.9), calls=%async_computation | async-start | bytes 2097152 | tf_op jit(solution)/shard_map/all_to_all | solution.py:196
  17.7 1.5 %copy-start.1 = (bf16[1,512,1280]{2,1,0:T(8,128)(2,1)S(1)}, bf16[1,512,1280]{2,1,0:T(8,128)(2,1)}, u32[]{:S(2)}) copy-start(bf16[1,512,1280]{2,1,0:T(8,128)(2,1)} %param.15) | copy-start | bytes 3932164
